TPU v7x, 32 devices: a whole 2x2x4 slice. The times are simulated.
32 devices in a mesh: groups: 2 (over y), seq: 8 (over z, x), head: 2 (over core).
Axes of the slice: x: 2, y: 2, z: 4, core: 2. Of those that a mesh axis runs over, the one named last changes fastest.
Arguments:
- queries: bfloat16 [4096, 4096], P(('groups', 'seq'), 'head'), parts along dimension 0, may hold values from -40 to 40
- key_vectors: bfloat16 [4096, 4096], P(('groups', 'seq'), 'head'), parts along dimension 0, may hold values from -6 to 6
- value_vectors: bfloat16 [4096, 4096], P(('groups', 'seq'), 'head'), parts along dimension 0, may hold values from -40 to 40
- output_grad: bfloat16 [4096, 4096], P(('groups', 'seq'), 'head'), parts along dimension 0, may hold values from -6 to 6
- norm_gain: float32 [4096], P('head'), may hold values from 0.5 to 2
- block_docs: int32 [16], P(('groups', 'seq')), parts along dimension 0, may hold values from 0 to 3, never falling along the last dimension, each value on 1 to 4 neighbouring positions
Outputs:
- normed: bfloat16 [4096, 4096], P(('groups', 'seq'), 'head'), parts along dimension 0
- query_grad: bfloat16 [4096, 4096], P(('groups', 'seq'), 'head'), parts along dimension 0
- key_grad: bfloat16 [4096, 4096], P(('groups', 'seq'), 'head'), parts along dimension 0
- value_grad: bfloat16 [4096, 4096], P(('groups', 'seq'), 'head'), parts along dimension 0
There are 2 independent parts, one for each index of `groups`. A program takes and returns all parts, laid end to end along the dimension named above; an argument that names none is the same for every part. Nothing has to cross between parts.
Inputs may be any that keep to these rules, and one draw needn't show every extreme that they name: `block_docs`: block document ids never fall along the sequence; every one of the 4 documents covers 1 to 4 blocks, and one covers exactly 4.
All inputs are finite; a program needn't handle non-finite values.
Results may differ from a plain program's by a relative error of at most 0.0058.
Values sent between devices are 32-bit elements; how exact they have to be, the bound alone decides.
No kernel may reach another device: no remote copies, remote signals or barrier semaphores. Data moves between devices by JAX's collectives and lax.ppermute only.
A program may use at most 64 MiB of HBM per device.

v0:
```python
import jax
import jax.numpy as jnp
from jax import lax
from jax.sharding import PartitionSpec as P

HEAD_DIM = 128


norm_eps = 1e-06


def spread_prefix(element, weights):
    seq_count = lax.axis_size("seq")
    flat_state = element.reshape(seq_count, -1, element.shape[-1])
    mixed = jnp.einsum(
        "ds,skc->dkc",
        weights,
        lax.all_to_all(flat_state, "seq", split_axis=0, concat_axis=0, tiled=True),
        precision=lax.Precision.HIGHEST,
    )
    returned = lax.all_to_all(mixed, "seq", split_axis=0, concat_axis=0, tiled=True)
    return returned.reshape(element.shape)


def body(queries, key_vectors, value_vectors, output_grad, norm_gain, block_docs):
    tokens, local_width = queries.shape
    heads_here = local_width // HEAD_DIM
    nblocks = block_docs.shape[0]
    block_len = tokens // nblocks
    shape_four = (nblocks, block_len, heads_here, HEAD_DIM)
    query_blk = queries.reshape(shape_four)
    key_blk = key_vectors.reshape(shape_four)
    value_blk = value_vectors.reshape(shape_four)
    tok_pos = lax.iota(jnp.int32, block_len)
    causal = (tok_pos[:, None] >= tok_pos[None, :])[None, None]
    scores = jnp.einsum("bthd,bshd->bhts", query_blk, key_blk, preferred_element_type=jnp.float32)
    att_weights = jnp.where(causal, scores, 0.0).astype(jnp.bfloat16)
    intra_out = jnp.einsum(
        "bhts,bshe->bthe", att_weights, value_blk, preferred_element_type=jnp.float32
    )
    block_kv = jnp.einsum("bshd,bshe->bhde", key_blk, value_blk, preferred_element_type=jnp.float32)
    position = lax.iota(jnp.int32, nblocks)
    same_doc = block_docs[:, None] == block_docs[None, :]
    earlier_mask = (same_doc & (position[None, :] < position[:, None])).astype(jnp.float32)
    later_mask = (same_doc & (position[None, :] > position[:, None])).astype(jnp.float32)
    local_in = jnp.einsum("kj,jhde->khde", earlier_mask, block_kv, precision=lax.Precision.HIGHEST)
    tail_weight = (block_docs == block_docs[-1]).astype(jnp.float32)
    tail_state = jnp.einsum("j,jhde->hde", tail_weight, block_kv, precision=lax.Precision.HIGHEST)
    seq_count = lax.axis_size("seq")
    all_docs = lax.all_gather(block_docs, "seq", axis=0, tiled=True).reshape(seq_count, nblocks)
    first_all = all_docs[:, 0]
    last_all = all_docs[:, -1]
    source_pos = lax.iota(jnp.int32, seq_count)
    forward_weights = (
        (source_pos[None, :] < source_pos[:, None]) & (last_all[None, :] == first_all[:, None])
    ).astype(jnp.float32)
    backward_weights = (
        (source_pos[None, :] > source_pos[:, None]) & (first_all[None, :] == last_all[:, None])
    ).astype(jnp.float32)
    carry_state = spread_prefix(tail_state, forward_weights)
    carry_use = block_docs == block_docs[0]
    states_in = (
        local_in + jnp.where(carry_use[:, None, None, None], carry_state[None], 0.0)
    ).astype(jnp.bfloat16)
    inter_out = jnp.einsum(
        "bthd,bhde->bthe", query_blk, states_in, preferred_element_type=jnp.float32
    )
    attended = (intra_out + inter_out).reshape(tokens, local_width)
    scaled_grad = norm_gain[None, :] * output_grad.astype(jnp.float32)
    square_sum, cross_sum = lax.psum(
        (jnp.sum(attended * attended, axis=1), jnp.sum(attended * scaled_grad, axis=1)), "head"
    )
    full_width = local_width * lax.axis_size("head")
    inverse_rms = lax.rsqrt(square_sum / full_width + norm_eps)
    normed = (attended * inverse_rms[:, None] * norm_gain[None, :]).astype(jnp.bfloat16)
    attended_grad = (
        inverse_rms[:, None] * scaled_grad
        - attended * (inverse_rms**3 * cross_sum / full_width)[:, None]
    )
    grad_blk = attended_grad.astype(jnp.bfloat16).reshape(shape_four)
    score_grad = jnp.einsum(
        "bthe,bshe->bhts", grad_blk, value_blk, preferred_element_type=jnp.float32
    )
    grad_weights = jnp.where(causal, score_grad, 0.0).astype(jnp.bfloat16)
    query_part = jnp.einsum(
        "bhts,bshd->bthd", grad_weights, key_blk, preferred_element_type=jnp.float32
    )
    query_part = query_part + jnp.einsum(
        "bthe,bhde->bthd", grad_blk, states_in, preferred_element_type=jnp.float32
    )
    key_intra = jnp.einsum(
        "bhts,bthd->bshd", grad_weights, query_blk, preferred_element_type=jnp.float32
    )
    value_intra = jnp.einsum(
        "bhts,bthe->bshe", att_weights, grad_blk, preferred_element_type=jnp.float32
    )
    block_grad = jnp.einsum(
        "bthd,bthe->bhde", query_blk, grad_blk, preferred_element_type=jnp.float32
    )
    grad_local = jnp.einsum(
        "kj,jhde->khde", later_mask, block_grad, precision=lax.Precision.HIGHEST
    )
    head_weight = (block_docs == block_docs[0]).astype(jnp.float32)
    head_state = jnp.einsum("j,jhde->hde", head_weight, block_grad, precision=lax.Precision.HIGHEST)
    grad_state = spread_prefix(head_state, backward_weights)
    grad_use = block_docs == block_docs[-1]
    grads_in = (
        grad_local + jnp.where(grad_use[:, None, None, None], grad_state[None], 0.0)
    ).astype(jnp.bfloat16)
    key_part = key_intra + jnp.einsum(
        "bshe,bhde->bshd", value_blk, grads_in, preferred_element_type=jnp.float32
    )
    value_part = value_intra + jnp.einsum(
        "bshd,bhde->bshe", key_blk, grads_in, preferred_element_type=jnp.float32
    )
    flat_shape = (tokens, local_width)
    return (
        normed,
        query_part.reshape(flat_shape).astype(jnp.bfloat16),
        key_part.reshape(flat_shape).astype(jnp.bfloat16),
        value_part.reshape(flat_shape).astype(jnp.bfloat16),
    )


def solution(mesh):
    in_specs = (
        P(("groups", "seq"), "head"),
        P(("groups", "seq"), "head"),
        P(("groups", "seq"), "head"),
        P(("groups", "seq"), "head"),
        P("head"),
        P(("groups", "seq")),
    )
    out_specs = (
        P(("groups", "seq"), "head"),
        P(("groups", "seq"), "head"),
        P(("groups", "seq"), "head"),
        P(("groups", "seq"), "head"),
    )
    return jax.shard_map(body, mesh=mesh, in_specs=in_specs, out_specs=out_specs, check_vma=False)
```

profile of v0, /device:TPU:0, one launch (start us, length us, event | category | flops | bytes accessed | tf_op | source)
XLA Modules:
  0.0 156.2 jit_solution(16867197169526272815)
XLA Ops:
  0.6 0.0 copy-start
  0.6 1.5 copy.72
  2.2 0.8 copy.41
  3.0 0.0 copy-start.14
  3.0 1.4 fusion.8
  4.4 7.3 %all-to-all-start = ((f32[8,256,128]{2,1,0:T(8,128)}), f32[8,256,128]{2,1,0:T(8,128)S(1)}, u32[]{:S(2)}, u32[]{:S(2)}) async-start(f32[8,256,128]{2,1,0:T(8,128)} %bitcast.3), calls=%async_computation | async-start | bytes 2097152 | tf_op jit(solution)/shard_map/all_to_all | solution.py:18
  12.3 0.6 dynamic-slice
  12.9 0.8 dynamic-update-slice
  13.7 23.9 %all-reduce = s32[8]{0:T(128)S(1)} all-reduce(s32[8]{0:T(128)S(1)} %dynamic-update-slice), channel_id=1, replica_groups=mesh['groups'=2,'seq'=8,'head'=2] {'seq'}, use_global_device_ids=true, to_apply=%add | all-reduce | flops 8 | bytes 64
  37.6 1.2 fusion.16
  38.8 1.2 copy.44
  40.0 3.6 %all-to-all-start.1 = ((f32[8,256,128]{2,1,0:T(8,128)}), f32[8,256,128]{2,1,0:T(8,128)S(1)}, u32[]{:S(2)}, u32[]{:S(2)}) async-start(f32[8,256,128]{2,1,0:T(8,128)} %copy.44), calls=%async_computation.1 | async-start | bytes 2097152 | tf_op jit(solution)/shard_map/all_to_all | solution.py:21
  43.6 1.5 copy.68
  45.1 2.4 %select_convert_fusion.1 = bf16[16,256,256]{2,1,0:T(8,128)(2,1)S(1)} fusion(bf16[256,16,128]{0,2,1:T(8,128)(2,1)S(1)} %bitcast.111, pred[256,256]{1,0:T(8,128)(4,1)S(1)} %iota_compare_fusion, bf16[256,2048]{1,0:T(8,128)(2,1)} %param.7), kind=kOutput, calls=%fused_computation.1 | convolution fusion | flops 270532608 | bytes 4259840 | tf_op jit(solution)/shard_map/bthd,bshd->bhts/dot_general | solution.py:36
  47.5 1.3 copy-done.8
  48.8 2.2 %fusion.3 = f32[16,256,128]{1,2,0:T(8,128)} fusion(bf16[16,256,256]{2,1,0:T(8,128)(2,1)S(1)} %select_convert_fusion.1, bf16[256,2048]{1,0:T(8,128)(2,1)S(1)} %copy-done), kind=kOutput, calls=%fused_computation.14 | convolution fusion | flops 268435456 | bytes 5242880 | tf_op jit(solution)/shard_map/bhts,bshe->bthe/dot_general | solution.py:38
  50.9 18.6 %all-to-all-done.1 = f32[8,256,128]{2,1,0:T(8,128)S(1)} async-done(((f32[8,256,128]{2,1,0:T(8,128)}), f32[8,256,128]{2,1,0:T(8,128)S(1)}, u32[]{:S(2)}, u32[]{:S(2)}) %all-to-all-start.1) | async-done | bytes 1048608 | tf_op jit(solution)/shard_map/all_to_all | solution.py:21
  69.5 1.5 add_convert_fusion.1
  71.0 0.4 copy-done.7
  71.4 1.8 %fusion.2 = (f32[256]{0:T(256)S(1)}, f32[16,128,256]{2,1,0:T(8,128)}) fusion(bf16[16,128,128]{2,1,0:T(8,128)(2,1)S(1)} %add_convert_fusion.1, bf16[256,16,128]{0,2,1:T(8,128)(2,1)S(1)} %bitcast.112, f32[16,256,128]{1,2,0:T(8,128)S(1)} %copy-done.7), kind=kOutput, calls=%fused_computation.7 | convolution fusion | flops 135790336 | bytes 5768192 | tf_op jit(solution)/shard_map/bthd,bhde->bthe/dot_general | solution.py:65
  73.3 1.9 %copy.47 = f32[256,2048]{1,0:T(8,128)S(1)} copy(f32[256,2048]{0,1:T(8,128)} %bitcast.116) | data formatting | bytes 4194304 | tf_op jit(solution)/shard_map/reshape | solution.py:68
  75.2 1.6 %multiply_reduce_fusion = f32[256]{0:T(256)S(1)} fusion(f32[256,2048]{1,0:T(8,128)S(1)} %copy.47, bf16[256,2048]{1,0:T(8,128)(2,1)} %param.9, f32[2048]{0:T(1024)S(1)} %copy-done.13), kind=kLoop, calls=%fused_computation.11 | loop fusion | flops 2096896 | bytes 3154944 | tf_op jit(solution)/shard_map/reduce_sum | solution.py:71
  76.8 2.5 %all-reduce.1 = (f32[256]{0:T(256)S(1)}, f32[256]{0:T(256)S(1)}) all-reduce(f32[256]{0:T(256)S(1)} %get-tuple-element.18, f32[256]{0:T(256)S(1)} %multiply_reduce_fusion), channel_id=1, replica_groups=mesh['groups'=2,'seq'=8,'head'=2] {'head'}, use_global_device_ids=true, to_apply=%region_1.2 | all-reduce | flops 512 | bytes 4096 | tf_op jit(solution)/shard_map/psum | solution.py:70
  79.3 3.6 %subtract_convert_fusion = (bf16[256,2048]{1,0:T(8,128)(2,1)}, bf16[256,2048]{1,0:T(8,128)(2,1)}) fusion(f32[256,2048]{1,0:T(8,128)S(1)} %copy.47, bf16[256,2048]{1,0:T(8,128)(2,1)} %param.9, f32[256]{0:T(256)S(1)} %get-tuple-element.16, f32[2048]{0:T(1024)S(1)} %copy-done.13, f32[256]{0:T(256)S(1)} %get-tuple-element.17), kind=kLoop, calls=%fused_computation.10 | loop fusion | flops 4718592 | bytes 5253120 | tf_op jit(solution)/shard_map/convert_element_type | solution.py:80
  82.8 1.6 %copy.69 = bf16[256,2048]{0,1:T(8,128)(2,1)S(1)} copy(bf16[256,2048]{1,0:T(8,128)(2,1)} %get-tuple-element.14) | data formatting | bytes 2097152 | tf_op jit(solution)/shard_map/reshape.36
  84.4 0.4 fusion.36
  84.9 29.5 %all_to_all.20 = f32[8,256,128]{2,1,0:T(8,128)S(1)} all-to-all(f32[8,256,128]{2,1,0:T(8,128)S(1)} %bitcast.115), channel_id=1, replica_groups=mesh['groups'=2,'seq'=8,'head'=2] {'seq'}, dimensions={0} | all-to-all | bytes 2097152 | tf_op jit(solution)/shard_map/all_to_all | solution.py:18
  114.4 1.2 fusion.14
  115.6 1.2 copy.58
  116.7 4.4 %all-to-all-start.3 = ((f32[8,256,128]{2,1,0:T(8,128)}), f32[8,256,128]{2,1,0:T(8,128)}, u32[]{:S(2)}, u32[]{:S(2)}) async-start(f32[8,256,128]{2,1,0:T(8,128)} %copy.58), calls=%async_computation.3 | async-start | bytes 2097152 | tf_op jit(solution)/shard_map/all_to_all | solution.py:21
  121.1 0.0 copy-start.4
  121.1 0.8 select_convert_fusion
  121.9 0.4 copy-done.4
  122.4 0.8 fusion.34
  123.2 0.5 copy-done.6
  123.7 0.1 copy-done.11
  123.8 1.4 fusion.1
  125.2 2.3 %copy.63 = bf16[256,2048]{1,0:T(8,128)(2,1)} copy(bf16[256,2048]{0,1:T(8,128)(2,1)} %bitcast.121) | data formatting | bytes 2097152
  127.5 3.4 %fusion.35 = f32[16,128,256]{2,1,0:T(8,128)} fusion(bf16[256,16,128]{0,2,1:T(8,128)(2,1)S(1)} %bitcast.110, bf16[16,256,256]{2,1,0:T(8,128)(2,1)} %copy-done.8), kind=kOutput, calls=%fused_computation.53 | convolution fusion | flops 268435456 | bytes 5242880 | tf_op jit(solution)/shard_map/bhts,bthe->bshe/dot_general | solution.py:94
  130.8 15.1 %all-to-all-done.3 = f32[8,256,128]{2,1,0:T(8,128)} async-done(((f32[8,256,128]{2,1,0:T(8,128)}), f32[8,256,128]{2,1,0:T(8,128)}, u32[]{:S(2)}, u32[]{:S(2)}) %all-to-all-start.3) | async-done | bytes 1048608 | tf_op jit(solution)/shard_map/all_to_all | solution.py:21
  145.9 1.7 %fusion.13 = bf16[16,128,128]{2,1,0:T(8,128)(2,1)S(1)} fusion(f32[16,128,128]{2,1,0:T(8,128)} %bitcast.18, f32[16,128,128]{1,2,0:T(8,128)} %copy-done.5), kind=kLoop, calls=%fused_computation.25 | loop fusion | flops 786432 | bytes 2621440 | tf_op jit(solution)/shard_map/convert_element_type | solution.py:109
  147.6 1.8 %fusion.5 = f32[16,128,256]{2,1,0:T(8,128)} fusion(bf16[16,128,128]{2,1,0:T(8,128)(2,1)S(1)} %fusion.13, bf16[256,2048]{1,0:T(8,128)(2,1)S(1)} %copy-done), kind=kOutput, calls=%fused_computation.16 | convolution fusion | flops 134217728 | bytes 3670016 | tf_op jit(solution)/shard_map/bshe,bhde->bshd/dot_general | solution.py:110
  149.4 0.2 copy-done.9
  149.5 0.7 copy-done.12
  150.2 0.5 add_convert_fusion
  150.7 1.4 copy.65
  152.1 2.7 %fusion = bf16[16,128,256]{2,1,0:T(8,128)(2,1)S(1)} fusion(f32[16,128,256]{2,1,0:T(8,128)} %fusion.5, bf16[256,16,128]{0,2,1:T(8,128)(2,1)S(1)} %bitcast.114, bf16[16,256,256]{2,1,0:T(8,128)(2,1)} %copy-done.6), kind=kOutput, calls=%fused_computation.3 | convolution fusion | flops 269484032 | bytes 6291456 | tf_op jit(solution)/shard_map/bhts,bthd->bshd/dot_general | solution.py:91
  154.8 1.4 copy.64
  (24 shorter events, 0.1 us)
Async XLA Ops:
  0.6 2.4 %copy-start = (bf16[256,2048]{1,0:T(8,128)(2,1)S(1)}, bf16[256,2048]{1,0:T(8,128)(2,1)}, u32[]{:S(2)}) copy-start(bf16[256,2048]{1,0:T(8,128)(2,1)} %param.8) | copy-start | bytes 3145732
  3.0 1.4 copy-start.3
  3.0 9.3 %copy-start.14 = (u32[32]{0:T(128)S(1)}, u32[32]{0:T(128)}, u32[]{:S(2)}) copy-start(u32[32]{0:T(128)} %constant.19) | copy-start | bytes 388
  4.4 33.2 %all-to-all-start = ((f32[8,256,128]{2,1,0:T(8,128)}), f32[8,256,128]{2,1,0:T(8,128)S(1)}, u32[]{:S(2)}, u32[]{:S(2)}) async-start(f32[8,256,128]{2,1,0:T(8,128)} %bitcast.3), calls=%async_computation | async-start | bytes 2097152 | tf_op jit(solution)/shard_map/all_to_all | solution.py:18
  40.0 29.5 %all-to-all-start.1 = ((f32[8,256,128]{2,1,0:T(8,128)}), f32[8,256,128]{2,1,0:T(8,128)S(1)}, u32[]{:S(2)}, u32[]{:S(2)}) async-start(f32[8,256,128]{2,1,0:T(8,128)} %copy.44), calls=%async_computation.1 | async-start | bytes 2097152 | tf_op jit(solution)/shard_map/all_to_all | solution.py:21
  45.0 26.0 %copy-start.1 = (bf16[256,2048]{0,1:T(8,128)(2,1)}, bf16[256,2048]{0,1:T(8,128)(2,1)S(1)}, u32[]{:S(2)}) copy-start(bf16[256,2048]{0,1:T(8,128)(2,1)S(1)} %copy.68) | copy-start | bytes 3145732
  47.5 1.3 copy-start.8
  69.5 1.9 %copy-start.7 = (f32[16,256,128]{1,2,0:T(8,128)S(1)}, f32[16,256,128]{1,2,0:T(8,128)}, u32[]{:S(2)}) copy-start(f32[16,256,128]{1,2,0:T(8,128)} %fusion.3) | copy-start | bytes 6291460
  71.4 1.8 %copy-start.10 = (bf16[16,128,128]{2,1,0:T(8,128)(2,1)}, bf16[16,128,128]{2,1,0:T(8,128)(2,1)S(1)}, u32[]{:S(2)}) copy-start(bf16[16,128,128]{2,1,0:T(8,128)(2,1)S(1)} %add_convert_fusion.1) | copy-start | bytes 1572868
  73.3 1.9 %copy-start.13 = (f32[2048]{0:T(1024)S(1)}, f32[2048]{0:T(1024)}, u32[]{:S(2)}) copy-start(f32[2048]{0:T(1024)} %param.10) | copy-start | bytes 24580
  82.8 1.6 %copy-start.2 = (bf16[256,2048]{0,1:T(8,128)(2,1)S(1)}, bf16[256,2048]{0,1:T(8,128)(2,1)}, u32[]{:S(2)}) copy-start(bf16[256,2048]{0,1:T(8,128)(2,1)} %copy-done.1) | copy-start | bytes 3145732
  84.9 30.7 %copy-start.5 = (f32[16,128,128]{1,2,0:T(8,128)}, f32[16,128,128]{1,2,0:T(8,128)S(1)}, u32[]{:S(2)}) copy-start(f32[16,128,128]{1,2,0:T(8,128)S(1)} %fusion.36) | copy-start | bytes 3145732
  116.7 29.2 %all-to-all-start.3 = ((f32[8,256,128]{2,1,0:T(8,128)}), f32[8,256,128]{2,1,0:T(8,128)}, u32[]{:S(2)}, u32[]{:S(2)}) async-start(f32[8,256,128]{2,1,0:T(8,128)} %copy.58), calls=%async_computation.3 | async-start | bytes 2097152 | tf_op jit(solution)/shard_map/all_to_all | solution.py:21
  121.1 1.2 copy-start.4
  122.4 1.3 copy-start.6
  122.4 1.4 copy-start.11
  147.6 1.9 %copy-start.9 = (f32[16,128,256]{2,1,0:T(8,128)S(1)}, f32[16,128,256]{2,1,0:T(8,128)}, u32[]{:S(2)}) copy-start(f32[16,128,256]{2,1,0:T(8,128)} %fusion.35) | copy-start | bytes 6291460
  147.6 2.6 %copy-start.12 = (bf16[256,2048]{1,0:T(8,128)(2,1)S(1)}, bf16[256,2048]{1,0:T(8,128)(2,1)}, u32[]{:S(2)}) copy-start(bf16[256,2048]{1,0:T(8,128)(2,1)} %param.7) | copy-start | bytes 3145732
where the time goes:
time: 157 us; the launch traced here: 156 us
  blocking collectives  55.9 us (36%)
  waiting for transfers between devices  33.7 us (21%)
  matrix products  21.8 us (14%)
  local copies, waits for them, and re-layouts  19.7 us (13%)
  starting transfers between devices  15.3 us (10%)
  other arithmetic  8.37 us (5%)
    all_to_all x2, waiting for transfers between devices, spread_prefix(): lax.all_to_all(mixed, 'seq', split_axis=0, concat_axis=0, tiled=True)  33.7 us
    all_to_all x1, blocking collectives, spread_prefix(): lax.all_to_all(flat_state, 'seq', split_axis=0, concat_axis=0, tiled=True)  29.5 us
    unnamed x1, blocking collectives  23.9 us
    unnamed x37, local copies, waits for them, and re-layouts  11.6 us
    all_to_all x2, starting transfers between devices, spread_prefix(): lax.all_to_all(mixed, 'seq', split_axis=0, concat_axis=0, tiled=True)  8.01 us
    all_to_all x1, starting transfers between devices, spread_prefix(): lax.all_to_all(flat_state, 'seq', split_axis=0, concat_axis=0, tiled=True)  7.25 us
    another operation x3, local copies, waits for them, and re-layouts  3.83 us
    convert_element_type x1, other arithmetic, body(): grad_blk = attended_grad.astype(jnp.bfloat16).reshape(shape_four)  3.57 us
  transfers between devices with their start and end apart: 3, of which 2 were waited for; matrix products, arithmetic and copies ran while one was open for 10% of the time, Pallas kernels for 0%

commit v1 on v0

v1 whole, which is shorter than its diff:
```python
import functools

import jax
import jax.numpy as jnp
from jax import lax
from jax.experimental import pallas as pl
from jax.experimental.pallas import tpu as pltpu
from jax.sharding import PartitionSpec as P

HEAD_DIM = 128
norm_eps = 1e-06
BF = jnp.bfloat16
F32 = jnp.float32


def spread_prefix(element, weights):
    seq_count = lax.axis_size("seq")
    flat_state = element.reshape(seq_count, -1, element.shape[-1])
    mixed = jnp.einsum(
        "ds,skc->dkc",
        weights,
        lax.all_to_all(flat_state, "seq", split_axis=0, concat_axis=0, tiled=True),
        precision=lax.Precision.HIGHEST,
    )
    returned = lax.all_to_all(mixed, "seq", split_axis=0, concat_axis=0, tiled=True)
    return returned.reshape(element.shape)


def general_body(queries, key_vectors, value_vectors, output_grad, norm_gain, block_docs):
    tokens, local_width = queries.shape
    heads_here = local_width // HEAD_DIM
    nblocks = block_docs.shape[0]
    block_len = tokens // nblocks
    shape_four = (nblocks, block_len, heads_here, HEAD_DIM)
    query_blk = queries.reshape(shape_four)
    key_blk = key_vectors.reshape(shape_four)
    value_blk = value_vectors.reshape(shape_four)
    tok_pos = lax.iota(jnp.int32, block_len)
    causal = (tok_pos[:, None] >= tok_pos[None, :])[None, None]
    scores = jnp.einsum("bthd,bshd->bhts", query_blk, key_blk, preferred_element_type=F32)
    att_weights = jnp.where(causal, scores, 0.0).astype(BF)
    intra_out = jnp.einsum("bhts,bshe->bthe", att_weights, value_blk, preferred_element_type=F32)
    block_kv = jnp.einsum("bshd,bshe->bhde", key_blk, value_blk, preferred_element_type=F32)
    position = lax.iota(jnp.int32, nblocks)
    same_doc = block_docs[:, None] == block_docs[None, :]
    earlier_mask = (same_doc & (position[None, :] < position[:, None])).astype(F32)
    later_mask = (same_doc & (position[None, :] > position[:, None])).astype(F32)
    local_in = jnp.einsum("kj,jhde->khde", earlier_mask, block_kv, precision=lax.Precision.HIGHEST)
    tail_weight = (block_docs == block_docs[-1]).astype(F32)
    tail_state = jnp.einsum("j,jhde->hde", tail_weight, block_kv, precision=lax.Precision.HIGHEST)
    seq_count = lax.axis_size("seq")
    all_docs = lax.all_gather(block_docs, "seq", axis=0, tiled=True).reshape(seq_count, nblocks)
    first_all = all_docs[:, 0]
    last_all = all_docs[:, -1]
    source_pos = lax.iota(jnp.int32, seq_count)
    forward_weights = (
        (source_pos[None, :] < source_pos[:, None]) & (last_all[None, :] == first_all[:, None])
    ).astype(F32)
    backward_weights = (
        (source_pos[None, :] > source_pos[:, None]) & (first_all[None, :] == last_all[:, None])
    ).astype(F32)
    carry_state = spread_prefix(tail_state, forward_weights)
    carry_use = block_docs == block_docs[0]
    states_in = (
        local_in + jnp.where(carry_use[:, None, None, None], carry_state[None], 0.0)
    ).astype(BF)
    inter_out = jnp.einsum("bthd,bhde->bthe", query_blk, states_in, preferred_element_type=F32)
    attended = (intra_out + inter_out).reshape(tokens, local_width)
    scaled_grad = norm_gain[None, :] * output_grad.astype(F32)
    square_sum, cross_sum = lax.psum(
        (jnp.sum(attended * attended, axis=1), jnp.sum(attended * scaled_grad, axis=1)), "head"
    )
    full_width = local_width * lax.axis_size("head")
    inverse_rms = lax.rsqrt(square_sum / full_width + norm_eps)
    normed = (attended * inverse_rms[:, None] * norm_gain[None, :]).astype(BF)
    attended_grad = (
        inverse_rms[:, None] * scaled_grad
        - attended * (inverse_rms**3 * cross_sum / full_width)[:, None]
    )
    grad_blk = attended_grad.astype(BF).reshape(shape_four)
    score_grad = jnp.einsum("bthe,bshe->bhts", grad_blk, value_blk, preferred_element_type=F32)
    grad_weights = jnp.where(causal, score_grad, 0.0).astype(BF)
    query_part = jnp.einsum("bhts,bshd->bthd", grad_weights, key_blk, preferred_element_type=F32)
    query_part = query_part + jnp.einsum(
        "bthe,bhde->bthd", grad_blk, states_in, preferred_element_type=F32
    )
    key_intra = jnp.einsum("bhts,bthd->bshd", grad_weights, query_blk, preferred_element_type=F32)
    value_intra = jnp.einsum("bhts,bthe->bshe", att_weights, grad_blk, preferred_element_type=F32)
    block_grad = jnp.einsum("bthd,bthe->bhde", query_blk, grad_blk, preferred_element_type=F32)
    grad_local = jnp.einsum(
        "kj,jhde->khde", later_mask, block_grad, precision=lax.Precision.HIGHEST
    )
    head_weight = (block_docs == block_docs[0]).astype(F32)
    head_state = jnp.einsum("j,jhde->hde", head_weight, block_grad, precision=lax.Precision.HIGHEST)
    grad_state = spread_prefix(head_state, backward_weights)
    grad_use = block_docs == block_docs[-1]
    grads_in = (
        grad_local + jnp.where(grad_use[:, None, None, None], grad_state[None], 0.0)
    ).astype(BF)
    key_part = key_intra + jnp.einsum(
        "bshe,bhde->bshd", value_blk, grads_in, preferred_element_type=F32
    )
    value_part = value_intra + jnp.einsum(
        "bshd,bhde->bshe", key_blk, grads_in, preferred_element_type=F32
    )
    flat_shape = (tokens, local_width)
    return (
        normed,
        query_part.reshape(flat_shape).astype(BF),
        key_part.reshape(flat_shape).astype(BF),
        value_part.reshape(flat_shape).astype(BF),
    )


HALVES = 2
STEPS = 4
VMEM_LIMIT = 48 * 1024 * 1024


def nn(a, b):
    return lax.dot_general(a, b, (((1,), (0,)), ((), ())), preferred_element_type=F32)


def nt(a, b):
    return lax.dot_general(a, b, (((1,), (1,)), ((), ())), preferred_element_type=F32)


def tn(a, b):
    return lax.dot_general(a, b, (((0,), (0,)), ((), ())), preferred_element_type=F32)


def cols(j):
    return slice(j * HEAD_DIM, (j + 1) * HEAD_DIM)


def own_tag(doc_ref):
    return (doc_ref[0] + 1).astype(F32)


def message_slabs(heads):
    return heads * HEAD_DIM // 8 + 1


def put_head(out_ref, head, value):
    out_ref[pl.ds(head * 16, 16)] = value.reshape(16, 8, HEAD_DIM)


def put_tag(out_ref, doc_ref):
    out_ref[out_ref.shape[0] - 1] = jnp.full((8, HEAD_DIM), own_tag(doc_ref), F32)


def kv_kernel(per, doc_ref, k_ref, v_ref, out_ref):
    i = pl.program_id(0)
    for j in range(per):
        put_head(out_ref, i * per + j, tn(k_ref[:, cols(j)], v_ref[:, cols(j)]))

    @pl.when(i == 0)
    def _():
        put_tag(out_ref, doc_ref)


def lower(n):
    return lax.broadcasted_iota(jnp.int32, (n, n), 0) >= lax.broadcasted_iota(jnp.int32, (n, n), 1)


def intra_kernel(per, q_ref, k_ref, v_ref, att_ref, out_ref):
    mask = lower(q_ref.shape[0])
    for j in range(per):
        scores = nt(q_ref[:, cols(j)], k_ref[:, cols(j)])
        att = jnp.where(mask, scores, 0.0).astype(BF)
        att_ref[j] = att
        out_ref[:, cols(j)] = nn(att, v_ref[:, cols(j)])


def gathered(head, doc_ref, flag_ref, r1_ref, r2_ref, r3_ref):
    own = own_tag(doc_ref)
    last = r1_ref.shape[0] - 1
    use3 = flag_ref[0]
    m1 = ((r1_ref[last] == own) & (use3 == 0)).astype(F32)
    m2 = (r2_ref[last] == own).astype(F32)
    m3 = ((r3_ref[last] == own) & (use3 == 1)).astype(F32)
    at = pl.ds(head * 16, 16)
    total = r2_ref[at] * m2 + r1_ref[at] * m1 + r3_ref[at] * m3
    return total.reshape(HEAD_DIM, HEAD_DIM).astype(BF)


def attend_kernel(per, last_half, doc_ref, flag_ref, q_ref, intra_ref, do_ref, gain_ref, r1_ref, r2_ref, r3_ref, *rest):
    if last_half:
        sum_in_ref, att_ref, state_ref, sum_ref, acc_ref = rest
    else:
        att_ref, state_ref, sum_ref, acc_ref = rest
    i = pl.program_id(0)

    @pl.when(i == 0)
    def _():
        if last_half:
            acc_ref[...] = sum_in_ref[...]
        else:
            acc_ref[...] = jnp.zeros_like(acc_ref)

    square = acc_ref[0]
    cross = acc_ref[1]
    for j in range(per):
        state = gathered(i * per + j, doc_ref, flag_ref, r1_ref, r2_ref, r3_ref)
        state_ref[j] = state
        att = intra_ref[:, cols(j)] + nn(q_ref[:, cols(j)], state)
        att_ref[:, cols(j)] = att
        square = square + att * att
        cross = cross + att * (gain_ref[:, cols(j)] * do_ref[:, cols(j)].astype(F32))
    acc_ref[0] = square
    acc_ref[1] = cross

    @pl.when(i == pl.num_programs(0) - 1)
    def _():
        if last_half:
            lane = lax.broadcasted_iota(jnp.int32, square.shape, 1)
            sq = jnp.sum(square, axis=1, keepdims=True)
            cr = jnp.sum(cross, axis=1, keepdims=True)
            sum_ref[...] = jnp.where(lane == 0, sq, jnp.where(lane == 1, cr, 0.0))
        else:
            sum_ref[0] = square
            sum_ref[1] = cross


def scales(mine_ref, other_ref, width):
    total = mine_ref[...] + other_ref[...]
    inverse = lax.rsqrt(total[:, 0:1] / width + norm_eps)
    coef = inverse * inverse * inverse * total[:, 1:2] / width
    return inverse, coef


def grad_kernel(per, width, doc_ref, q_ref, att_ref, do_ref, gain_ref, mine_ref, other_ref, ag_ref, out_ref):
    i = pl.program_id(0)
    inverse, coef = scales(mine_ref, other_ref, width)
    for j in range(per):
        scaled = gain_ref[:, cols(j)] * do_ref[:, cols(j)].astype(F32)
        ag = (inverse * scaled - att_ref[:, cols(j)] * coef).astype(BF)
        ag_ref[:, cols(j)] = ag
        put_head(out_ref, i * per + j, tn(q_ref[:, cols(j)], ag))

    @pl.when(i == 0)
    def _():
        put_tag(out_ref, doc_ref)


def back_kernel(per, width, q_ref, k_ref, v_ref, ag_ref, atw_ref, state_ref, att_ref, gain_ref, mine_ref, other_ref, *rest):
    normed_ref, qg_ref, kin_ref, vin_ref = rest[-4:]
    inverse, _ = scales(mine_ref, other_ref, width)
    mask = lower(q_ref.shape[0])
    for j in range(per):
        q = q_ref[:, cols(j)]
        ag = ag_ref[:, cols(j)]
        normed_ref[:, cols(j)] = (att_ref[:, cols(j)] * inverse * gain_ref[:, cols(j)]).astype(BF)
        gw = jnp.where(mask, nt(ag, v_ref[:, cols(j)]), 0.0).astype(BF)
        qg_ref[:, cols(j)] = (nn(gw, k_ref[:, cols(j)]) + nt(ag, state_ref[j])).astype(BF)
        kin_ref[:, cols(j)] = tn(gw, q)
        vin_ref[:, cols(j)] = tn(atw_ref[j], ag)


def final_kernel(per, doc_ref, flag_ref, k_ref, v_ref, kin_ref, vin_ref, r1_ref, r2_ref, r3_ref, *rest):
    kg_ref, vg_ref = rest[-2:]
    i = pl.program_id(0)
    for j in range(per):
        grads = gathered(i * per + j, doc_ref, flag_ref, r1_ref, r2_ref, r3_ref)
        kg_ref[:, cols(j)] = (kin_ref[:, cols(j)] + nt(v_ref[:, cols(j)], grads)).astype(BF)
        vg_ref[:, cols(j)] = (vin_ref[:, cols(j)] + nn(k_ref[:, cols(j)], grads)).astype(BF)


def call(kernel, name, in_specs, out_specs, out_shape, scratch=(), aliases=None, flops=0, steps=STEPS):
    return pl.pallas_call(
        kernel,
        grid=(steps,),
        in_specs=in_specs,
        out_specs=out_specs,
        out_shape=out_shape,
        scratch_shapes=list(scratch),
        input_output_aliases=aliases or {},
        name=name,
        cost_estimate=pl.CostEstimate(flops=flops, transcendentals=0, bytes_accessed=4 << 20),
        compiler_params=pltpu.CompilerParams(
            dimension_semantics=("arbitrary",), vmem_limit_bytes=VMEM_LIMIT
        ),
    )


def pairs_of(seq, head, rule):
    out = []
    for s in range(seq):
        for h in range(head):
            to = rule(s, h)
            if to is not None and 0 <= to < seq:
                out.append((s * head + h, to * head + h))
    return out


def routes(seq, head, sign):
    first = pairs_of(seq, head, lambda s, h: s ^ 1 if h % 2 == 0 else s + 2 * sign)
    second = pairs_of(seq, head, lambda s, h: s + 2 * sign if h % 2 == 0 else s + sign)
    parity = 0 if sign > 0 else 1
    third = pairs_of(
        seq, head, lambda s, h: s + 2 * sign if h % 2 == 0 and s % 2 == parity else None
    )
    return first, second, third


def send(x, pairs):
    return lax.ppermute(x, ("seq", "head"), pairs)


def join_kernel(role_ref, own_ref, got_ref, out_ref):
    last = own_ref.shape[0] - 1
    same = (own_ref[last] == got_ref[last]).astype(F32)

    @pl.when(role_ref[0] == 1)
    def _():
        out_ref[...] = got_ref[...] + own_ref[...] * same[None]
        out_ref[last] = got_ref[last]

    @pl.when(role_ref[0] == 0)
    def _():
        out_ref[...] = own_ref[...] + got_ref[...] * same[None]
        out_ref[last] = own_ref[last]


def block_body(queries, key_vectors, value_vectors, output_grad, norm_gain, block_docs):
    tokens, width = queries.shape
    heads = width // HEAD_DIM
    seq = lax.axis_size("seq")
    head = lax.axis_size("head")
    full = width * head
    hh = heads // HALVES
    steps = STEPS
    per = hh // steps
    pw = per * HEAD_DIM
    hw = hh * HEAD_DIM
    gain = norm_gain.reshape(1, width)
    seq_at = lax.axis_index("seq")
    core_at = lax.axis_index("head")
    even_core = core_at % 2 == 0
    odd_block = seq_at % 2 == 1
    smem = pl.BlockSpec(memory_space=pltpu.SMEM)
    slabs = message_slabs(hh)
    message = jax.ShapeDtypeStruct((slabs, 8, HEAD_DIM), F32)
    whole = pl.BlockSpec((slabs, 8, HEAD_DIM), lambda i: (0, 0, 0))
    sums_spec = pl.BlockSpec((tokens, HEAD_DIM), lambda i: (0, 0))
    local = pl.BlockSpec((tokens, pw), lambda i: (0, i))
    square = pl.BlockSpec((per, tokens, tokens), lambda i: (i, 0, 0))
    states = pl.BlockSpec((per, HEAD_DIM, HEAD_DIM), lambda i: (i, 0, 0))
    acc_shape = jax.ShapeDtypeStruct((2, tokens, HEAD_DIM), F32)
    acc_spec = pl.BlockSpec((2, tokens, HEAD_DIM), lambda i: (0, 0, 0))
    untouched = pl.BlockSpec(memory_space=pl.ANY)
    wide = jax.ShapeDtypeStruct((tokens, width), BF)
    half32 = jax.ShapeDtypeStruct((tokens, hw), F32)

    def part(n):
        return pl.BlockSpec((tokens, pw), lambda i: (0, i + n * steps))

    def gain_part(n):
        return pl.BlockSpec((1, pw), lambda i: (0, i + n * steps))

    mm = 2 * tokens * HEAD_DIM * HEAD_DIM * hh

    def exchange(messages, sign):
        first, second, third = routes(seq, head, sign)
        low_block = odd_block if sign < 0 else ~odd_block
        got1 = [send(m, first) for m in messages]
        use3 = (even_core & low_block).astype(jnp.int32).reshape(1)
        on = [
            call(join_kernel, f"join{n}", [smem, whole, whole], whole, message, steps=1)(use3, m, g)
            for n, (m, g) in enumerate(zip(messages, got1))
        ]
        got2 = [send(m, second) for m in on]
        got3 = [send(g, third) for g in got2]
        return use3, list(zip(got1, got2, got3))

    kv = [
        call(functools.partial(kv_kernel, per), f"kv{n}", [smem, part(n), part(n)], whole, message, flops=mm)(
            block_docs, key_vectors, value_vectors
        )
        for n in range(HALVES)
    ]
    use3, got = exchange(kv, 1)
    intra = [
        call(
            functools.partial(intra_kernel, per), f"intra{n}",
            [part(n)] * 3, [square, local],
            [jax.ShapeDtypeStruct((hh, tokens, tokens), BF), half32], flops=4 * mm,
        )(queries, key_vectors, value_vectors)
        for n in range(HALVES)
    ]
    attended, state, sums = [], [], None
    for n in range(HALVES):
        last = n == HALVES - 1
        extra = [acc_spec] if n else []
        att, st, sums = call(
            functools.partial(attend_kernel, per, last), f"attend{n}",
            [smem, smem, part(n), local, part(n), gain_part(n), whole, whole, whole] + extra,
            [local, states, sums_spec if last else acc_spec],
            [
                half32,
                jax.ShapeDtypeStruct((hh, HEAD_DIM, HEAD_DIM), BF),
                jax.ShapeDtypeStruct((tokens, HEAD_DIM), F32) if last else acc_shape,
            ],
            scratch=[pltpu.VMEM((2, tokens, HEAD_DIM), F32)], flops=mm,
        )(block_docs, use3, queries, intra[n][1], output_grad, gain, *got[n], *([sums] if n else []))
        attended.append(att)
        state.append(st)
    other = lax.ppermute(sums, "head", [(c, c ^ 1) for c in range(head)])
    ag, bg = [], []
    for n in range(HALVES):
        a, b = call(
            functools.partial(grad_kernel, per, full), f"grad{n}",
            [smem, part(n), local, part(n), gain_part(n), sums_spec, sums_spec],
            [local, whole], [jax.ShapeDtypeStruct((tokens, hw), BF), message], flops=mm,
        )(block_docs, queries, attended[n], output_grad, gain, sums, other)
        ag.append(a)
        bg.append(b)
    use3b, gotb = exchange(bg, -1)
    kin, vin, normed, query_grad = [], [], None, None
    for n in range(HALVES):
        extra = [normed, query_grad] if n else []
        base = 10
        normed, query_grad, ki, vi = call(
            functools.partial(back_kernel, per, full), f"back{n}",
            [part(n)] * 3 + [local, square, states, local, gain_part(n), sums_spec, sums_spec] + [untouched] * len(extra),
            [part(n), part(n), local, local], [wide, wide, half32, half32],
            aliases={base: 0, base + 1: 1} if n else None, flops=7 * mm,
        )(queries, key_vectors, value_vectors, ag[n], intra[n][0], state[n], attended[n], gain, sums, other, *extra)
        kin.append(ki)
        vin.append(vi)
    key_grad, value_grad = None, None
    for n in range(HALVES):
        extra = [key_grad, value_grad] if n else []
        base = 9
        key_grad, value_grad = call(
            functools.partial(final_kernel, per), f"final{n}",
            [smem, smem, part(n), part(n), local, local, whole, whole, whole] + [untouched] * len(extra),
            [part(n), part(n)], [wide, wide],
            aliases={base: 0, base + 1: 1} if n else None, flops=2 * mm,
        )(block_docs, use3b, key_vectors, value_vectors, kin[n], vin[n], *gotb[n], *extra)
    return normed, query_grad, key_grad, value_grad


def solution(mesh):
    rows = P(("groups", "seq"), "head")
    in_specs = (rows, rows, rows, rows, P("head"), P(("groups", "seq")))
    out_specs = (rows, rows, rows, rows)
    seq = mesh.shape["seq"]
    short = seq == 8 and mesh.shape["head"] == 2

    def body(queries, key_vectors, value_vectors, output_grad, norm_gain, block_docs):
        one = block_docs.shape[0] == 1
        fn = block_body if short and one else general_body
        return fn(queries, key_vectors, value_vectors, output_grad, norm_gain, block_docs)

    return jax.shard_map(body, mesh=mesh, in_specs=in_specs, out_specs=out_specs, check_vma=False)
```

time: 157 us -> 121 us (0.77)
  blocking collectives: 55.9 us -> 0 us
  Pallas kernels: 0 us -> 39.7 us
  starting transfers between devices: 15.3 us -> 38.2 us
  matrix products: 21.8 us -> 0 us
  local copies, waits for them, and re-layouts: 19.7 us -> 6.17 us
  other arithmetic: 8.37 us -> 0 us
    pallas_call x0 -> x16, Pallas kernels: none -> 39.7 us  [the longest x2 10.8 us: block_body(): call(functools.partial(back_kernel, per, full), f'back{n}', [part(n)] * 3...]
    ppermute x0 -> x13, starting transfers between devices: none -> 38.2 us  [the longest x12 38.1 us: send(): return lax.ppermute(x, ('seq', 'head'), pairs)]
    ppermute x0 -> x13, waiting for transfers between devices: none -> 34.1 us  [the longest x12 32.8 us: send(): return lax.ppermute(x, ('seq', 'head'), pairs)]
    all_to_all x3 -> x0, waiting for transfers between devices: 33.7 us -> none  [the longest x2 33.7 us: spread_prefix(): lax.all_to_all(mixed, 'seq', split_axis=0, concat_axis=0, tiled=True)]
    all_to_all x1 -> x0, blocking collectives: 29.5 us -> none  [spread_prefix(): lax.all_to_all(flat_state, 'seq', split_axis=0, concat_axis=0, tiled=True)]
    unnamed x1 -> x0, blocking collectives: 23.9 us -> none
    dot_general x14 -> x0, matrix products: 21.8 us -> none  [the longest x1 3.37 us: body(): jnp.einsum('bhts,bthe->bshe', att_weights, grad_blk, preferred_element_ty...]
    all_to_all x3 -> x0, starting transfers between devices: 15.3 us -> none  [the longest x2 8.01 us: spread_prefix(): lax.all_to_all(mixed, 'seq', split_axis=0, concat_axis=0, tiled=True)]
  transfers between devices with their start and end apart: 3 -> 13, of which waited for: 2 -> 9; matrix products, arithmetic and copies ran while one was open for 10% -> 0% of each run, Pallas kernels for 0% -> 25%
where the time goes in v1:
time: 121 us; the launch traced here: 120 us
  Pallas kernels  39.7 us (33%)
  starting transfers between devices  38.2 us (32%)
  waiting for transfers between devices  34.1 us (28%)
  local copies, waits for them, and re-layouts  6.17 us (5%)
  between operations  1.71 us (1%)
    ppermute x12, starting transfers between devices, send(): return lax.ppermute(x, ('seq', 'head'), pairs)  38.1 us
    ppermute x12, waiting for transfers between devices, send(): return lax.ppermute(x, ('seq', 'head'), pairs)  32.8 us
    pallas_call x2, Pallas kernels, block_body(): call(functools.partial(back_kernel, per, full), f'back{n}', [part(n)] * 3...  10.8 us
    pallas_call x2, Pallas kernels, block_body(): call(functools.partial(attend_kernel, per, last), f'attend{n}', [smem, sm...  6.38 us
    unnamed x48, local copies, waits for them, and re-layouts  6.17 us
    pallas_call x2, Pallas kernels, block_body(): call(functools.partial(final_kernel, per), f'final{n}', [smem, smem, part...  5.76 us
    pallas_call x2, Pallas kernels, block_body(): call(functools.partial(grad_kernel, per, full), f'grad{n}', [smem, part(n...  5.21 us
    pallas_call x2, Pallas kernels, block_body(): call(functools.partial(intra_kernel, per), f'intra{n}', [part(n)] * 3, [s...  4.82 us
  transfers between devices with their start and end apart: 13, of which 9 were waited for; matrix products, arithmetic and copies ran while one was open for 0% of the time, Pallas kernels for 25%

profile of v1, /device:TPU:0, one launch (start us, length us, event | category | flops | bytes accessed | tf_op | source)
XLA Modules:
  0.0 119.9 jit_solution(16633174300612873498)
XLA Ops:
  1.3 0.0 copy-start
  1.3 1.2 %copy-done = bf16[256,2048]{1,0:T(8,128)(2,1)S(1)} copy-done((bf16[256,2048]{1,0:T(8,128)(2,1)S(1)}, bf16[256,2048]{1,0:T(8,128)(2,1)}, u32[]{:S(2)}) %copy-start) | copy-done | bytes 1048600
  2.5 1.2 %copy-done.2 = bf16[256,2048]{1,0:T(8,128)(2,1)S(1)} copy-done((bf16[256,2048]{1,0:T(8,128)(2,1)S(1)}, bf16[256,2048]{1,0:T(8,128)(2,1)}, u32[]{:S(2)}) %copy-start.2) | copy-done | bytes 1048600
  3.7 1.1 kv0.1.own_ref
  4.9 4.8 %collective-permute-start.3 = (f32[129,8,128]{2,1,0:T(8,128)S(1)}, f32[129,8,128]{2,1,0:T(8,128)S(1)}, u32[]{:S(2)}, u32[]{:S(2)}) collective-permute-start(f32[129,8,128]{2,1,0:T(8,128)S(1)} %kv0.1.own_ref), channel_id=1, source_target_pairs={{0,2},{1,5},{2,0},{3,7},{4,6},{5,9},{6,4},{7,11},{8,10},{9,13},{10... | collective-permute-start | bytes 1585160 | tf_op jit(solution)/shard_map/ppermute | solution.py:307
  9.7 1.9 %kv1.1.own_ref = f32[129,8,128]{2,1,0:T(8,128)} custom-call(s32[1]{0:T(128)S(6)} %copy.18.doc_ref, bf16[256,2048]{1,0:T(8,128)(2,1)S(1)} %copy-done, bf16[256,2048]{1,0:T(8,128)(2,1)S(1)} %copy-done.2), custom_call_target="tpu_custom_call" | custom-call | flops 67108864 | bytes 4194304 | tf_op jit(solution)/shard_map/kv1/pallas_call | solution.py:377
  11.6 1.9 %collective-permute-start = (f32[129,8,128]{2,1,0:T(8,128)}, f32[129,8,128]{2,1,0:T(8,128)}, u32[]{:S(2)}, u32[]{:S(2)}) collective-permute-start(f32[129,8,128]{2,1,0:T(8,128)} %kv1.1.own_ref), channel_id=1, source_target_pairs={{0,2},{1,5},{2,0},{3,7},{4,6},{5,9},{6,4},{7,11},{8,10},{9,13},{10... | collective-permute-start | bytes 1585160 | tf_op jit(solution)/shard_map/ppermute | solution.py:307
  13.6 3.3 %collective-permute-done.3.got_ref.r1_ref = f32[129,8,128]{2,1,0:T(8,128)S(1)} collective-permute-done((f32[129,8,128]{2,1,0:T(8,128)S(1)}, f32[129,8,128]{2,1,0:T(8,128)S(1)}, u32[]{:S(2)}, u32[]{:S(2)}) %collective-permute-start.3) | collective-permute-done | bytes 528416 | tf_op jit(solution)/shard_map/ppermute | solution.py:307
  16.9 1.0 copy-done.12
  18.0 0.1 join0.2
  18.0 0.0 copy-start.9
  18.1 0.8 copy-done.9
  18.8 4.2 %collective-permute-start.4 = (f32[129,8,128]{2,1,0:T(8,128)S(1)}, f32[129,8,128]{2,1,0:T(8,128)S(1)}, u32[]{:S(2)}, u32[]{:S(2)}) collective-permute-start(f32[129,8,128]{2,1,0:T(8,128)S(1)} %join0.2), channel_id=1, source_target_pairs={{0,4},{1,3},{2,6},{3,5},{4,8},{5,7},{6,10},{7,9},{8,12},{9,11},{10... | collective-permute-start | bytes 1585160 | tf_op jit(solution)/shard_map/ppermute | solution.py:307
  23.0 0.2 collective-permute-done.got_ref.r1_ref
  23.2 1.3 %join1.2 = f32[129,8,128]{2,1,0:T(8,128)S(1)} custom-call(s32[1]{0:T(128)} %bitcast.role_ref.flag_ref, f32[129,8,128]{2,1,0:T(8,128)} %kv1.1.own_ref, f32[129,8,128]{2,1,0:T(8,128)} %collective-permute-done.got_ref.r1_ref), custom_call_target="tpu_custom_call" | custom-call | bytes 4194304 | tf_op jit(solution)/shard_map/join1/pallas_call | solution.py:369
  24.5 3.5 %collective-permute-start.1 = (f32[129,8,128]{2,1,0:T(8,128)S(1)}, f32[129,8,128]{2,1,0:T(8,128)S(1)}, u32[]{:S(2)}, u32[]{:S(2)}) collective-permute-start(f32[129,8,128]{2,1,0:T(8,128)S(1)} %join1.2), channel_id=1, source_target_pairs={{0,4},{1,3},{2,6},{3,5},{4,8},{5,7},{6,10},{7,9},{8,12},{9,11},{10... | collective-permute-start | bytes 1585160 | tf_op jit(solution)/shard_map/ppermute | solution.py:307
  28.0 1.7 %collective-permute-done.4.r2_ref = f32[129,8,128]{2,1,0:T(8,128)S(1)} collective-permute-done((f32[129,8,128]{2,1,0:T(8,128)S(1)}, f32[129,8,128]{2,1,0:T(8,128)S(1)}, u32[]{:S(2)}, u32[]{:S(2)}) %collective-permute-start.4) | collective-permute-done | bytes 528416 | tf_op jit(solution)/shard_map/ppermute | solution.py:307
  29.7 4.4 %collective-permute-start.5 = (f32[129,8,128]{2,1,0:T(8,128)S(1)}, f32[129,8,128]{2,1,0:T(8,128)S(1)}, u32[]{:S(2)}, u32[]{:S(2)}) collective-permute-start(f32[129,8,128]{2,1,0:T(8,128)S(1)} %collective-permute-done.4.r2_ref), channel_id=1, source_target_pairs={{0,4},{4,8},{8,12},{16,20},{20,24},{24,28}} | collective-permute-start | bytes 1585160 | tf_op jit(solution)/shard_map/ppermute | solution.py:307
  34.1 1.2 %collective-permute-done.1.r2_ref = f32[129,8,128]{2,1,0:T(8,128)S(1)} collective-permute-done((f32[129,8,128]{2,1,0:T(8,128)S(1)}, f32[129,8,128]{2,1,0:T(8,128)S(1)}, u32[]{:S(2)}, u32[]{:S(2)}) %collective-permute-start.1) | collective-permute-done | bytes 528416 | tf_op jit(solution)/shard_map/ppermute | solution.py:307
  35.4 4.4 %collective-permute-start.2 = (f32[129,8,128]{2,1,0:T(8,128)S(1)}, f32[129,8,128]{2,1,0:T(8,128)S(1)}, u32[]{:S(2)}, u32[]{:S(2)}) collective-permute-start(f32[129,8,128]{2,1,0:T(8,128)S(1)} %collective-permute-done.1.r2_ref), channel_id=1, source_target_pairs={{0,4},{4,8},{8,12},{16,20},{20,24},{24,28}} | collective-permute-start | bytes 1585160 | tf_op jit(solution)/shard_map/ppermute | solution.py:307
  39.8 2.4 %intra1.1 = (bf16[8,256,256]{2,1,0:T(8,128)(2,1)S(1)}, f32[256,1024]{1,0:T(8,128)S(1)}) custom-call(bf16[256,2048]{1,0:T(8,128)(2,1)S(1)} %copy-done.5, bf16[256,2048]{1,0:T(8,128)(2,1)S(1)} %copy-done.1, bf16[256,2048]{1,0:T(8,128)(2,1)S(1)} %copy-done.3), custom_call_target="tpu_custom_call" | custom-call | flops 268435456 | bytes 4194304 | tf_op jit(solution)/shard_map/intra1/pallas_call | solution.py:384
  42.2 0.0 copy-start.13
  42.3 2.4 %intra0.1 = (bf16[8,256,256]{2,1,0:T(8,128)(2,1)S(1)}, f32[256,1024]{1,0:T(8,128)S(1)}) custom-call(bf16[256,2048]{1,0:T(8,128)(2,1)S(1)} %copy-done.5, bf16[256,2048]{1,0:T(8,128)(2,1)S(1)} %copy-done.1, bf16[256,2048]{1,0:T(8,128)(2,1)S(1)} %copy-done.3), custom_call_target="tpu_custom_call" | custom-call | flops 268435456 | bytes 4194304 | tf_op jit(solution)/shard_map/intra0/pallas_call | solution.py:384
  44.7 1.0 copy-done.14
  45.7 2.8 %attend0.1 = (f32[256,1024]{1,0:T(8,128)S(1)}, bf16[8,128,128]{2,1,0:T(8,128)(2,1)S(1)}, f32[2,256,128]{2,1,0:T(8,128)S(1)}) custom-call(s32[1]{0:T(128)S(6)} %copy.18.doc_ref, s32[1]{0:T(128)} %bitcast.role_ref.flag_ref, bf16[256,2048]{1,0:T(8,128)(2,1)S(1)} %copy-done.5, f32[256,1024]{1,0:T(8,128)S(1)} %get-tuple-element.31.intra_ref, ...), custom_call_target="tpu_custom_call" | custom-call | flops 67108864 | bytes 4194304 | tf_op jit(solution)/shard_map/attend0/pallas_call | solution.py:395
  48.5 3.6 %attend1.1 = (f32[256,1024]{1,0:T(8,128)S(1)}, bf16[8,128,128]{2,1,0:T(8,128)(2,1)S(1)}, f32[256,128]{1,0:T(8,128)S(1)}) custom-call(s32[1]{0:T(128)S(6)} %copy.18.doc_ref, s32[1]{0:T(128)} %bitcast.role_ref.flag_ref, bf16[256,2048]{1,0:T(8,128)(2,1)S(1)} %copy-done.5, f32[256,1024]{1,0:T(8,128)S(1)} %get-tuple-element.30.intra_ref, ...), custom_call_target="tpu_custom_call" | custom-call | flops 67108864 | bytes 4194304 | tf_op jit(solution)/shard_map/attend1/pallas_call | solution.py:395
  52.2 0.0 copy-start.7
  52.2 0.1 collective-permute-start.6
  52.3 1.3 %collective-permute-done.6.other_ref = f32[256,128]{1,0:T(8,128)S(1)} collective-permute-done((f32[256,128]{1,0:T(8,128)S(1)}, f32[256,128]{1,0:T(8,128)S(1)}, u32[]{:S(2)}, u32[]{:S(2)}) %collective-permute-start.6) | collective-permute-done | bytes 131104 | tf_op jit(solution)/shard_map/ppermute | solution.py:408
  53.6 2.6 %grad0.1 = (bf16[256,1024]{1,0:T(8,128)(2,1)S(1)}, f32[129,8,128]{2,1,0:T(8,128)}) custom-call(s32[1]{0:T(128)S(6)} %copy.18.doc_ref, bf16[256,2048]{1,0:T(8,128)(2,1)S(1)} %copy-done.5, f32[256,1024]{1,0:T(8,128)S(1)} %get-tuple-element.38.att_ref, bf16[256,2048]{1,0:T(8,128)(2,1)S(1)} %copy-done.6, f32[1,2048]{1,0:T(1,128)S(1)} %bitcast.5, ...), custom_call_target="tpu_custom_call" | custom-call | flops 67108864 | bytes 4194304 | tf_op jit(solution)/shard_map/grad0/pallas_call | solution.py:411
  56.2 8.9 %collective-permute-start.10 = (f32[129,8,128]{2,1,0:T(8,128)}, f32[129,8,128]{2,1,0:T(8,128)}, u32[]{:S(2)}, u32[]{:S(2)}) collective-permute-start(f32[129,8,128]{2,1,0:T(8,128)} %get-tuple-element.51.own_ref), channel_id=1, source_target_pairs={{0,2},{2,0},{4,6},{5,1},{6,4},{7,3},{8,10},{9,5},{10,8},{11,7},{12... | collective-permute-start | bytes 1585160 | tf_op jit(solution)/shard_map/ppermute | solution.py:307
  65.2 2.6 %grad1.1 = (bf16[256,1024]{1,0:T(8,128)(2,1)S(1)}, f32[129,8,128]{2,1,0:T(8,128)}) custom-call(s32[1]{0:T(128)S(6)} %copy.18.doc_ref, bf16[256,2048]{1,0:T(8,128)(2,1)S(1)} %copy-done.5, f32[256,1024]{1,0:T(8,128)S(1)} %get-tuple-element.33.att_ref, bf16[256,2048]{1,0:T(8,128)(2,1)S(1)} %copy-done.6, f32[1,2048]{1,0:T(1,128)S(1)} %bitcast.6, ...), custom_call_target="tpu_custom_call" | custom-call | flops 67108864 | bytes 4194304 | tf_op jit(solution)/shard_map/grad1/pallas_call | solution.py:411
  67.8 0.8 copy-done.15
  68.6 1.9 %collective-permute-start.7 = (f32[129,8,128]{2,1,0:T(8,128)}, f32[129,8,128]{2,1,0:T(8,128)S(1)}, u32[]{:S(2)}, u32[]{:S(2)}) collective-permute-start(f32[129,8,128]{2,1,0:T(8,128)} %get-tuple-element.48.own_ref), channel_id=1, source_target_pairs={{0,2},{2,0},{4,6},{5,1},{6,4},{7,3},{8,10},{9,5},{10,8},{11,7},{12... | collective-permute-start | bytes 1585160 | tf_op jit(solution)/shard_map/ppermute | solution.py:307
  70.5 2.1 %collective-permute-done.10.got_ref.r1_ref = f32[129,8,128]{2,1,0:T(8,128)} collective-permute-done((f32[129,8,128]{2,1,0:T(8,128)}, f32[129,8,128]{2,1,0:T(8,128)}, u32[]{:S(2)}, u32[]{:S(2)}) %collective-permute-start.10) | collective-permute-done | bytes 528416 | tf_op jit(solution)/shard_map/ppermute | solution.py:307
  72.6 1.3 %join0.3 = f32[129,8,128]{2,1,0:T(8,128)S(1)} custom-call(s32[1]{0:T(128)} %bitcast.2.role_ref.flag_ref, f32[129,8,128]{2,1,0:T(8,128)} %get-tuple-element.51.own_ref, f32[129,8,128]{2,1,0:T(8,128)} %collective-permute-done.10.got_ref.r1_ref), custom_call_target="tpu_custom_call" | custom-call | bytes 4194304 | tf_op jit(solution)/shard_map/join0/pallas_call | solution.py:369
  73.9 1.4 %collective-permute-start.11 = (f32[129,8,128]{2,1,0:T(8,128)S(1)}, f32[129,8,128]{2,1,0:T(8,128)S(1)}, u32[]{:S(2)}, u32[]{:S(2)}) collective-permute-start(f32[129,8,128]{2,1,0:T(8,128)S(1)} %join0.3), channel_id=1, source_target_pairs={{3,1},{4,0},{5,3},{6,2},{7,5},{8,4},{9,7},{10,6},{11,9},{12,8},{13... | collective-permute-start | bytes 1585160 | tf_op jit(solution)/shard_map/ppermute | solution.py:307
  75.4 5.5 %collective-permute-done.7.got_ref.r1_ref = f32[129,8,128]{2,1,0:T(8,128)S(1)} collective-permute-done((f32[129,8,128]{2,1,0:T(8,128)}, f32[129,8,128]{2,1,0:T(8,128)S(1)}, u32[]{:S(2)}, u32[]{:S(2)}) %collective-permute-start.7) | collective-permute-done | bytes 528416 | tf_op jit(solution)/shard_map/ppermute | solution.py:307
  80.9 1.1 join1.3
  82.0 1.3 %collective-permute-start.8 = (f32[129,8,128]{2,1,0:T(8,128)S(1)}, f32[129,8,128]{2,1,0:T(8,128)S(1)}, u32[]{:S(2)}, u32[]{:S(2)}) collective-permute-start(f32[129,8,128]{2,1,0:T(8,128)S(1)} %join1.3), channel_id=1, source_target_pairs={{3,1},{4,0},{5,3},{6,2},{7,5},{8,4},{9,7},{10,6},{11,9},{12,8},{13... | collective-permute-start | bytes 1585160 | tf_op jit(solution)/shard_map/ppermute | solution.py:307
  83.3 8.0 %collective-permute-done.11.r2_ref = f32[129,8,128]{2,1,0:T(8,128)S(1)} collective-permute-done((f32[129,8,128]{2,1,0:T(8,128)S(1)}, f32[129,8,128]{2,1,0:T(8,128)S(1)}, u32[]{:S(2)}, u32[]{:S(2)}) %collective-permute-start.11) | collective-permute-done | bytes 528416 | tf_op jit(solution)/shard_map/ppermute | solution.py:307
  91.2 0.7 collective-permute-start.12
  91.9 10.6 %collective-permute-done.8.r2_ref = f32[129,8,128]{2,1,0:T(8,128)S(1)} collective-permute-done((f32[129,8,128]{2,1,0:T(8,128)S(1)}, f32[129,8,128]{2,1,0:T(8,128)S(1)}, u32[]{:S(2)}, u32[]{:S(2)}) %collective-permute-start.8) | collective-permute-done | bytes 528416 | tf_op jit(solution)/shard_map/ppermute | solution.py:307
  102.6 0.7 collective-permute-start.9
  103.3 5.4 %back0.1 = (bf16[256,2048]{1,0:T(8,128)(2,1)}, bf16[256,2048]{1,0:T(8,128)(2,1)}, f32[256,1024]{1,0:T(8,128)S(1)}, f32[256,1024]{1,0:T(8,128)S(1)}) custom-call(bf16[256,2048]{1,0:T(8,128)(2,1)S(1)} %copy-done.5, bf16[256,2048]{1,0:T(8,128)(2,1)S(1)} %copy-done.1, bf16[256,2048]{1,0:T(8,128)(2,1)} %v_ref.15, bf16[256,1024]{1,0:T(8,128)(2,1)S(1)} %copy-done.18, ...), custom_call_target="tpu_custom_call" | custom-call | flops 469762048 | bytes 4194304 | tf_op jit(solution)/shard_map/back0/pallas_call | solution.py:423
  108.7 5.4 %back1.1 = (bf16[256,2048]{1,0:T(8,128)(2,1)}, bf16[256,2048]{1,0:T(8,128)(2,1)}, f32[256,1024]{1,0:T(8,128)S(1)}, f32[256,1024]{1,0:T(8,128)S(1)}) custom-call(bf16[256,2048]{1,0:T(8,128)(2,1)S(1)} %copy-done.5, bf16[256,2048]{1,0:T(8,128)(2,1)S(1)} %copy-done.1, bf16[256,2048]{1,0:T(8,128)(2,1)} %v_ref.15, ...), custom_call_target="tpu_custom_call", output_to_operand_aliasing={{0}: (10, {}), {1}: (11, {})} | custom-call | flops 469762048 | bytes 4194304 | tf_op jit(solution)/shard_map/back1/pallas_call | solution.py:423
  114.2 3.4 %final0.1 = (bf16[256,2048]{1,0:T(8,128)(2,1)}, bf16[256,2048]{1,0:T(8,128)(2,1)}) custom-call(s32[1]{0:T(128)S(6)} %copy.18.doc_ref, s32[1]{0:T(128)} %bitcast.2.role_ref.flag_ref, bf16[256,2048]{1,0:T(8,128)(2,1)S(1)} %copy-done.1, bf16[256,2048]{1,0:T(8,128)(2,1)S(1)} %copy-done.4, f32[256,1024]{1,0:T(8,128)S(1)} %get-tuple-element.49.kin_ref, ...), custom_call_target="tpu_custom_call" | custom-call | flops 134217728 | bytes 4194304 | tf_op jit(solution)/shard_map/final0/pallas_call | solution.py:435
  117.5 2.4 %final1.1 = (bf16[256,2048]{1,0:T(8,128)(2,1)}, bf16[256,2048]{1,0:T(8,128)(2,1)}) custom-call(s32[1]{0:T(128)S(6)} %copy.18.doc_ref, s32[1]{0:T(128)} %bitcast.2.role_ref.flag_ref, bf16[256,2048]{1,0:T(8,128)(2,1)S(1)} %copy-done.1, bf16[256,2048]{1,0:T(8,128)(2,1)S(1)} %copy-done.4, ...), custom_call_target="tpu_custom_call", output_to_operand_aliasing={{0}: (9, {}), {1}: (10, {})} | custom-call | flops 134217728 | bytes 4194304 | tf_op jit(solution)/shard_map/final1/pallas_call | solution.py:435
  (42 shorter events, 0.1 us)
Async XLA Ops:
  1.3 1.2 %copy-start = (bf16[256,2048]{1,0:T(8,128)(2,1)S(1)}, bf16[256,2048]{1,0:T(8,128)(2,1)}, u32[]{:S(2)}) copy-start(bf16[256,2048]{1,0:T(8,128)(2,1)} %k_ref.15) | copy-start | bytes 3145732
  2.5 1.2 %copy-start.2 = (bf16[256,2048]{1,0:T(8,128)(2,1)S(1)}, bf16[256,2048]{1,0:T(8,128)(2,1)}, u32[]{:S(2)}) copy-start(bf16[256,2048]{1,0:T(8,128)(2,1)} %v_ref.15) | copy-start | bytes 3145732
  4.8 6.8 %copy-start.11 = (f32[129,8,128]{2,1,0:T(8,128)}, f32[129,8,128]{2,1,0:T(8,128)S(1)}, u32[]{:S(2)}) copy-start(f32[129,8,128]{2,1,0:T(8,128)S(1)} %kv0.1.own_ref) | copy-start | bytes 1585156
  4.9 12.0 %collective-permute-start.3 = (f32[129,8,128]{2,1,0:T(8,128)S(1)}, f32[129,8,128]{2,1,0:T(8,128)S(1)}, u32[]{:S(2)}, u32[]{:S(2)}) collective-permute-start(f32[129,8,128]{2,1,0:T(8,128)S(1)} %kv0.1.own_ref), channel_id=1, source_target_pairs={{0,2},{1,5},{2,0},{3,7},{4,6},{5,9},{6,4},{7,11},{8,10},{9,13},{10... | collective-permute-start | bytes 1585160 | tf_op jit(solution)/shard_map/ppermute | solution.py:307
  11.6 11.6 %collective-permute-start = (f32[129,8,128]{2,1,0:T(8,128)}, f32[129,8,128]{2,1,0:T(8,128)}, u32[]{:S(2)}, u32[]{:S(2)}) collective-permute-start(f32[129,8,128]{2,1,0:T(8,128)} %kv1.1.own_ref), channel_id=1, source_target_pairs={{0,2},{1,5},{2,0},{3,7},{4,6},{5,9},{6,4},{7,11},{8,10},{9,13},{10... | collective-permute-start | bytes 1585160 | tf_op jit(solution)/shard_map/ppermute | solution.py:307
  16.9 1.0 copy-start.12
  17.9 21.8 %copy-start.3 = (bf16[256,2048]{1,0:T(8,128)(2,1)S(1)}, bf16[256,2048]{1,0:T(8,128)(2,1)}, u32[]{:S(2)}) copy-start(bf16[256,2048]{1,0:T(8,128)(2,1)} %v_ref.15) | copy-start | bytes 3145732
  18.0 21.8 %copy-start.5 = (bf16[256,2048]{1,0:T(8,128)(2,1)S(1)}, bf16[256,2048]{1,0:T(8,128)(2,1)}, u32[]{:S(2)}) copy-start(bf16[256,2048]{1,0:T(8,128)(2,1)} %q_ref.15) | copy-start | bytes 3145732
  18.0 0.8 copy-start.9
  18.8 21.0 %copy-start.1 = (bf16[256,2048]{1,0:T(8,128)(2,1)S(1)}, bf16[256,2048]{1,0:T(8,128)(2,1)}, u32[]{:S(2)}) copy-start(bf16[256,2048]{1,0:T(8,128)(2,1)} %k_ref.15) | copy-start | bytes 3145732
  18.8 10.9 %collective-permute-start.4 = (f32[129,8,128]{2,1,0:T(8,128)S(1)}, f32[129,8,128]{2,1,0:T(8,128)S(1)}, u32[]{:S(2)}, u32[]{:S(2)}) collective-permute-start(f32[129,8,128]{2,1,0:T(8,128)S(1)} %join0.2), channel_id=1, source_target_pairs={{0,4},{1,3},{2,6},{3,5},{4,8},{5,7},{6,10},{7,9},{8,12},{9,11},{10... | collective-permute-start | bytes 1585160 | tf_op jit(solution)/shard_map/ppermute | solution.py:307
  24.5 10.9 %collective-permute-start.1 = (f32[129,8,128]{2,1,0:T(8,128)S(1)}, f32[129,8,128]{2,1,0:T(8,128)S(1)}, u32[]{:S(2)}, u32[]{:S(2)}) collective-permute-start(f32[129,8,128]{2,1,0:T(8,128)S(1)} %join1.2), channel_id=1, source_target_pairs={{0,4},{1,3},{2,6},{3,5},{4,8},{5,7},{6,10},{7,9},{8,12},{9,11},{10... | collective-permute-start | bytes 1585160 | tf_op jit(solution)/shard_map/ppermute | solution.py:307
  29.7 16.0 %collective-permute-start.5 = (f32[129,8,128]{2,1,0:T(8,128)S(1)}, f32[129,8,128]{2,1,0:T(8,128)S(1)}, u32[]{:S(2)}, u32[]{:S(2)}) collective-permute-start(f32[129,8,128]{2,1,0:T(8,128)S(1)} %collective-permute-done.4.r2_ref), channel_id=1, source_target_pairs={{0,4},{4,8},{8,12},{16,20},{20,24},{24,28}} | collective-permute-start | bytes 1585160 | tf_op jit(solution)/shard_map/ppermute | solution.py:307
  35.4 13.2 %collective-permute-start.2 = (f32[129,8,128]{2,1,0:T(8,128)S(1)}, f32[129,8,128]{2,1,0:T(8,128)S(1)}, u32[]{:S(2)}, u32[]{:S(2)}) collective-permute-start(f32[129,8,128]{2,1,0:T(8,128)S(1)} %collective-permute-done.1.r2_ref), channel_id=1, source_target_pairs={{0,4},{4,8},{8,12},{16,20},{20,24},{24,28}} | collective-permute-start | bytes 1585160 | tf_op jit(solution)/shard_map/ppermute | solution.py:307
  42.2 2.5 %copy-start.13 = (bf16[8,256,256]{2,1,0:T(8,128)(2,1)}, bf16[8,256,256]{2,1,0:T(8,128)(2,1)S(1)}, u32[]{:S(2)}) copy-start(bf16[8,256,256]{2,1,0:T(8,128)(2,1)S(1)} %get-tuple-element.36.atw_ref) | copy-start | bytes 3145732
  42.2 3.5 %copy-start.10 = (f32[129,8,128]{2,1,0:T(8,128)S(1)}, f32[129,8,128]{2,1,0:T(8,128)}, u32[]{:S(2)}) copy-start(f32[129,8,128]{2,1,0:T(8,128)} %copy-done.9) | copy-start | bytes 1585156
  42.3 3.5 %copy-start.19 = (f32[2048]{0:T(1024)S(1)}, f32[2048]{0:T(1024)}, u32[]{:S(2)}) copy-start(f32[2048]{0:T(1024)} %param.10) | copy-start | bytes 24580
  44.7 1.0 copy-start.14
  48.5 3.7 %copy-start.22 = (bf16[8,128,128]{2,1,0:T(8,128)(2,1)}, bf16[8,128,128]{2,1,0:T(8,128)(2,1)S(1)}, u32[]{:S(2)}) copy-start(bf16[8,128,128]{2,1,0:T(8,128)(2,1)S(1)} %get-tuple-element.41.state_ref) | copy-start | bytes 786436
  48.5 5.1 %copy-start.8 = (f32[256,1024]{1,0:T(8,128)}, f32[256,1024]{1,0:T(8,128)S(1)}, u32[]{:S(2)}) copy-start(f32[256,1024]{1,0:T(8,128)S(1)} %get-tuple-element.38.att_ref) | copy-start | bytes 3145732
  48.5 5.1 %copy-start.6 = (bf16[256,2048]{1,0:T(8,128)(2,1)S(1)}, bf16[256,2048]{1,0:T(8,128)(2,1)}, u32[]{:S(2)}) copy-start(bf16[256,2048]{1,0:T(8,128)(2,1)} %do_ref.7) | copy-start | bytes 3145732
  52.2 4.0 %copy-start.20 = (bf16[8,128,128]{2,1,0:T(8,128)(2,1)}, bf16[8,128,128]{2,1,0:T(8,128)(2,1)S(1)}, u32[]{:S(2)}) copy-start(bf16[8,128,128]{2,1,0:T(8,128)(2,1)S(1)} %get-tuple-element.37.state_ref) | copy-start | bytes 786436
  52.2 13.0 %copy-start.7 = (f32[256,1024]{1,0:T(8,128)}, f32[256,1024]{1,0:T(8,128)S(1)}, u32[]{:S(2)}) copy-start(f32[256,1024]{1,0:T(8,128)S(1)} %get-tuple-element.33.att_ref) | copy-start | bytes 3145732
  52.2 1.4 %collective-permute-start.6 = (f32[256,128]{1,0:T(8,128)S(1)}, f32[256,128]{1,0:T(8,128)S(1)}, u32[]{:S(2)}, u32[]{:S(2)}) collective-permute-start(f32[256,128]{1,0:T(8,128)S(1)} %get-tuple-element.34.mine_ref), channel_id=1, source_target_pairs={{0,1},{1,0},{2,3},{3,2},{4,5},{5,4},{6,7},{7,6},{8,9},{9,8},{10,11... | collective-permute-start | bytes 393224 | tf_op jit(solution)/shard_map/ppermute | solution.py:408
  56.2 11.6 %copy-start.17 = (bf16[256,1024]{1,0:T(8,128)(2,1)}, bf16[256,1024]{1,0:T(8,128)(2,1)S(1)}, u32[]{:S(2)}) copy-start(bf16[256,1024]{1,0:T(8,128)(2,1)S(1)} %get-tuple-element.39.ag_ref) | copy-start | bytes 1572868
  56.2 16.5 %collective-permute-start.10 = (f32[129,8,128]{2,1,0:T(8,128)}, f32[129,8,128]{2,1,0:T(8,128)}, u32[]{:S(2)}, u32[]{:S(2)}) collective-permute-start(f32[129,8,128]{2,1,0:T(8,128)} %get-tuple-element.51.own_ref), channel_id=1, source_target_pairs={{0,2},{2,0},{4,6},{5,1},{6,4},{7,3},{8,10},{9,5},{10,8},{11,7},{12... | collective-permute-start | bytes 1585160 | tf_op jit(solution)/shard_map/ppermute | solution.py:307
  67.8 0.8 copy-start.15
  68.6 12.3 %collective-permute-start.7 = (f32[129,8,128]{2,1,0:T(8,128)}, f32[129,8,128]{2,1,0:T(8,128)S(1)}, u32[]{:S(2)}, u32[]{:S(2)}) collective-permute-start(f32[129,8,128]{2,1,0:T(8,128)} %get-tuple-element.48.own_ref), channel_id=1, source_target_pairs={{0,2},{2,0},{4,6},{5,1},{6,4},{7,3},{8,10},{9,5},{10,8},{11,7},{12... | collective-permute-start | bytes 1585160 | tf_op jit(solution)/shard_map/ppermute | solution.py:307
  73.9 29.4 %copy-start.18 = (bf16[256,1024]{1,0:T(8,128)(2,1)S(1)}, bf16[256,1024]{1,0:T(8,128)(2,1)}, u32[]{:S(2)}) copy-start(bf16[256,1024]{1,0:T(8,128)(2,1)} %copy-done.17) | copy-start | bytes 1572868
  73.9 29.4 %copy-start.23 = (bf16[8,128,128]{2,1,0:T(8,128)(2,1)S(1)}, bf16[8,128,128]{2,1,0:T(8,128)(2,1)}, u32[]{:S(2)}) copy-start(bf16[8,128,128]{2,1,0:T(8,128)(2,1)} %copy-done.22) | copy-start | bytes 786436
  73.9 17.3 %collective-permute-start.11 = (f32[129,8,128]{2,1,0:T(8,128)S(1)}, f32[129,8,128]{2,1,0:T(8,128)S(1)}, u32[]{:S(2)}, u32[]{:S(2)}) collective-permute-start(f32[129,8,128]{2,1,0:T(8,128)S(1)} %join0.3), channel_id=1, source_target_pairs={{3,1},{4,0},{5,3},{6,2},{7,5},{8,4},{9,7},{10,6},{11,9},{12,8},{13... | collective-permute-start | bytes 1585160 | tf_op jit(solution)/shard_map/ppermute | solution.py:307
  82.0 20.6 %collective-permute-start.8 = (f32[129,8,128]{2,1,0:T(8,128)S(1)}, f32[129,8,128]{2,1,0:T(8,128)S(1)}, u32[]{:S(2)}, u32[]{:S(2)}) collective-permute-start(f32[129,8,128]{2,1,0:T(8,128)S(1)} %join1.3), channel_id=1, source_target_pairs={{3,1},{4,0},{5,3},{6,2},{7,5},{8,4},{9,7},{10,6},{11,9},{12,8},{13... | collective-permute-start | bytes 1585160 | tf_op jit(solution)/shard_map/ppermute | solution.py:307
  91.2 22.9 %collective-permute-start.12 = (f32[129,8,128]{2,1,0:T(8,128)S(1)}, f32[129,8,128]{2,1,0:T(8,128)S(1)}, u32[]{:S(2)}, u32[]{:S(2)}) collective-permute-start(f32[129,8,128]{2,1,0:T(8,128)S(1)} %collective-permute-done.11.r2_ref), channel_id=1, source_target_pairs={{6,2},{10,6},{14,10},{22,18},{26,22},{30,26}} | collective-permute-start | bytes 1585160 | tf_op jit(solution)/shard_map/ppermute | solution.py:307
  102.6 15.0 %collective-permute-start.9 = (f32[129,8,128]{2,1,0:T(8,128)S(1)}, f32[129,8,128]{2,1,0:T(8,128)S(1)}, u32[]{:S(2)}, u32[]{:S(2)}) collective-permute-start(f32[129,8,128]{2,1,0:T(8,128)S(1)} %collective-permute-done.8.r2_ref), channel_id=1, source_target_pairs={{6,2},{10,6},{14,10},{22,18},{26,22},{30,26}} | collective-permute-start | bytes 1585160 | tf_op jit(solution)/shard_map/ppermute | solution.py:307
  103.3 5.4 %copy-start.16 = (bf16[256,1024]{1,0:T(8,128)(2,1)S(1)}, bf16[256,1024]{1,0:T(8,128)(2,1)}, u32[]{:S(2)}) copy-start(bf16[256,1024]{1,0:T(8,128)(2,1)} %copy-done.15) | copy-start | bytes 1572868
  103.3 5.4 %copy-start.21 = (bf16[8,128,128]{2,1,0:T(8,128)(2,1)S(1)}, bf16[8,128,128]{2,1,0:T(8,128)(2,1)}, u32[]{:S(2)}) copy-start(bf16[8,128,128]{2,1,0:T(8,128)(2,1)} %copy-done.20) | copy-start | bytes 786436
  108.7 5.5 %copy-start.4 = (bf16[256,2048]{1,0:T(8,128)(2,1)S(1)}, bf16[256,2048]{1,0:T(8,128)(2,1)}, u32[]{:S(2)}) copy-start(bf16[256,2048]{1,0:T(8,128)(2,1)} %v_ref.15) | copy-start | bytes 3145732

commit v2 on v1

--- a/solution.py
+++ b/solution.py
@@ -113,8 +113,9 @@
 
 
 HALVES = 2
-STEPS = 4
-VMEM_LIMIT = 48 * 1024 * 1024
+GROUPS = 1
+QUARTER_STEPS = 1
+VMEM_LIMIT = 32 * 1024 * 1024
 
 
 def nn(a, b):
@@ -137,12 +138,8 @@
     return (doc_ref[0] + 1).astype(F32)
 
 
-def message_slabs(heads):
-    return heads * HEAD_DIM // 8 + 1
-
-
-def put_head(out_ref, head, value):
-    out_ref[pl.ds(head * 16, 16)] = value.reshape(16, 8, HEAD_DIM)
+def put_head(out_ref, j, value):
+    out_ref[pl.ds(j * 16, 16)] = value.reshape(16, 8, HEAD_DIM)
 
 
 def put_tag(out_ref, doc_ref):
@@ -150,36 +147,40 @@
 
 
 def kv_kernel(per, doc_ref, k_ref, v_ref, out_ref):
-    i = pl.program_id(0)
     for j in range(per):
-        put_head(out_ref, i * per + j, tn(k_ref[:, cols(j)], v_ref[:, cols(j)]))
-
-    @pl.when(i == 0)
-    def _():
-        put_tag(out_ref, doc_ref)
+        put_head(out_ref, j, tn(k_ref[:, cols(j)], v_ref[:, cols(j)]))
+    put_tag(out_ref, doc_ref)
 
 
 def lower(n):
     return lax.broadcasted_iota(jnp.int32, (n, n), 0) >= lax.broadcasted_iota(jnp.int32, (n, n), 1)
 
 
-def intra_kernel(per, q_ref, k_ref, v_ref, att_ref, out_ref):
+def lower_t(n):
+    return lax.broadcasted_iota(jnp.int32, (n, n), 0) <= lax.broadcasted_iota(jnp.int32, (n, n), 1)
+
+
+def intra_kernel(per, q_ref, k_ref, v_ref, after_ref, out_ref):
     mask = lower(q_ref.shape[0])
     for j in range(per):
         scores = nt(q_ref[:, cols(j)], k_ref[:, cols(j)])
         att = jnp.where(mask, scores, 0.0).astype(BF)
-        att_ref[j] = att
         out_ref[:, cols(j)] = nn(att, v_ref[:, cols(j)])
 
 
-def gathered(head, doc_ref, flag_ref, r1_ref, r2_ref, r3_ref):
+def gate(doc_ref, flag_ref, r1_ref, r2_ref, r3_ref):
     own = own_tag(doc_ref)
     last = r1_ref.shape[0] - 1
     use3 = flag_ref[0]
     m1 = ((r1_ref[last] == own) & (use3 == 0)).astype(F32)
     m2 = (r2_ref[last] == own).astype(F32)
     m3 = ((r3_ref[last] == own) & (use3 == 1)).astype(F32)
-    at = pl.ds(head * 16, 16)
+    return m1, m2, m3
+
+
+def gathered(j, gates, r1_ref, r2_ref, r3_ref):
+    m1, m2, m3 = gates
+    at = pl.ds(j * 16, 16)
     total = r2_ref[at] * m2 + r1_ref[at] * m1 + r3_ref[at] * m3
     return total.reshape(HEAD_DIM, HEAD_DIM).astype(BF)
 
@@ -198,10 +199,11 @@
         else:
             acc_ref[...] = jnp.zeros_like(acc_ref)
 
+    gates = gate(doc_ref, flag_ref, r1_ref, r2_ref, r3_ref)
     square = acc_ref[0]
     cross = acc_ref[1]
     for j in range(per):
-        state = gathered(i * per + j, doc_ref, flag_ref, r1_ref, r2_ref, r3_ref)
+        state = gathered(j, gates, r1_ref, r2_ref, r3_ref)
         state_ref[j] = state
         att = intra_ref[:, cols(j)] + nn(q_ref[:, cols(j)], state)
         att_ref[:, cols(j)] = att
@@ -229,50 +231,96 @@
     return inverse, coef
 
 
-def grad_kernel(per, width, doc_ref, q_ref, att_ref, do_ref, gain_ref, mine_ref, other_ref, ag_ref, out_ref):
-    i = pl.program_id(0)
+def grad_kernel(per, width, doc_ref, q_ref, att_ref, do_ref, gain_ref, mine_ref, other_ref, *rest):
+    normed_ref, ag_ref, out_ref = rest[-3:]
     inverse, coef = scales(mine_ref, other_ref, width)
     for j in range(per):
+        att = att_ref[:, cols(j)]
         scaled = gain_ref[:, cols(j)] * do_ref[:, cols(j)].astype(F32)
-        ag = (inverse * scaled - att_ref[:, cols(j)] * coef).astype(BF)
+        normed_ref[:, cols(j)] = (att * inverse * gain_ref[:, cols(j)]).astype(BF)
+        ag = (inverse * scaled - att * coef).astype(BF)
         ag_ref[:, cols(j)] = ag
-        put_head(out_ref, i * per + j, tn(q_ref[:, cols(j)], ag))
-
-    @pl.when(i == 0)
-    def _():
-        put_tag(out_ref, doc_ref)
-
-
-def back_kernel(per, width, q_ref, k_ref, v_ref, ag_ref, atw_ref, state_ref, att_ref, gain_ref, mine_ref, other_ref, *rest):
-    normed_ref, qg_ref, kin_ref, vin_ref = rest[-4:]
-    inverse, _ = scales(mine_ref, other_ref, width)
+        put_head(out_ref, j, tn(q_ref[:, cols(j)], ag))
+    put_tag(out_ref, doc_ref)
+
+
+def back_kernel(per, q_ref, k_ref, v_ref, ag_ref, state_ref, *rest):
+    qg_ref, kin_ref, vin_ref = rest[-3:]
     mask = lower(q_ref.shape[0])
+    upper = lower_t(q_ref.shape[0])
     for j in range(per):
         q = q_ref[:, cols(j)]
+        k = k_ref[:, cols(j)]
+        v = v_ref[:, cols(j)]
         ag = ag_ref[:, cols(j)]
-        normed_ref[:, cols(j)] = (att_ref[:, cols(j)] * inverse * gain_ref[:, cols(j)]).astype(BF)
-        gw = jnp.where(mask, nt(ag, v_ref[:, cols(j)]), 0.0).astype(BF)
-        qg_ref[:, cols(j)] = (nn(gw, k_ref[:, cols(j)]) + nt(ag, state_ref[j])).astype(BF)
-        kin_ref[:, cols(j)] = tn(gw, q)
-        vin_ref[:, cols(j)] = tn(atw_ref[j], ag)
+        gw = jnp.where(mask, nt(ag, v), 0.0).astype(BF)
+        qg_ref[:, cols(j)] = (nn(gw, k) + nt(ag, state_ref[j])).astype(BF)
+        gw_t = jnp.where(upper, nt(v, ag), 0.0).astype(BF)
+        kin_ref[:, cols(j)] = nn(gw_t, q)
+        att_t = jnp.where(upper, nt(k, q), 0.0).astype(BF)
+        vin_ref[:, cols(j)] = nn(att_t, ag)
 
 
 def final_kernel(per, doc_ref, flag_ref, k_ref, v_ref, kin_ref, vin_ref, r1_ref, r2_ref, r3_ref, *rest):
     kg_ref, vg_ref = rest[-2:]
-    i = pl.program_id(0)
+    gates = gate(doc_ref, flag_ref, r1_ref, r2_ref, r3_ref)
     for j in range(per):
-        grads = gathered(i * per + j, doc_ref, flag_ref, r1_ref, r2_ref, r3_ref)
+        grads = gathered(j, gates, r1_ref, r2_ref, r3_ref)
         kg_ref[:, cols(j)] = (kin_ref[:, cols(j)] + nt(v_ref[:, cols(j)], grads)).astype(BF)
         vg_ref[:, cols(j)] = (vin_ref[:, cols(j)] + nn(k_ref[:, cols(j)], grads)).astype(BF)
 
 
-def call(kernel, name, in_specs, out_specs, out_shape, scratch=(), aliases=None, flops=0, steps=STEPS):
+def join_kernel(role_ref, own_ref, got_ref, after_ref, out_ref):
+    last = own_ref.shape[0] - 1
+    same = (own_ref[last] == got_ref[last]).astype(F32)
+
+    @pl.when(role_ref[0] == 1)
+    def _():
+        out_ref[...] = got_ref[...] + own_ref[...] * same[None]
+        out_ref[last] = got_ref[last]
+
+    @pl.when(role_ref[0] == 0)
+    def _():
+        out_ref[...] = own_ref[...] + got_ref[...] * same[None]
+        out_ref[last] = own_ref[last]
+
+
+def order_kernel(x_ref, after_ref, out_ref):
+    pass
+
+
+def in_hbm(x):
+    return pltpu.with_memory_space_constraint(x, pltpu.HBM)
+
+
+def ordered(x, after, name):
+    untouched = pl.BlockSpec(memory_space=pl.ANY)
+    return pl.pallas_call(
+        order_kernel,
+        in_specs=[untouched, untouched],
+        out_specs=untouched,
+        out_shape=jax.ShapeDtypeStruct(x.shape, x.dtype),
+        input_output_aliases={0: 0},
+        name=name,
+    )(x, in_hbm(after))
+
+
+class Far(jax.ShapeDtypeStruct):
+    pass
+
+
+def call(kernel, name, in_specs, out_specs, out_shape, scratch=(), aliases=None, flops=0, steps=GROUPS):
+    many = isinstance(out_shape, list)
+    shapes = [
+        pltpu.HBM(x.shape, x.dtype) if isinstance(x, Far) else x
+        for x in (out_shape if many else [out_shape])
+    ]
     return pl.pallas_call(
         kernel,
         grid=(steps,),
         in_specs=in_specs,
         out_specs=out_specs,
-        out_shape=out_shape,
+        out_shape=shapes if many else shapes[0],
         scratch_shapes=list(scratch),
         input_output_aliases=aliases or {},
         name=name,
@@ -307,21 +355,6 @@
     return lax.ppermute(x, ("seq", "head"), pairs)
 
 
-def join_kernel(role_ref, own_ref, got_ref, out_ref):
-    last = own_ref.shape[0] - 1
-    same = (own_ref[last] == got_ref[last]).astype(F32)
-
-    @pl.when(role_ref[0] == 1)
-    def _():
-        out_ref[...] = got_ref[...] + own_ref[...] * same[None]
-        out_ref[last] = got_ref[last]
-
-    @pl.when(role_ref[0] == 0)
-    def _():
-        out_ref[...] = own_ref[...] + got_ref[...] * same[None]
-        out_ref[last] = own_ref[last]
-
-
 def block_body(queries, key_vectors, value_vectors, output_grad, norm_gain, block_docs):
     tokens, width = queries.shape
     heads = width // HEAD_DIM
@@ -329,115 +362,144 @@
     head = lax.axis_size("head")
     full = width * head
     hh = heads // HALVES
-    steps = STEPS
-    per = hh // steps
-    pw = per * HEAD_DIM
     hw = hh * HEAD_DIM
     gain = norm_gain.reshape(1, width)
-    seq_at = lax.axis_index("seq")
-    core_at = lax.axis_index("head")
-    even_core = core_at % 2 == 0
-    odd_block = seq_at % 2 == 1
+    odd_block = lax.axis_index("seq") % 2 == 1
+    even_core = lax.axis_index("head") % 2 == 0
     smem = pl.BlockSpec(memory_space=pltpu.SMEM)
-    slabs = message_slabs(hh)
-    message = jax.ShapeDtypeStruct((slabs, 8, HEAD_DIM), F32)
-    whole = pl.BlockSpec((slabs, 8, HEAD_DIM), lambda i: (0, 0, 0))
+    untouched = pl.BlockSpec(memory_space=pl.ANY)
+    per = hh // GROUPS
+    pw = per * HEAD_DIM
+    run = per * 16 + 1
+    message = jax.ShapeDtypeStruct((GROUPS * run, 8, HEAD_DIM), F32)
+    slabs = pl.BlockSpec((run, 8, HEAD_DIM), lambda i: (i, 0, 0))
     sums_spec = pl.BlockSpec((tokens, HEAD_DIM), lambda i: (0, 0))
     local = pl.BlockSpec((tokens, pw), lambda i: (0, i))
-    square = pl.BlockSpec((per, tokens, tokens), lambda i: (i, 0, 0))
     states = pl.BlockSpec((per, HEAD_DIM, HEAD_DIM), lambda i: (i, 0, 0))
     acc_shape = jax.ShapeDtypeStruct((2, tokens, HEAD_DIM), F32)
     acc_spec = pl.BlockSpec((2, tokens, HEAD_DIM), lambda i: (0, 0, 0))
-    untouched = pl.BlockSpec(memory_space=pl.ANY)
-    wide = jax.ShapeDtypeStruct((tokens, width), BF)
+    wide = Far((tokens, width), BF)
     half32 = jax.ShapeDtypeStruct((tokens, hw), F32)
+    far32 = Far((tokens, hw), F32)
 
     def part(n):
-        return pl.BlockSpec((tokens, pw), lambda i: (0, i + n * steps))
+        return pl.BlockSpec((tokens, pw), lambda i: (0, i + n * GROUPS))
 
     def gain_part(n):
-        return pl.BlockSpec((1, pw), lambda i: (0, i + n * steps))
+        return pl.BlockSpec((1, pw), lambda i: (0, i + n * GROUPS))
 
     mm = 2 * tokens * HEAD_DIM * HEAD_DIM * hh
 
-    def exchange(messages, sign):
-        first, second, third = routes(seq, head, sign)
-        low_block = odd_block if sign < 0 else ~odd_block
-        got1 = [send(m, first) for m in messages]
-        use3 = (even_core & low_block).astype(jnp.int32).reshape(1)
-        on = [
-            call(join_kernel, f"join{n}", [smem, whole, whole], whole, message, steps=1)(use3, m, g)
-            for n, (m, g) in enumerate(zip(messages, got1))
-        ]
-        got2 = [send(m, second) for m in on]
-        got3 = [send(g, third) for g in got2]
-        return use3, list(zip(got1, got2, got3))
-
+    def role(sign):
+        return (even_core & (odd_block if sign < 0 else ~odd_block)).astype(jnp.int32).reshape(1)
+
+    def join(n, flag, own, got, after):
+        return call(join_kernel, f"join{n}", [smem, slabs, slabs, untouched], slabs, message)(
+            flag, own, got, after
+        )
+
+    def intra(n, after):
+        return call(
+            functools.partial(intra_kernel, per), f"intra{n}",
+            [part(n)] * 3 + [untouched],
+            local, far32, flops=4 * mm,
+        )(queries, key_vectors, value_vectors, after)
+
+    up = routes(seq, head, 1)
+    flag = role(1)
     kv = [
-        call(functools.partial(kv_kernel, per), f"kv{n}", [smem, part(n), part(n)], whole, message, flops=mm)(
-            block_docs, key_vectors, value_vectors
+        call(functools.partial(kv_kernel, per), f"kv{n}", [smem, part(n), part(n)], slabs, message, flops=mm)(
+            block_docs, in_hbm(key_vectors), in_hbm(value_vectors)
         )
         for n in range(HALVES)
     ]
-    use3, got = exchange(kv, 1)
-    intra = [
-        call(
-            functools.partial(intra_kernel, per), f"intra{n}",
-            [part(n)] * 3, [square, local],
-            [jax.ShapeDtypeStruct((hh, tokens, tokens), BF), half32], flops=4 * mm,
-        )(queries, key_vectors, value_vectors)
-        for n in range(HALVES)
-    ]
+    got1 = [send(m, up[0]) for m in kv]
+    intra0 = intra(0, kv[1])
+    on0 = join(0, flag, kv[0], got1[0], in_hbm(intra0))
+    got2a = send(on0, up[1])
+    on1 = join(1, flag, kv[1], got1[1], on0)
+    got2b = send(on1, up[1])
+    intra1 = intra(1, on1)
+    got2a = ordered(got2a, intra1, "order0")
+    got3a = send(got2a, up[2])
+    got3b = send(got2b, up[2])
+    got = [(got1[0], got2a, got3a), (got1[1], got2b, got3b)]
+    inner = [intra0, intra1]
     attended, state, sums = [], [], None
     for n in range(HALVES):
         last = n == HALVES - 1
         extra = [acc_spec] if n else []
         att, st, sums = call(
             functools.partial(attend_kernel, per, last), f"attend{n}",
-            [smem, smem, part(n), local, part(n), gain_part(n), whole, whole, whole] + extra,
+            [smem, smem, part(n), local, part(n), gain_part(n), slabs, slabs, slabs] + extra,
             [local, states, sums_spec if last else acc_spec],
             [
                 half32,
-                jax.ShapeDtypeStruct((hh, HEAD_DIM, HEAD_DIM), BF),
+                Far((hh, HEAD_DIM, HEAD_DIM), BF),
                 jax.ShapeDtypeStruct((tokens, HEAD_DIM), F32) if last else acc_shape,
             ],
             scratch=[pltpu.VMEM((2, tokens, HEAD_DIM), F32)], flops=mm,
-        )(block_docs, use3, queries, intra[n][1], output_grad, gain, *got[n], *([sums] if n else []))
+        )(block_docs, flag, queries, in_hbm(inner[n]), in_hbm(output_grad), gain, *got[n], *([sums] if n else []))
         attended.append(att)
         state.append(st)
     other = lax.ppermute(sums, "head", [(c, c ^ 1) for c in range(head)])
-    ag, bg = [], []
+    ag, bg, normed = [], [], None
     for n in range(HALVES):
-        a, b = call(
+        extra = [normed] if n else []
+        normed, a, b = call(
             functools.partial(grad_kernel, per, full), f"grad{n}",
-            [smem, part(n), local, part(n), gain_part(n), sums_spec, sums_spec],
-            [local, whole], [jax.ShapeDtypeStruct((tokens, hw), BF), message], flops=mm,
-        )(block_docs, queries, attended[n], output_grad, gain, sums, other)
+            [smem, part(n), local, part(n), gain_part(n), sums_spec, sums_spec] + [untouched] * n,
+            [part(n), local, slabs], [wide, Far((tokens, hw), BF), message], aliases={7: 0} if n else None, flops=mm,
+        )(block_docs, queries, attended[n], output_grad, gain, sums, other, *(in_hbm(x) for x in extra))
         ag.append(a)
         bg.append(b)
-    use3b, gotb = exchange(bg, -1)
-    kin, vin, normed, query_grad = [], [], None, None
-    for n in range(HALVES):
-        extra = [normed, query_grad] if n else []
-        base = 10
-        normed, query_grad, ki, vi = call(
-            functools.partial(back_kernel, per, full), f"back{n}",
-            [part(n)] * 3 + [local, square, states, local, gain_part(n), sums_spec, sums_spec] + [untouched] * len(extra),
-            [part(n), part(n), local, local], [wide, wide, half32, half32],
-            aliases={base: 0, base + 1: 1} if n else None, flops=7 * mm,
-        )(queries, key_vectors, value_vectors, ag[n], intra[n][0], state[n], attended[n], gain, sums, other, *extra)
-        kin.append(ki)
-        vin.append(vi)
+
+    qper = hh // 2 // QUARTER_STEPS
+    qw = qper * HEAD_DIM
+
+    def back(c, before, after):
+        n, sub = divmod(c, 2)
+        wide_spec = pl.BlockSpec((tokens, qw), lambda i: (0, i + c * QUARTER_STEPS))
+        half_spec = pl.BlockSpec((tokens, qw), lambda i: (0, i + sub * QUARTER_STEPS))
+        state_spec = pl.BlockSpec((qper, HEAD_DIM, HEAD_DIM), lambda i: (i + sub * QUARTER_STEPS, 0, 0))
+        base = 6
+        carried = list(before[: 3 if sub else 1]) if before else []
+        return call(
+            functools.partial(back_kernel, qper), f"back{c}",
+            [wide_spec] * 3 + [half_spec, state_spec, untouched] + [untouched] * len(carried),
+            [wide_spec, half_spec, half_spec], [wide, far32, far32],
+            aliases={base + i: i for i in range(len(carried))}, flops=8 * mm // 2, steps=QUARTER_STEPS,
+        )(queries, key_vectors, value_vectors, in_hbm(ag[n]),
+          in_hbm(state[n]), after, *(in_hbm(x) for x in carried))
+
+    down = routes(seq, head, -1)
+    flag = role(-1)
+    got1 = [send(m, down[0]) for m in bg]
+    back0 = back(0, None, bg[1])
+    on0 = join(0, flag, bg[0], got1[0], in_hbm(back0[0]))
+    got2a = send(on0, down[1])
+    back1 = back(1, back0, on0)
+    on1 = join(1, flag, bg[1], got1[1], in_hbm(back1[0]))
+    got2b = send(on1, down[1])
+    back2 = back(2, back1, on1)
+    got2a = ordered(got2a, back2[0], "order1")
+    got3a = send(got2a, down[2])
+    back3 = back(3, back2, got2a)
+    got2b = ordered(got2b, back3[0], "order2")
+    got3b = send(got2b, down[2])
+    got = [(got1[0], got2a, got3a), (got1[1], got2b, got3b)]
+    query_grad = back3[0]
+    inside = [back1[1:3], back3[1:3]]
     key_grad, value_grad = None, None
     for n in range(HALVES):
         extra = [key_grad, value_grad] if n else []
         base = 9
         key_grad, value_grad = call(
             functools.partial(final_kernel, per), f"final{n}",
-            [smem, smem, part(n), part(n), local, local, whole, whole, whole] + [untouched] * len(extra),
+            [smem, smem, part(n), part(n), local, local, slabs, slabs, slabs] + [untouched] * len(extra),
             [part(n), part(n)], [wide, wide],
             aliases={base: 0, base + 1: 1} if n else None, flops=2 * mm,
-        )(block_docs, use3b, key_vectors, value_vectors, kin[n], vin[n], *gotb[n], *extra)
+        )(block_docs, flag, key_vectors, value_vectors, *(in_hbm(x) for x in inside[n]), *got[n], *(in_hbm(x) for x in extra))
     return normed, query_grad, key_grad, value_grad
 
 
@@ -445,8 +507,7 @@
     rows = P(("groups", "seq"), "head")
     in_specs = (rows, rows, rows, rows, P("head"), P(("groups", "seq")))
     out_specs = (rows, rows, rows, rows)
-    seq = mesh.shape["seq"]
-    short = seq == 8 and mesh.shape["head"] == 2
+    short = mesh.shape["seq"] == 8 and mesh.shape["head"] == 2
 
     def body(queries, key_vectors, value_vectors, output_grad, norm_gain, block_docs):
         one = block_docs.shape[0] == 1

time: 121 us -> 102 us (0.84)
  waiting for transfers between devices: 34.1 us -> 21.4 us
  local copies, waits for them, and re-layouts: 6.17 us -> 0.02 us
  Pallas kernels: 39.7 us -> 44.2 us
  starting transfers between devices: 38.2 us -> 33.8 us
    ppermute x12, waiting for transfers between devices: 32.8 us -> 20.1 us  [send(): return lax.ppermute(x, ('seq', 'head'), pairs)]
    unnamed x48 -> x10, local copies, waits for them, and re-layouts: 6.17 us -> 0.02 us
    pallas_call x8 -> x13, Pallas kernels: 19.3 us -> 23.9 us  [the longest x4 13.4 us: back(): call(functools.partial(back_kernel, qper), f'back{c}', [wide_spec] * 3 +...]
    ppermute x12, starting transfers between devices: 38.1 us -> 33.8 us  [send(): return lax.ppermute(x, ('seq', 'head'), pairs)]
    pallas_call x2, Pallas kernels: 3.03 us -> 4.79 us  [block_body(): call(functools.partial(kv_kernel, per), f'kv{n}', [smem, part(n), part(n)...]
    pallas_call x2, Pallas kernels: 5.21 us -> 3.51 us  [block_body(): call(functools.partial(grad_kernel, per, full), f'grad{n}', [smem, part(n...]
  transfers between devices with their start and end apart: 13 -> 13, of which waited for: 9 -> 9; matrix products, arithmetic and copies ran while one was open for 0% -> 0% of each run, Pallas kernels for 25% -> 34%
where the time goes in v2:
time: 102 us; the launch traced here: 101 us
  Pallas kernels  44.2 us (43%)
  starting transfers between devices  33.8 us (33%)
  waiting for transfers between devices  21.4 us (21%)
  between operations  1.45 us (1%)
    ppermute x12, starting transfers between devices, send(): return lax.ppermute(x, ('seq', 'head'), pairs)  33.8 us
    ppermute x12, waiting for transfers between devices, send(): return lax.ppermute(x, ('seq', 'head'), pairs)  20.1 us
    pallas_call x4, Pallas kernels, back(): call(functools.partial(back_kernel, qper), f'back{c}', [wide_spec] * 3 +...  13.4 us
    pallas_call x2, Pallas kernels, block_body(): call(functools.partial(final_kernel, per), f'final{n}', [smem, smem, part...  6.76 us
    pallas_call x4, Pallas kernels, join(): call(join_kernel, f'join{n}', [smem, slabs, slabs, untouched], slabs, mes...  6.62 us
    pallas_call x2, Pallas kernels, block_body(): call(functools.partial(attend_kernel, per, last), f'attend{n}', [smem, sm...  5.19 us
    pallas_call x2, Pallas kernels, block_body(): call(functools.partial(kv_kernel, per), f'kv{n}', [smem, part(n), part(n)...  4.79 us
    pallas_call x2, Pallas kernels, intra(): call(functools.partial(intra_kernel, per), f'intra{n}', [part(n)] * 3 + [...  3.9 us
  transfers between devices with their start and end apart: 13, of which 9 were waited for; matrix products, arithmetic and copies ran while one was open for 0% of the time, Pallas kernels for 34%

profile of v2, /device:TPU:0, one launch (start us, length us, event | category | flops | bytes accessed | tf_op | source)
XLA Modules:
  0.0 100.9 jit_solution(17680260626745885424)
XLA Ops:
  1.3 0.0 copy-start.2
  1.3 2.4 %kv0.1.own_ref = f32[129,8,128]{2,1,0:T(8,128)} custom-call(s32[1]{0:T(128)S(6)} %copy.36.doc_ref, bf16[256,2048]{1,0:T(8,128)(2,1)} %k_ref.19, bf16[256,2048]{1,0:T(8,128)(2,1)} %v_ref.19), custom_call_target="tpu_custom_call" | custom-call | flops 67108864 | bytes 4194304 | tf_op jit(solution)/shard_map/kv0/pallas_call | solution.py:411
  3.7 5.0 %collective-permute-start.1 = (f32[129,8,128]{2,1,0:T(8,128)}, f32[129,8,128]{2,1,0:T(8,128)}, u32[]{:S(2)}, u32[]{:S(2)}) collective-permute-start(f32[129,8,128]{2,1,0:T(8,128)} %kv0.1.own_ref), channel_id=1, source_target_pairs={{0,2},{1,5},{2,0},{3,7},{4,6},{5,9},{6,4},{7,11},{8,10},{9,13},{10... | collective-permute-start | bytes 1585160 | tf_op jit(solution)/shard_map/ppermute | solution.py:355
  8.7 2.4 %kv1.1.after_ref.own_ref = f32[129,8,128]{2,1,0:T(8,128)} custom-call(s32[1]{0:T(128)S(6)} %copy.36.doc_ref, bf16[256,2048]{1,0:T(8,128)(2,1)} %k_ref.19, bf16[256,2048]{1,0:T(8,128)(2,1)} %v_ref.19), custom_call_target="tpu_custom_call" | custom-call | flops 67108864 | bytes 4194304 | tf_op jit(solution)/shard_map/kv1/pallas_call | solution.py:411
  11.1 1.9 %collective-permute-start = (f32[129,8,128]{2,1,0:T(8,128)}, f32[129,8,128]{2,1,0:T(8,128)}, u32[]{:S(2)}, u32[]{:S(2)}) collective-permute-start(f32[129,8,128]{2,1,0:T(8,128)} %kv1.1.after_ref.own_ref), channel_id=1, source_target_pairs={{0,2},{1,5},{2,0},{3,7},{4,6},{5,9},{6,4},{7,11},{8,10},{9,13},{10... | collective-permute-start | bytes 1585160 | tf_op jit(solution)/shard_map/ppermute | solution.py:355
  13.0 0.0 copy-done.2
  13.0 0.0 copy-done
  13.0 0.0 copy-done.1
  13.0 1.9 %intra0.1.after_ref.intra_ref = f32[256,1024]{1,0:T(8,128)} custom-call(bf16[256,2048]{1,0:T(8,128)(2,1)S(1)} %copy-done.2, bf16[256,2048]{1,0:T(8,128)(2,1)S(1)} %copy-done, bf16[256,2048]{1,0:T(8,128)(2,1)S(1)} %copy-done.1, f32[129,8,128]{2,1,0:T(8,128)} %kv1.1.after_ref.own_ref), custom_call_target="tpu_custom_call" | custom-call | flops 268435456 | bytes 4194304 | tf_op jit(solution)/shard_map/intra0/pallas_call | solution.py:402
  15.0 1.2 %collective-permute-done.1.got_ref.r1_ref = f32[129,8,128]{2,1,0:T(8,128)} collective-permute-done((f32[129,8,128]{2,1,0:T(8,128)}, f32[129,8,128]{2,1,0:T(8,128)}, u32[]{:S(2)}, u32[]{:S(2)}) %collective-permute-start.1) | collective-permute-done | bytes 528416 | tf_op jit(solution)/shard_map/ppermute | solution.py:355
  16.2 1.3 %join0.2.after_ref = f32[129,8,128]{2,1,0:T(8,128)S(1)} custom-call(s32[1]{0:T(128)} %bitcast.role_ref.flag_ref, f32[129,8,128]{2,1,0:T(8,128)} %kv0.1.own_ref, f32[129,8,128]{2,1,0:T(8,128)} %collective-permute-done.1.got_ref.r1_ref, f32[256,1024]{1,0:T(8,128)} %intra0.1.after_ref.intra_ref), custom_call_target="tpu_custom_call" | custom-call | bytes 4194304 | tf_op jit(solution)/shard_map/join0/pallas_call | solution.py:397
  17.5 4.8 %collective-permute-start.4 = (f32[129,8,128]{2,1,0:T(8,128)S(1)}, f32[129,8,128]{2,1,0:T(8,128)}, u32[]{:S(2)}, u32[]{:S(2)}) collective-permute-start(f32[129,8,128]{2,1,0:T(8,128)S(1)} %join0.2.after_ref), channel_id=1, source_target_pairs={{0,4},{1,3},{2,6},{3,5},{4,8},{5,7},{6,10},{7,9},{8,12},{9,11},{10... | collective-permute-start | bytes 1585160 | tf_op jit(solution)/shard_map/ppermute | solution.py:355
  22.3 0.2 collective-permute-done.got_ref.r1_ref
  22.5 2.1 %join1.2.after_ref = f32[129,8,128]{2,1,0:T(8,128)} custom-call(s32[1]{0:T(128)} %bitcast.role_ref.flag_ref, f32[129,8,128]{2,1,0:T(8,128)} %kv1.1.after_ref.own_ref, f32[129,8,128]{2,1,0:T(8,128)} %collective-permute-done.got_ref.r1_ref, f32[129,8,128]{2,1,0:T(8,128)S(1)} %join0.2.after_ref), custom_call_target="tpu_custom_call" | custom-call | bytes 4194304 | tf_op jit(solution)/shard_map/join1/pallas_call | solution.py:397
  24.5 4.3 %collective-permute-start.2 = (f32[129,8,128]{2,1,0:T(8,128)}, f32[129,8,128]{2,1,0:T(8,128)}, u32[]{:S(2)}, u32[]{:S(2)}) collective-permute-start(f32[129,8,128]{2,1,0:T(8,128)} %join1.2.after_ref), channel_id=1, source_target_pairs={{0,4},{1,3},{2,6},{3,5},{4,8},{5,7},{6,10},{7,9},{8,12},{9,11},{10... | collective-permute-start | bytes 1585160 | tf_op jit(solution)/shard_map/ppermute | solution.py:355
  28.8 1.9 %intra1.1.after_ref.intra_ref = f32[256,1024]{1,0:T(8,128)} custom-call(bf16[256,2048]{1,0:T(8,128)(2,1)S(1)} %copy-done.2, bf16[256,2048]{1,0:T(8,128)(2,1)S(1)} %copy-done, bf16[256,2048]{1,0:T(8,128)(2,1)S(1)} %copy-done.1, f32[129,8,128]{2,1,0:T(8,128)} %join1.2.after_ref), custom_call_target="tpu_custom_call" | custom-call | flops 268435456 | bytes 4194304 | tf_op jit(solution)/shard_map/intra1/pallas_call | solution.py:402
  30.8 0.0 collective-permute-done.4.x_ref
  30.8 2.8 %collective-permute-start.5 = (f32[129,8,128]{2,1,0:T(8,128)}, f32[129,8,128]{2,1,0:T(8,128)S(1)}, u32[]{:S(2)}, u32[]{:S(2)}) collective-permute-start(f32[129,8,128]{2,1,0:T(8,128)} %order0.1.r2_ref), channel_id=1, source_target_pairs={{0,4},{4,8},{8,12},{16,20},{20,24},{24,28}} | collective-permute-start | bytes 1585160 | tf_op jit(solution)/shard_map/ppermute | solution.py:355
  33.6 1.4 %collective-permute-done.2.r2_ref = f32[129,8,128]{2,1,0:T(8,128)} collective-permute-done((f32[129,8,128]{2,1,0:T(8,128)}, f32[129,8,128]{2,1,0:T(8,128)}, u32[]{:S(2)}, u32[]{:S(2)}) %collective-permute-start.2) | collective-permute-done | bytes 528416 | tf_op jit(solution)/shard_map/ppermute | solution.py:355
  35.1 4.4 %collective-permute-start.3 = (f32[129,8,128]{2,1,0:T(8,128)}, f32[129,8,128]{2,1,0:T(8,128)S(1)}, u32[]{:S(2)}, u32[]{:S(2)}) collective-permute-start(f32[129,8,128]{2,1,0:T(8,128)} %collective-permute-done.2.r2_ref), channel_id=1, source_target_pairs={{0,4},{4,8},{8,12},{16,20},{20,24},{24,28}} | collective-permute-start | bytes 1585160 | tf_op jit(solution)/shard_map/ppermute | solution.py:355
  39.5 1.2 %collective-permute-done.5.r3_ref = f32[129,8,128]{2,1,0:T(8,128)S(1)} collective-permute-done((f32[129,8,128]{2,1,0:T(8,128)}, f32[129,8,128]{2,1,0:T(8,128)S(1)}, u32[]{:S(2)}, u32[]{:S(2)}) %collective-permute-start.5) | collective-permute-done | bytes 528416 | tf_op jit(solution)/shard_map/ppermute | solution.py:355
  40.7 2.5 %attend0.1 = (f32[256,1024]{1,0:T(8,128)S(1)}, bf16[8,128,128]{2,1,0:T(8,128)(2,1)}, f32[2,256,128]{2,1,0:T(8,128)S(1)}) custom-call(s32[1]{0:T(128)S(6)} %copy.36.doc_ref, s32[1]{0:T(128)} %bitcast.role_ref.flag_ref, bf16[256,2048]{1,0:T(8,128)(2,1)S(1)} %copy-done.2, f32[256,1024]{1,0:T(8,128)} %intra0.1.after_ref.intra_ref, bf16[256,2048]{1,0:T(8,128)(2,1)} %do_ref.7, ...), custom_call_target="tpu_custom_call" | custom-call | flops 67108864 | bytes 4194304 | tf_op jit(solution)/shard_map/attend0/pallas_call | solution.py:432
  43.3 3.2 %collective-permute-done.3.r3_ref = f32[129,8,128]{2,1,0:T(8,128)S(1)} collective-permute-done((f32[129,8,128]{2,1,0:T(8,128)}, f32[129,8,128]{2,1,0:T(8,128)S(1)}, u32[]{:S(2)}, u32[]{:S(2)}) %collective-permute-start.3) | collective-permute-done | bytes 528416 | tf_op jit(solution)/shard_map/ppermute | solution.py:355
  46.5 2.6 %attend1.1 = (f32[256,1024]{1,0:T(8,128)S(1)}, bf16[8,128,128]{2,1,0:T(8,128)(2,1)}, f32[256,128]{1,0:T(8,128)S(1)}) custom-call(s32[1]{0:T(128)S(6)} %copy.36.doc_ref, s32[1]{0:T(128)} %bitcast.role_ref.flag_ref, bf16[256,2048]{1,0:T(8,128)(2,1)S(1)} %copy-done.2, f32[256,1024]{1,0:T(8,128)} %intra1.1.after_ref.intra_ref, bf16[256,2048]{1,0:T(8,128)(2,1)} %do_ref.7, ...), custom_call_target="tpu_custom_call" | custom-call | flops 67108864 | bytes 4194304 | tf_op jit(solution)/shard_map/attend1/pallas_call | solution.py:432
  49.1 0.0 collective-permute-start.6
  49.1 1.3 %collective-permute-done.6.other_ref = f32[256,128]{1,0:T(8,128)S(1)} collective-permute-done((f32[256,128]{1,0:T(8,128)S(1)}, f32[256,128]{1,0:T(8,128)S(1)}, u32[]{:S(2)}, u32[]{:S(2)}) %collective-permute-start.6) | collective-permute-done | bytes 131104 | tf_op jit(solution)/shard_map/ppermute | solution.py:445
  50.5 1.8 %grad0.1 = (bf16[256,2048]{1,0:T(8,128)(2,1)}, bf16[256,1024]{1,0:T(8,128)(2,1)}, f32[129,8,128]{2,1,0:T(8,128)}) custom-call(s32[1]{0:T(128)S(6)} %copy.36.doc_ref, bf16[256,2048]{1,0:T(8,128)(2,1)S(1)} %copy-done.2, f32[256,1024]{1,0:T(8,128)S(1)} %get-tuple-element.35.att_ref, bf16[256,2048]{1,0:T(8,128)(2,1)S(1)} %copy-done.3, f32[1,2048]{1,0:T(1,128)S(1)} %bitcast.5, ...), custom_call_target="tpu_custom_call" | custom-call | flops 67108864 | bytes 4194304 | tf_op jit(solution)/shard_map/grad0/pallas_call | solution.py:449
  52.2 3.6 %collective-permute-start.7 = (f32[129,8,128]{2,1,0:T(8,128)}, f32[129,8,128]{2,1,0:T(8,128)}, u32[]{:S(2)}, u32[]{:S(2)}) collective-permute-start(f32[129,8,128]{2,1,0:T(8,128)} %get-tuple-element.40.own_ref), channel_id=1, source_target_pairs={{0,2},{2,0},{4,6},{5,1},{6,4},{7,3},{8,10},{9,5},{10,8},{11,7},{12... | collective-permute-start | bytes 1585160 | tf_op jit(solution)/shard_map/ppermute | solution.py:355
  55.9 1.8 %grad1.1 = (bf16[256,2048]{1,0:T(8,128)(2,1)}, bf16[256,1024]{1,0:T(8,128)(2,1)}, f32[129,8,128]{2,1,0:T(8,128)}) custom-call(s32[1]{0:T(128)S(6)} %copy.36.doc_ref, bf16[256,2048]{1,0:T(8,128)(2,1)S(1)} %copy-done.2, f32[256,1024]{1,0:T(8,128)S(1)} %get-tuple-element.33.att_ref, bf16[256,2048]{1,0:T(8,128)(2,1)S(1)} %copy-done.3, ...), custom_call_target="tpu_custom_call", output_to_operand_aliasing={{0}: (7, {})} | custom-call | flops 67108864 | bytes 4194304 | tf_op jit(solution)/shard_map/grad1/pallas_call | solution.py:449
  57.6 2.2 %collective-permute-start.9 = (f32[129,8,128]{2,1,0:T(8,128)}, f32[129,8,128]{2,1,0:T(8,128)}, u32[]{:S(2)}, u32[]{:S(2)}) collective-permute-start(f32[129,8,128]{2,1,0:T(8,128)} %get-tuple-element.43.rest_0_.own_ref), channel_id=1, source_target_pairs={{0,2},{2,0},{4,6},{5,1},{6,4},{7,3},{8,10},{9,5},{10,8},{11,7},{12... | collective-permute-start | bytes 1585160 | tf_op jit(solution)/shard_map/ppermute | solution.py:355
  59.8 3.3 %back0.1 = (bf16[256,2048]{1,0:T(8,128)(2,1)}, f32[256,1024]{1,0:T(8,128)}, f32[256,1024]{1,0:T(8,128)}) custom-call(bf16[256,2048]{1,0:T(8,128)(2,1)S(1)} %copy-done.2, bf16[256,2048]{1,0:T(8,128)(2,1)S(1)} %copy-done, bf16[256,2048]{1,0:T(8,128)(2,1)S(1)} %copy-done.1, bf16[256,1024]{1,0:T(8,128)(2,1)} %get-tuple-element.41.ag_ref, ...), custom_call_target="tpu_custom_call" | custom-call | flops 268435456 | bytes 4194304 | tf_op jit(solution)/shard_map/back0/pallas_call | solution.py:467
  63.2 0.5 collective-permute-done.7.got_ref.r1_ref
  63.7 1.3 %join0.3.rest_0_ = f32[129,8,128]{2,1,0:T(8,128)S(1)} custom-call(s32[1]{0:T(128)} %bitcast.2.role_ref.flag_ref, f32[129,8,128]{2,1,0:T(8,128)} %get-tuple-element.40.own_ref, f32[129,8,128]{2,1,0:T(8,128)} %collective-permute-done.7.got_ref.r1_ref, bf16[256,2048]{1,0:T(8,128)(2,1)} %get-tuple-element.44.after_ref.rest_1_), custom_call_target="tpu_custom_call" | custom-call | bytes 4194304 | tf_op jit(solution)/shard_map/join0/pallas_call | solution.py:397
  64.9 1.3 %collective-permute-start.8 = (f32[129,8,128]{2,1,0:T(8,128)S(1)}, f32[129,8,128]{2,1,0:T(8,128)}, u32[]{:S(2)}, u32[]{:S(2)}) collective-permute-start(f32[129,8,128]{2,1,0:T(8,128)S(1)} %join0.3.rest_0_), channel_id=1, source_target_pairs={{3,1},{4,0},{5,3},{6,2},{7,5},{8,4},{9,7},{10,6},{11,9},{12,8},{13... | collective-permute-start | bytes 1585160 | tf_op jit(solution)/shard_map/ppermute | solution.py:355
  66.2 3.4 %back1.1 = (bf16[256,2048]{1,0:T(8,128)(2,1)}, f32[256,1024]{1,0:T(8,128)}, f32[256,1024]{1,0:T(8,128)}) custom-call(bf16[256,2048]{1,0:T(8,128)(2,1)S(1)} %copy-done.2, bf16[256,2048]{1,0:T(8,128)(2,1)S(1)} %copy-done, bf16[256,2048]{1,0:T(8,128)(2,1)S(1)} %copy-done.1, ...), custom_call_target="tpu_custom_call", output_to_operand_aliasing={{0}: (6, {}), {1}: (7, {}), {2}: (8, {})} | custom-call | flops 268435456 | bytes 4194304 | tf_op jit(solution)/shard_map/back1/pallas_call | solution.py:467
  69.6 0.0 collective-permute-done.9.got_ref.r1_ref
  69.6 2.1 %join1.3.rest_0_ = f32[129,8,128]{2,1,0:T(8,128)} custom-call(s32[1]{0:T(128)} %bitcast.2.role_ref.flag_ref, f32[129,8,128]{2,1,0:T(8,128)} %get-tuple-element.43.rest_0_.own_ref, f32[129,8,128]{2,1,0:T(8,128)} %collective-permute-done.9.got_ref.r1_ref, bf16[256,2048]{1,0:T(8,128)(2,1)} %get-tuple-element.47.after_ref.rest_1_), custom_call_target="tpu_custom_call" | custom-call | bytes 4194304 | tf_op jit(solution)/shard_map/join1/pallas_call | solution.py:397
  71.7 1.3 %collective-permute-start.10 = (f32[129,8,128]{2,1,0:T(8,128)}, f32[129,8,128]{2,1,0:T(8,128)}, u32[]{:S(2)}, u32[]{:S(2)}) collective-permute-start(f32[129,8,128]{2,1,0:T(8,128)} %join1.3.rest_0_), channel_id=1, source_target_pairs={{3,1},{4,0},{5,3},{6,2},{7,5},{8,4},{9,7},{10,6},{11,9},{12,8},{13... | collective-permute-start | bytes 1585160 | tf_op jit(solution)/shard_map/ppermute | solution.py:355
  72.9 3.3 %back2.1 = (bf16[256,2048]{1,0:T(8,128)(2,1)}, f32[256,1024]{1,0:T(8,128)}, f32[256,1024]{1,0:T(8,128)}) custom-call(bf16[256,2048]{1,0:T(8,128)(2,1)S(1)} %copy-done.2, bf16[256,2048]{1,0:T(8,128)(2,1)S(1)} %copy-done, bf16[256,2048]{1,0:T(8,128)(2,1)S(1)} %copy-done.1, ...), custom_call_target="tpu_custom_call", output_to_operand_aliasing={{0}: (6, {})} | custom-call | flops 268435456 | bytes 4194304 | tf_op jit(solution)/shard_map/back2/pallas_call | solution.py:467
  76.3 5.9 %collective-permute-done.8.x_ref = f32[129,8,128]{2,1,0:T(8,128)} collective-permute-done((f32[129,8,128]{2,1,0:T(8,128)S(1)}, f32[129,8,128]{2,1,0:T(8,128)}, u32[]{:S(2)}, u32[]{:S(2)}) %collective-permute-start.8) | collective-permute-done | bytes 528416 | tf_op jit(solution)/shard_map/ppermute | solution.py:355
  82.2 1.5 %collective-permute-start.12 = (f32[129,8,128]{2,1,0:T(8,128)}, f32[129,8,128]{2,1,0:T(8,128)}, u32[]{:S(2)}, u32[]{:S(2)}) collective-permute-start(f32[129,8,128]{2,1,0:T(8,128)} %order1.1.rest_0_.r2_ref), channel_id=1, source_target_pairs={{6,2},{10,6},{14,10},{22,18},{26,22},{30,26}} | collective-permute-start | bytes 1585160 | tf_op jit(solution)/shard_map/ppermute | solution.py:355
  83.6 3.4 %back3.1 = (bf16[256,2048]{1,0:T(8,128)(2,1)}, f32[256,1024]{1,0:T(8,128)}, f32[256,1024]{1,0:T(8,128)}) custom-call(bf16[256,2048]{1,0:T(8,128)(2,1)S(1)} %copy-done.2, bf16[256,2048]{1,0:T(8,128)(2,1)S(1)} %copy-done, bf16[256,2048]{1,0:T(8,128)(2,1)S(1)} %copy-done.1, ...), custom_call_target="tpu_custom_call", output_to_operand_aliasing={{0}: (6, {}), {1}: (7, {}), {2}: (8, {})} | custom-call | flops 268435456 | bytes 4194304 | tf_op jit(solution)/shard_map/back3/pallas_call | solution.py:467
  87.0 6.4 %collective-permute-done.10.x_ref = f32[129,8,128]{2,1,0:T(8,128)} collective-permute-done((f32[129,8,128]{2,1,0:T(8,128)}, f32[129,8,128]{2,1,0:T(8,128)}, u32[]{:S(2)}, u32[]{:S(2)}) %collective-permute-start.10) | collective-permute-done | bytes 528416 | tf_op jit(solution)/shard_map/ppermute | solution.py:355
  93.4 0.7 collective-permute-start.11
  94.1 0.0 collective-permute-done.12.r3_ref
  94.1 3.5 %final0.1 = (bf16[256,2048]{1,0:T(8,128)(2,1)}, bf16[256,2048]{1,0:T(8,128)(2,1)}) custom-call(s32[1]{0:T(128)S(6)} %copy.36.doc_ref, s32[1]{0:T(128)} %bitcast.2.role_ref.flag_ref, bf16[256,2048]{1,0:T(8,128)(2,1)S(1)} %copy-done, bf16[256,2048]{1,0:T(8,128)(2,1)S(1)} %copy-done.1, f32[256,1024]{1,0:T(8,128)} %get-tuple-element.54.kin_ref, ...), custom_call_target="tpu_custom_call" | custom-call | flops 134217728 | bytes 4194304 | tf_op jit(solution)/shard_map/final0/pallas_call | solution.py:497
  97.6 0.0 collective-permute-done.11.r3_ref
  97.6 3.3 %final1.1 = (bf16[256,2048]{1,0:T(8,128)(2,1)}, bf16[256,2048]{1,0:T(8,128)(2,1)}) custom-call(s32[1]{0:T(128)S(6)} %copy.36.doc_ref, s32[1]{0:T(128)} %bitcast.2.role_ref.flag_ref, bf16[256,2048]{1,0:T(8,128)(2,1)S(1)} %copy-done, bf16[256,2048]{1,0:T(8,128)(2,1)S(1)} %copy-done.1, ...), custom_call_target="tpu_custom_call", output_to_operand_aliasing={{0}: (9, {}), {1}: (10, {})} | custom-call | flops 134217728 | bytes 4194304 | tf_op jit(solution)/shard_map/final1/pallas_call | solution.py:497
  (9 shorter events, 0.0 us)
Async XLA Ops:
  1.3 11.7 %copy-start.2 = (bf16[256,2048]{1,0:T(8,128)(2,1)S(1)}, bf16[256,2048]{1,0:T(8,128)(2,1)}, u32[]{:S(2)}) copy-start(bf16[256,2048]{1,0:T(8,128)(2,1)} %q_ref.19) | copy-start | bytes 3145732
  3.7 9.3 %copy-start = (bf16[256,2048]{1,0:T(8,128)(2,1)S(1)}, bf16[256,2048]{1,0:T(8,128)(2,1)}, u32[]{:S(2)}) copy-start(bf16[256,2048]{1,0:T(8,128)(2,1)} %k_ref.19) | copy-start | bytes 3145732
  3.7 9.3 %copy-start.1 = (bf16[256,2048]{1,0:T(8,128)(2,1)S(1)}, bf16[256,2048]{1,0:T(8,128)(2,1)}, u32[]{:S(2)}) copy-start(bf16[256,2048]{1,0:T(8,128)(2,1)} %v_ref.19) | copy-start | bytes 3145732
  3.7 12.5 %collective-permute-start.1 = (f32[129,8,128]{2,1,0:T(8,128)}, f32[129,8,128]{2,1,0:T(8,128)}, u32[]{:S(2)}, u32[]{:S(2)}) collective-permute-start(f32[129,8,128]{2,1,0:T(8,128)} %kv0.1.own_ref), channel_id=1, source_target_pairs={{0,2},{1,5},{2,0},{3,7},{4,6},{5,9},{6,4},{7,11},{8,10},{9,13},{10... | collective-permute-start | bytes 1585160 | tf_op jit(solution)/shard_map/ppermute | solution.py:355
  11.1 11.4 %collective-permute-start = (f32[129,8,128]{2,1,0:T(8,128)}, f32[129,8,128]{2,1,0:T(8,128)}, u32[]{:S(2)}, u32[]{:S(2)}) collective-permute-start(f32[129,8,128]{2,1,0:T(8,128)} %kv1.1.after_ref.own_ref), channel_id=1, source_target_pairs={{0,2},{1,5},{2,0},{3,7},{4,6},{5,9},{6,4},{7,11},{8,10},{9,13},{10... | collective-permute-start | bytes 1585160 | tf_op jit(solution)/shard_map/ppermute | solution.py:355
  17.5 13.3 %collective-permute-start.4 = (f32[129,8,128]{2,1,0:T(8,128)S(1)}, f32[129,8,128]{2,1,0:T(8,128)}, u32[]{:S(2)}, u32[]{:S(2)}) collective-permute-start(f32[129,8,128]{2,1,0:T(8,128)S(1)} %join0.2.after_ref), channel_id=1, source_target_pairs={{0,4},{1,3},{2,6},{3,5},{4,8},{5,7},{6,10},{7,9},{8,12},{9,11},{10... | collective-permute-start | bytes 1585160 | tf_op jit(solution)/shard_map/ppermute | solution.py:355
  24.5 10.5 %collective-permute-start.2 = (f32[129,8,128]{2,1,0:T(8,128)}, f32[129,8,128]{2,1,0:T(8,128)}, u32[]{:S(2)}, u32[]{:S(2)}) collective-permute-start(f32[129,8,128]{2,1,0:T(8,128)} %join1.2.after_ref), channel_id=1, source_target_pairs={{0,4},{1,3},{2,6},{3,5},{4,8},{5,7},{6,10},{7,9},{8,12},{9,11},{10... | collective-permute-start | bytes 1585160 | tf_op jit(solution)/shard_map/ppermute | solution.py:355
  30.8 9.9 %copy-start.4 = (f32[2048]{0:T(1024)S(1)}, f32[2048]{0:T(1024)}, u32[]{:S(2)}) copy-start(f32[2048]{0:T(1024)} %param.10) | copy-start | bytes 24580
  30.8 9.9 %collective-permute-start.5 = (f32[129,8,128]{2,1,0:T(8,128)}, f32[129,8,128]{2,1,0:T(8,128)S(1)}, u32[]{:S(2)}, u32[]{:S(2)}) collective-permute-start(f32[129,8,128]{2,1,0:T(8,128)} %order0.1.r2_ref), channel_id=1, source_target_pairs={{0,4},{4,8},{8,12},{16,20},{20,24},{24,28}} | collective-permute-start | bytes 1585160 | tf_op jit(solution)/shard_map/ppermute | solution.py:355
  35.1 11.4 %collective-permute-start.3 = (f32[129,8,128]{2,1,0:T(8,128)}, f32[129,8,128]{2,1,0:T(8,128)S(1)}, u32[]{:S(2)}, u32[]{:S(2)}) collective-permute-start(f32[129,8,128]{2,1,0:T(8,128)} %collective-permute-done.2.r2_ref), channel_id=1, source_target_pairs={{0,4},{4,8},{8,12},{16,20},{20,24},{24,28}} | collective-permute-start | bytes 1585160 | tf_op jit(solution)/shard_map/ppermute | solution.py:355
  46.5 4.0 %copy-start.3 = (bf16[256,2048]{1,0:T(8,128)(2,1)S(1)}, bf16[256,2048]{1,0:T(8,128)(2,1)}, u32[]{:S(2)}) copy-start(bf16[256,2048]{1,0:T(8,128)(2,1)} %do_ref.7) | copy-start | bytes 3145732
  49.1 1.3 %collective-permute-start.6 = (f32[256,128]{1,0:T(8,128)S(1)}, f32[256,128]{1,0:T(8,128)S(1)}, u32[]{:S(2)}, u32[]{:S(2)}) collective-permute-start(f32[256,128]{1,0:T(8,128)S(1)} %get-tuple-element.34.mine_ref), channel_id=1, source_target_pairs={{0,1},{1,0},{2,3},{3,2},{4,5},{5,4},{6,7},{7,6},{8,9},{9,8},{10,11... | collective-permute-start | bytes 393224 | tf_op jit(solution)/shard_map/ppermute | solution.py:445
  52.2 11.4 %collective-permute-start.7 = (f32[129,8,128]{2,1,0:T(8,128)}, f32[129,8,128]{2,1,0:T(8,128)}, u32[]{:S(2)}, u32[]{:S(2)}) collective-permute-start(f32[129,8,128]{2,1,0:T(8,128)} %get-tuple-element.40.own_ref), channel_id=1, source_target_pairs={{0,2},{2,0},{4,6},{5,1},{6,4},{7,3},{8,10},{9,5},{10,8},{11,7},{12... | collective-permute-start | bytes 1585160 | tf_op jit(solution)/shard_map/ppermute | solution.py:355
  57.6 12.0 %collective-permute-start.9 = (f32[129,8,128]{2,1,0:T(8,128)}, f32[129,8,128]{2,1,0:T(8,128)}, u32[]{:S(2)}, u32[]{:S(2)}) collective-permute-start(f32[129,8,128]{2,1,0:T(8,128)} %get-tuple-element.43.rest_0_.own_ref), channel_id=1, source_target_pairs={{0,2},{2,0},{4,6},{5,1},{6,4},{7,3},{8,10},{9,5},{10,8},{11,7},{12... | collective-permute-start | bytes 1585160 | tf_op jit(solution)/shard_map/ppermute | solution.py:355
  64.9 17.2 %collective-permute-start.8 = (f32[129,8,128]{2,1,0:T(8,128)S(1)}, f32[129,8,128]{2,1,0:T(8,128)}, u32[]{:S(2)}, u32[]{:S(2)}) collective-permute-start(f32[129,8,128]{2,1,0:T(8,128)S(1)} %join0.3.rest_0_), channel_id=1, source_target_pairs={{3,1},{4,0},{5,3},{6,2},{7,5},{8,4},{9,7},{10,6},{11,9},{12,8},{13... | collective-permute-start | bytes 1585160 | tf_op jit(solution)/shard_map/ppermute | solution.py:355
  71.7 21.7 %collective-permute-start.10 = (f32[129,8,128]{2,1,0:T(8,128)}, f32[129,8,128]{2,1,0:T(8,128)}, u32[]{:S(2)}, u32[]{:S(2)}) collective-permute-start(f32[129,8,128]{2,1,0:T(8,128)} %join1.3.rest_0_), channel_id=1, source_target_pairs={{3,1},{4,0},{5,3},{6,2},{7,5},{8,4},{9,7},{10,6},{11,9},{12,8},{13... | collective-permute-start | bytes 1585160 | tf_op jit(solution)/shard_map/ppermute | solution.py:355
  82.2 11.9 %collective-permute-start.12 = (f32[129,8,128]{2,1,0:T(8,128)}, f32[129,8,128]{2,1,0:T(8,128)}, u32[]{:S(2)}, u32[]{:S(2)}) collective-permute-start(f32[129,8,128]{2,1,0:T(8,128)} %order1.1.rest_0_.r2_ref), channel_id=1, source_target_pairs={{6,2},{10,6},{14,10},{22,18},{26,22},{30,26}} | collective-permute-start | bytes 1585160 | tf_op jit(solution)/shard_map/ppermute | solution.py:355
  93.4 4.2 %collective-permute-start.11 = (f32[129,8,128]{2,1,0:T(8,128)}, f32[129,8,128]{2,1,0:T(8,128)S(1)}, u32[]{:S(2)}, u32[]{:S(2)}) collective-permute-start(f32[129,8,128]{2,1,0:T(8,128)} %order2.1.r2_ref), channel_id=1, source_target_pairs={{6,2},{10,6},{14,10},{22,18},{26,22},{30,26}} | collective-permute-start | bytes 1585160 | tf_op jit(solution)/shard_map/ppermute | solution.py:355

commit v3 on v2

v3 whole, which is shorter than its diff:
```python
import functools

import jax
import jax.numpy as jnp
from jax import lax
from jax.experimental import pallas as pl
from jax.experimental.pallas import tpu as pltpu
from jax.sharding import PartitionSpec as P

HEAD_DIM = 128
norm_eps = 1e-06
BF = jnp.bfloat16
F32 = jnp.float32


def spread_prefix(element, weights):
    seq_count = lax.axis_size("seq")
    flat_state = element.reshape(seq_count, -1, element.shape[-1])
    mixed = jnp.einsum(
        "ds,skc->dkc",
        weights,
        lax.all_to_all(flat_state, "seq", split_axis=0, concat_axis=0, tiled=True),
        precision=lax.Precision.HIGHEST,
    )
    returned = lax.all_to_all(mixed, "seq", split_axis=0, concat_axis=0, tiled=True)
    return returned.reshape(element.shape)


def general_body(queries, key_vectors, value_vectors, output_grad, norm_gain, block_docs):
    tokens, local_width = queries.shape
    heads_here = local_width // HEAD_DIM
    nblocks = block_docs.shape[0]
    block_len = tokens // nblocks
    shape_four = (nblocks, block_len, heads_here, HEAD_DIM)
    query_blk = queries.reshape(shape_four)
    key_blk = key_vectors.reshape(shape_four)
    value_blk = value_vectors.reshape(shape_four)
    tok_pos = lax.iota(jnp.int32, block_len)
    causal = (tok_pos[:, None] >= tok_pos[None, :])[None, None]
    scores = jnp.einsum("bthd,bshd->bhts", query_blk, key_blk, preferred_element_type=F32)
    att_weights = jnp.where(causal, scores, 0.0).astype(BF)
    intra_out = jnp.einsum("bhts,bshe->bthe", att_weights, value_blk, preferred_element_type=F32)
    block_kv = jnp.einsum("bshd,bshe->bhde", key_blk, value_blk, preferred_element_type=F32)
    position = lax.iota(jnp.int32, nblocks)
    same_doc = block_docs[:, None] == block_docs[None, :]
    earlier_mask = (same_doc & (position[None, :] < position[:, None])).astype(F32)
    later_mask = (same_doc & (position[None, :] > position[:, None])).astype(F32)
    local_in = jnp.einsum("kj,jhde->khde", earlier_mask, block_kv, precision=lax.Precision.HIGHEST)
    tail_weight = (block_docs == block_docs[-1]).astype(F32)
    tail_state = jnp.einsum("j,jhde->hde", tail_weight, block_kv, precision=lax.Precision.HIGHEST)
    seq_count = lax.axis_size("seq")
    all_docs = lax.all_gather(block_docs, "seq", axis=0, tiled=True).reshape(seq_count, nblocks)
    first_all = all_docs[:, 0]
    last_all = all_docs[:, -1]
    source_pos = lax.iota(jnp.int32, seq_count)
    forward_weights = (
        (source_pos[None, :] < source_pos[:, None]) & (last_all[None, :] == first_all[:, None])
    ).astype(F32)
    backward_weights = (
        (source_pos[None, :] > source_pos[:, None]) & (first_all[None, :] == last_all[:, None])
    ).astype(F32)
    carry_state = spread_prefix(tail_state, forward_weights)
    carry_use = block_docs == block_docs[0]
    states_in = (
        local_in + jnp.where(carry_use[:, None, None, None], carry_state[None], 0.0)
    ).astype(BF)
    inter_out = jnp.einsum("bthd,bhde->bthe", query_blk, states_in, preferred_element_type=F32)
    attended = (intra_out + inter_out).reshape(tokens, local_width)
    scaled_grad = norm_gain[None, :] * output_grad.astype(F32)
    square_sum, cross_sum = lax.psum(
        (jnp.sum(attended * attended, axis=1), jnp.sum(attended * scaled_grad, axis=1)), "head"
    )
    full_width = local_width * lax.axis_size("head")
    inverse_rms = lax.rsqrt(square_sum / full_width + norm_eps)
    normed = (attended * inverse_rms[:, None] * norm_gain[None, :]).astype(BF)
    attended_grad = (
        inverse_rms[:, None] * scaled_grad
        - attended * (inverse_rms**3 * cross_sum / full_width)[:, None]
    )
    grad_blk = attended_grad.astype(BF).reshape(shape_four)
    score_grad = jnp.einsum("bthe,bshe->bhts", grad_blk, value_blk, preferred_element_type=F32)
    grad_weights = jnp.where(causal, score_grad, 0.0).astype(BF)
    query_part = jnp.einsum("bhts,bshd->bthd", grad_weights, key_blk, preferred_element_type=F32)
    query_part = query_part + jnp.einsum(
        "bthe,bhde->bthd", grad_blk, states_in, preferred_element_type=F32
    )
    key_intra = jnp.einsum("bhts,bthd->bshd", grad_weights, query_blk, preferred_element_type=F32)
    value_intra = jnp.einsum("bhts,bthe->bshe", att_weights, grad_blk, preferred_element_type=F32)
    block_grad = jnp.einsum("bthd,bthe->bhde", query_blk, grad_blk, preferred_element_type=F32)
    grad_local = jnp.einsum(
        "kj,jhde->khde", later_mask, block_grad, precision=lax.Precision.HIGHEST
    )
    head_weight = (block_docs == block_docs[0]).astype(F32)
    head_state = jnp.einsum("j,jhde->hde", head_weight, block_grad, precision=lax.Precision.HIGHEST)
    grad_state = spread_prefix(head_state, backward_weights)
    grad_use = block_docs == block_docs[-1]
    grads_in = (
        grad_local + jnp.where(grad_use[:, None, None, None], grad_state[None], 0.0)
    ).astype(BF)
    key_part = key_intra + jnp.einsum(
        "bshe,bhde->bshd", value_blk, grads_in, preferred_element_type=F32
    )
    value_part = value_intra + jnp.einsum(
        "bshd,bhde->bshe", key_blk, grads_in, preferred_element_type=F32
    )
    flat_shape = (tokens, local_width)
    return (
        normed,
        query_part.reshape(flat_shape).astype(BF),
        key_part.reshape(flat_shape).astype(BF),
        value_part.reshape(flat_shape).astype(BF),
    )


HALVES = 2
CHUNKS = 4
VMEM_LIMIT = 16 * 1024 * 1024


def nn(a, b):
    return lax.dot_general(a, b, (((1,), (0,)), ((), ())), preferred_element_type=F32)


def nt(a, b):
    return lax.dot_general(a, b, (((1,), (1,)), ((), ())), preferred_element_type=F32)


def tn(a, b):
    return lax.dot_general(a, b, (((0,), (0,)), ((), ())), preferred_element_type=F32)


def cols(j):
    return slice(j * HEAD_DIM, (j + 1) * HEAD_DIM)


def own_tag(doc_ref):
    return (doc_ref[0] + 1).astype(F32)


def put_head(out_ref, j, value):
    out_ref[j * 16 : (j + 1) * 16] = value.reshape(16, 8, HEAD_DIM)


def put_tag(out_ref, doc_ref):
    out_ref[out_ref.shape[0] - 1] = jnp.full((8, HEAD_DIM), own_tag(doc_ref), F32)


def kv_kernel(n, hh, doc_ref, k_hbm, v_hbm, k_ref, v_ref, out_ref, k_sems, v_sems):
    step = hh // CHUNKS
    width = step * HEAD_DIM

    def copies(c):
        there = slice((n * CHUNKS + c) * width, (n * CHUNKS + c + 1) * width)
        here = slice(c * width, (c + 1) * width)
        return (
            pltpu.make_async_copy(k_hbm.at[:, there], k_ref.at[:, here], k_sems.at[c]),
            pltpu.make_async_copy(v_hbm.at[:, there], v_ref.at[:, here], v_sems.at[c]),
        )

    for c in range(CHUNKS):
        for copy in copies(c):
            copy.start()
    put_tag(out_ref, doc_ref)
    for c in range(CHUNKS):
        for copy in copies(c):
            copy.wait()
        for j in range(c * step, (c + 1) * step):
            put_head(out_ref, j, tn(k_ref[:, cols(j)], v_ref[:, cols(j)]))


def lower(n):
    return lax.broadcasted_iota(jnp.int32, (n, n), 0) >= lax.broadcasted_iota(jnp.int32, (n, n), 1)


def upper(n):
    return lax.broadcasted_iota(jnp.int32, (n, n), 0) <= lax.broadcasted_iota(jnp.int32, (n, n), 1)


def intra_kernel(n, hh, q_ref, k_ref, v_ref, after_ref, out_ref):
    mask = lower(q_ref.shape[0])
    for j in range(hh):
        scores = nt(q_ref[:, cols(n * hh + j)], k_ref[:, cols(j)])
        att = jnp.where(mask, scores, 0.0).astype(BF)
        out_ref[:, cols(j)] = nn(att, v_ref[:, cols(j)])


def near_block(parity):
    even_core = 1 - (lax.axis_index("head") & 1)
    odd_block = lax.axis_index("seq") & 1
    return even_core * (odd_block if parity else 1 - odd_block)


def gate(parity, doc_ref, r1_ref, r2_ref, r3_ref):
    own = own_tag(doc_ref)
    last = r1_ref.shape[0] - 1
    use3 = near_block(parity).astype(F32)
    m1 = (r1_ref[last] == own).astype(F32) * (1.0 - use3)
    m2 = (r2_ref[last] == own).astype(F32)
    m3 = (r3_ref[last] == own).astype(F32) * use3
    return m1, m2, m3


def gathered(j, gates, r1_ref, r2_ref, r3_ref):
    m1, m2, m3 = gates
    at = slice(j * 16, (j + 1) * 16)
    total = r2_ref[at] * m2 + r1_ref[at] * m1 + r3_ref[at] * m3
    return total.reshape(HEAD_DIM, HEAD_DIM).astype(BF)


def attend_kernel(n, hh, doc_ref, q_ref, intra_ref, do_ref, gain_ref, r1_ref, r2_ref, r3_ref, *rest):
    last_half = n == HALVES - 1
    if n:
        sum_in_ref, att_ref, state_ref, sum_ref = rest
        square = sum_in_ref[0]
        cross = sum_in_ref[1]
    else:
        att_ref, state_ref, sum_ref = rest
        square = jnp.zeros((q_ref.shape[0], HEAD_DIM), F32)
        cross = square
    gates = gate(0, doc_ref, r1_ref, r2_ref, r3_ref)
    for j in range(hh):
        at = cols(n * hh + j)
        state = gathered(j, gates, r1_ref, r2_ref, r3_ref)
        state_ref[j] = state
        att = intra_ref[:, cols(j)] + nn(q_ref[:, at], state)
        att_ref[:, cols(j)] = att
        square = square + att * att
        cross = cross + att * (gain_ref[:, at] * do_ref[:, at].astype(F32))
    if last_half:
        lane = lax.broadcasted_iota(jnp.int32, square.shape, 1)
        sq = jnp.sum(square, axis=1, keepdims=True)
        cr = jnp.sum(cross, axis=1, keepdims=True)
        sum_ref[...] = jnp.where(lane == 0, sq, jnp.where(lane == 1, cr, 0.0))
    else:
        sum_ref[0] = square
        sum_ref[1] = cross


def grad_kernel(n, hh, width, doc_ref, q_ref, att_ref, do_ref, gain_ref, mine_ref, other_ref, *rest):
    normed_ref, ag_ref, out_ref = rest[-3:]
    total = mine_ref[...] + other_ref[...]
    inverse = lax.rsqrt(total[:, 0:1] / width + norm_eps)
    coef = inverse * inverse * inverse * total[:, 1:2] / width
    for j in range(hh):
        at = cols(n * hh + j)
        att = att_ref[:, cols(j)]
        scaled = gain_ref[:, at] * do_ref[:, at].astype(F32)
        normed_ref[:, at] = (att * inverse * gain_ref[:, at]).astype(BF)
        ag = (inverse * scaled - att * coef).astype(BF)
        ag_ref[:, cols(j)] = ag
        put_head(out_ref, j, tn(q_ref[:, at], ag))
    put_tag(out_ref, doc_ref)


def back_kernel(c, hh, q_ref, k_ref, v_ref, ag_ref, state_ref, *rest):
    qg_ref, qg_sems, normed_sem = rest[-3:]
    if c == 0:
        normed_ref = rest[1]
        normed_hbm, qg_hbm, kin_ref, vin_ref = rest[-7:-3]
        normed_copy = pltpu.make_async_copy(normed_ref, normed_hbm, normed_sem)
        normed_copy.start()
    else:
        qg_hbm, kin_ref, vin_ref = rest[-6:-3]
    mask = lower(q_ref.shape[0])
    mask_t = upper(q_ref.shape[0])
    count = hh // 2
    copies = []
    for i in range(count):
        at = cols(c * count + i)
        j = (c % 2) * count + i
        q = q_ref[:, at]
        k = k_ref[:, cols(j)]
        v = v_ref[:, cols(j)]
        ag = ag_ref[:, cols(j)]
        gw = jnp.where(mask, nt(ag, v), 0.0).astype(BF)
        qg_ref[:, cols(i)] = (nn(gw, k) + nt(ag, state_ref[j])).astype(BF)
        copies.append(pltpu.make_async_copy(qg_ref.at[:, cols(i)], qg_hbm.at[:, at], qg_sems.at[i]))
        copies[-1].start()
        gw_t = jnp.where(mask_t, nt(v, ag), 0.0).astype(BF)
        kin_ref[:, cols(i)] = nn(gw_t, q)
        att_t = jnp.where(mask_t, nt(k, q), 0.0).astype(BF)
        vin_ref[:, cols(i)] = nn(att_t, ag)
    for copy in copies:
        copy.wait()
    if c == 0:
        normed_copy.wait()


def final_kernel(n, hh, doc_ref, k_ref, v_ref, kin0, kin1, vin0, vin1, r1_ref, r2_ref, r3_ref, *rest):
    kg_hbm, vg_hbm, kg_ref, vg_ref, k_sems, v_sems = rest[-6:]
    gates = gate(1, doc_ref, r1_ref, r2_ref, r3_ref)
    count = hh // 2
    step = hh // CHUNKS
    width = step * HEAD_DIM

    def copies(c):
        there = slice((n * CHUNKS + c) * width, (n * CHUNKS + c + 1) * width)
        here = slice(c * width, (c + 1) * width)
        return (
            pltpu.make_async_copy(kg_ref.at[:, here], kg_hbm.at[:, there], k_sems.at[c]),
            pltpu.make_async_copy(vg_ref.at[:, here], vg_hbm.at[:, there], v_sems.at[c]),
        )

    for c in range(CHUNKS):
        for j in range(c * step, (c + 1) * step):
            kin_ref, vin_ref = (kin0, vin0) if j < count else (kin1, vin1)
            within = cols(j % count)
            grads = gathered(j, gates, r1_ref, r2_ref, r3_ref)
            kg_ref[:, cols(j)] = (kin_ref[:, within] + nt(v_ref[:, cols(j)], grads)).astype(BF)
            vg_ref[:, cols(j)] = (vin_ref[:, within] + nn(k_ref[:, cols(j)], grads)).astype(BF)
        for copy in copies(c):
            copy.start()
    for c in range(CHUNKS):
        for copy in copies(c):
            copy.wait()


def join_kernel(parity, own_ref, got_ref, after_ref, out_ref):
    role = near_block(parity)
    last = own_ref.shape[0] - 1
    same = (own_ref[last] == got_ref[last]).astype(F32)

    @pl.when(role == 1)
    def _():
        out_ref[...] = got_ref[...] + own_ref[...] * same[None]
        out_ref[last] = got_ref[last]

    @pl.when(role == 0)
    def _():
        out_ref[...] = own_ref[...] + got_ref[...] * same[None]
        out_ref[last] = own_ref[last]


def order_kernel(x_ref, after_ref, out_ref):
    pass


VMEM, SMEM, HBM = pltpu.VMEM, pltpu.SMEM, pltpu.HBM


def call(kernel, name, ins, outs, scratch=(), aliases=None, flops=0):
    def spec(memory):
        return pl.BlockSpec(memory_space=pl.ANY if memory is HBM else memory)

    out_shape = [memory(shape, dtype) for memory, shape, dtype in outs]
    out_specs = [spec(memory) for memory, _, _ in outs]
    one = len(outs) == 1
    args = [x if m is SMEM else pltpu.with_memory_space_constraint(x, m) for m, x in ins]
    return pl.pallas_call(
        kernel,
        in_specs=[spec(m) for m, _ in ins],
        out_specs=out_specs[0] if one else out_specs,
        out_shape=out_shape[0] if one else out_shape,
        scratch_shapes=list(scratch),
        input_output_aliases=aliases or {},
        name=name,
        cost_estimate=pl.CostEstimate(flops=flops, transcendentals=0, bytes_accessed=4 << 20),
        compiler_params=pltpu.CompilerParams(vmem_limit_bytes=VMEM_LIMIT),
    )(*args)


def pairs_of(seq, head, rule):
    out = []
    for s in range(seq):
        for h in range(head):
            to = rule(s, h)
            if to is not None and 0 <= to < seq:
                out.append((s * head + h, to * head + h))
    return out


def routes(seq, head, sign):
    first = pairs_of(seq, head, lambda s, h: s ^ 1 if h % 2 == 0 else s + 2 * sign)
    second = pairs_of(seq, head, lambda s, h: s + 2 * sign if h % 2 == 0 else s + sign)
    parity = 0 if sign > 0 else 1
    third = pairs_of(
        seq, head, lambda s, h: s + 2 * sign if h % 2 == 0 and s % 2 == parity else None
    )
    return first, second, third


def send(x, pairs):
    return lax.ppermute(x, ("seq", "head"), pairs)


def block_body(queries, key_vectors, value_vectors, output_grad, norm_gain, block_docs):
    tokens, width = queries.shape
    heads = width // HEAD_DIM
    seq = lax.axis_size("seq")
    head = lax.axis_size("head")
    full = width * head
    hh = heads // HALVES
    hw = hh * HEAD_DIM
    gain = norm_gain.reshape(1, width)
    message = (VMEM, (hh * 16 + 1, 8, HEAD_DIM), F32)
    wide = (VMEM, (tokens, width), BF)
    half16 = (VMEM, (tokens, hw), BF)
    half32 = (VMEM, (tokens, hw), F32)
    quarter32 = (VMEM, (tokens, hw // 2), F32)
    sums_shape = (VMEM, (tokens, HEAD_DIM), F32)
    state_shape = (VMEM, (hh, HEAD_DIM, HEAD_DIM), BF)
    mm = 2 * tokens * HEAD_DIM * HEAD_DIM * hh
    sems = [pltpu.SemaphoreType.DMA((CHUNKS,))] * 2
    docs = (SMEM, block_docs)

    def near(*arrays):
        return [(VMEM, x) for x in arrays]

    def join(n, parity, own, got, after):
        return call(functools.partial(join_kernel, parity), f"join{n}", near(own, got, after), [message])

    def ordered(x, after, name):
        return call(order_kernel, name, near(x, after), [(VMEM, x.shape, x.dtype)], aliases={0: 0})

    def intra(n, after):
        return call(
            functools.partial(intra_kernel, n, hh), f"intra{n}",
            near(queries, keys[n], values[n], after), [half32], flops=4 * mm,
        )

    up = routes(seq, head, 1)
    keys, values, kv = zip(*(
        call(
            functools.partial(kv_kernel, n, hh), f"kv{n}",
            [docs, (HBM, key_vectors), (HBM, value_vectors)], [half16, half16, message],
            scratch=sems, flops=mm,
        )
        for n in range(HALVES)
    ))
    got1 = [send(m, up[0]) for m in kv]
    intra0 = intra(0, kv[1])
    on0 = join(0, 0, kv[0], got1[0], intra0)
    got2a = send(on0, up[1])
    on1 = join(1, 0, kv[1], got1[1], on0)
    got2b = send(on1, up[1])
    intra1 = intra(1, on1)
    got2a = ordered(got2a, intra1, "order0")
    got3a = send(got2a, up[2])
    got3b = send(got2b, up[2])
    got = [(got1[0], got2a, got3a), (got1[1], got2b, got3b)]
    inner = [intra0, intra1]
    attended, state, sums = [], [], None
    for n in range(HALVES):
        last = n == HALVES - 1
        att, st, sums = call(
            functools.partial(attend_kernel, n, hh), f"attend{n}",
            [docs] + near(queries, inner[n], output_grad, gain, *got[n], *([sums] if n else [])),
            [half32, state_shape, sums_shape if last else (VMEM, (2, tokens, HEAD_DIM), F32)],
            flops=mm,
        )
        attended.append(att)
        state.append(st)
    other = lax.ppermute(sums, "head", [(c, c ^ 1) for c in range(head)])
    ag, bg, normed = [], [], None
    for n in range(HALVES):
        normed, a, b = call(
            functools.partial(grad_kernel, n, hh, full), f"grad{n}",
            [docs] + near(queries, attended[n], output_grad, gain, sums, other, *([normed] if n else [])),
            [wide, half16, message], aliases={7: 0} if n else None, flops=mm,
        )
        ag.append(a)
        bg.append(b)

    def back(c, query_grad, after):
        n = c // 2
        ins = near(queries, keys[n], values[n], ag[n], state[n], after)
        ins += [(HBM, query_grad)] if c else near(normed)
        outs = [(HBM, (tokens, width), BF), quarter32, quarter32]
        return call(
            functools.partial(back_kernel, c, hh), f"back{c}", ins, outs if c else [outs[0]] + outs,
            scratch=[
                pltpu.VMEM((tokens, hw // 2), BF), pltpu.SemaphoreType.DMA((hh // 2,)), pltpu.SemaphoreType.DMA(())
            ],
            aliases={6: 0} if c else None, flops=7 * mm // 2,
        )

    down = routes(seq, head, -1)
    got1 = [send(m, down[0]) for m in bg]
    normed, query_grad, kin0, vin0 = back(0, None, bg[1])
    on0 = join(0, 1, bg[0], got1[0], kin0)
    got2a = send(on0, down[1])
    query_grad, kin1, vin1 = back(1, query_grad, on0)
    on1 = join(1, 1, bg[1], got1[1], kin1)
    got2b = send(on1, down[1])
    query_grad, kin2, vin2 = back(2, query_grad, on1)
    got2a = ordered(got2a, kin2, "order1")
    got3a = send(got2a, down[2])
    query_grad, kin3, vin3 = back(3, query_grad, got2a)
    got2b = ordered(got2b, kin3, "order2")
    got3b = send(got2b, down[2])
    got = [(got1[0], got2a, got3a), (got1[1], got2b, got3b)]
    inside = [(kin0, kin1, vin0, vin1), (kin2, kin3, vin2, vin3)]
    grads = None
    for n in range(HALVES):
        grads = call(
            functools.partial(final_kernel, n, hh), f"final{n}",
            [docs] + near(keys[n], values[n], *inside[n], *got[n]) + ([(HBM, x) for x in grads] if n else []),
            [(HBM, (tokens, width), BF)] * 2,
            scratch=[pltpu.VMEM((tokens, hw), BF)] * 2 + sems,
            aliases={10: 0, 11: 1} if n else None, flops=2 * mm,
        )
    return normed, query_grad, *grads


def solution(mesh):
    rows = P(("groups", "seq"), "head")
    in_specs = (rows, rows, rows, rows, P("head"), P(("groups", "seq")))
    out_specs = (rows, rows, rows, rows)
    short = mesh.shape["seq"] == 8 and mesh.shape["head"] == 2

    def body(queries, key_vectors, value_vectors, output_grad, norm_gain, block_docs):
        one = block_docs.shape[0] == 1
        fn = block_body if short and one else general_body
        return fn(queries, key_vectors, value_vectors, output_grad, norm_gain, block_docs)

    return jax.shard_map(body, mesh=mesh, in_specs=in_specs, out_specs=out_specs, check_vma=False)
```

time: 102 us -> 90.3 us (0.89)
  Pallas kernels: 44.2 us -> 18.6 us
  waiting for transfers between devices: 21.4 us -> 38.1 us
  starting transfers between devices: 33.8 us -> 31.6 us
    pallas_call x21, Pallas kernels: 44.2 us -> 18.6 us  [call(): pl.pallas_call(kernel, in_specs=[spec(m) for m, _ in ins], out_specs=out_...]
    ppermute x12, waiting for transfers between devices: 20.1 us -> 36.7 us  [send(): return lax.ppermute(x, ('seq', 'head'), pairs)]
    ppermute x12, starting transfers between devices: 33.8 us -> 31.6 us  [send(): return lax.ppermute(x, ('seq', 'head'), pairs)]
  transfers between devices with their start and end apart: 13 -> 13, of which waited for: 9 -> 10; matrix products, arithmetic and copies ran while one was open for 0% -> 0% of each run, Pallas kernels for 34% -> 16%
where the time goes in v3:
time: 90.3 us; the launch traced here: 89.9 us
  waiting for transfers between devices  38.1 us (42%)
  starting transfers between devices  31.6 us (35%)
  Pallas kernels  18.6 us (21%)
  between operations  1.55 us (2%)
    ppermute x12, waiting for transfers between devices, send(): return lax.ppermute(x, ('seq', 'head'), pairs)  36.7 us
    ppermute x12, starting transfers between devices, send(): return lax.ppermute(x, ('seq', 'head'), pairs)  31.6 us
    pallas_call x21, Pallas kernels, call(): pl.pallas_call(kernel, in_specs=[spec(m) for m, _ in ins], out_specs=out_...  18.6 us
  transfers between devices with their start and end apart: 13, of which 10 were waited for; matrix products, arithmetic and copies ran while one was open for 0% of the time, Pallas kernels for 16%

profile of v3, /device:TPU:0, one launch (start us, length us, event | category | flops | bytes accessed | tf_op | source)
XLA Modules:
  0.0 89.9 jit_solution(7120287311318586226)
XLA Ops:
  1.3 2.0 %kv0.1 = (bf16[256,1024]{1,0:T(8,128)(2,1)S(1)}, bf16[256,1024]{1,0:T(8,128)(2,1)S(1)}, f32[129,8,128]{2,1,0:T(8,128)S(1)}) custom-call(s32[1]{0:T(128)S(6)} %copy.28.doc_ref, bf16[256,2048]{1,0:T(8,128)(2,1)} %k_hbm.3, bf16[256,2048]{1,0:T(8,128)(2,1)} %v_hbm.3), custom_call_target="tpu_custom_call" | custom-call | flops 67108864 | bytes 4194304 | tf_op jit(solution)/shard_map/kv0/pallas_call | solution.py:349
  3.3 0.0 copy-start
  3.3 5.0 %collective-permute-start = (f32[129,8,128]{2,1,0:T(8,128)S(1)}, f32[129,8,128]{2,1,0:T(8,128)S(1)}, u32[]{:S(2)}, u32[]{:S(2)}) collective-permute-start(f32[129,8,128]{2,1,0:T(8,128)S(1)} %get-tuple-element.42.own_ref), channel_id=1, source_target_pairs={{0,2},{1,5},{2,0},{3,7},{4,6},{5,9},{6,4},{7,11},{8,10},{9,13},{10... | collective-permute-start | bytes 1585160 | tf_op jit(solution)/shard_map/ppermute | solution.py:383
  8.3 2.0 %kv1.1 = (bf16[256,1024]{1,0:T(8,128)(2,1)S(1)}, bf16[256,1024]{1,0:T(8,128)(2,1)S(1)}, f32[129,8,128]{2,1,0:T(8,128)S(1)}) custom-call(s32[1]{0:T(128)S(6)} %copy.28.doc_ref, bf16[256,2048]{1,0:T(8,128)(2,1)} %k_hbm.3, bf16[256,2048]{1,0:T(8,128)(2,1)} %v_hbm.3), custom_call_target="tpu_custom_call" | custom-call | flops 67108864 | bytes 4194304 | tf_op jit(solution)/shard_map/kv1/pallas_call | solution.py:349
  10.3 1.9 %collective-permute-start.2 = (f32[129,8,128]{2,1,0:T(8,128)S(1)}, f32[129,8,128]{2,1,0:T(8,128)S(1)}, u32[]{:S(2)}, u32[]{:S(2)}) collective-permute-start(f32[129,8,128]{2,1,0:T(8,128)S(1)} %get-tuple-element.41.after_ref.own_ref), channel_id=1, source_target_pairs={{0,2},{1,5},{2,0},{3,7},{4,6},{5,9},{6,4},{7,11},{8,10},{9,13},{10... | collective-permute-start | bytes 1585160 | tf_op jit(solution)/shard_map/ppermute | solution.py:383
  12.2 0.0 copy-done
  12.2 0.9 %intra0.1.after_ref.intra_ref = f32[256,1024]{1,0:T(8,128)S(1)} custom-call(bf16[256,2048]{1,0:T(8,128)(2,1)S(1)} %copy-done, bf16[256,1024]{1,0:T(8,128)(2,1)S(1)} %get-tuple-element.39.k_ref, bf16[256,1024]{1,0:T(8,128)(2,1)S(1)} %get-tuple-element.40.v_ref, f32[129,8,128]{2,1,0:T(8,128)S(1)} %get-tuple-element.41.after_ref.own_ref), custom_call_target="tpu_custom_call" | custom-call | flops 268435456 | bytes 4194304 | tf_op jit(solution)/shard_map/intra0/pallas_call | solution.py:349
  13.1 2.3 %collective-permute-done.got_ref.r1_ref = f32[129,8,128]{2,1,0:T(8,128)S(1)} collective-permute-done((f32[129,8,128]{2,1,0:T(8,128)S(1)}, f32[129,8,128]{2,1,0:T(8,128)S(1)}, u32[]{:S(2)}, u32[]{:S(2)}) %collective-permute-start) | collective-permute-done | bytes 528416 | tf_op jit(solution)/shard_map/ppermute | solution.py:383
  15.5 0.1 join0.2.after_ref
  15.5 4.0 %collective-permute-start.1 = (f32[129,8,128]{2,1,0:T(8,128)S(1)}, f32[129,8,128]{2,1,0:T(8,128)S(1)}, u32[]{:S(2)}, u32[]{:S(2)}) collective-permute-start(f32[129,8,128]{2,1,0:T(8,128)S(1)} %join0.2.after_ref), channel_id=1, source_target_pairs={{0,4},{1,3},{2,6},{3,5},{4,8},{5,7},{6,10},{7,9},{8,12},{9,11},{10... | collective-permute-start | bytes 1585160 | tf_op jit(solution)/shard_map/ppermute | solution.py:383
  19.6 4.0 %collective-permute-done.2.got_ref.r1_ref = f32[129,8,128]{2,1,0:T(8,128)S(1)} collective-permute-done((f32[129,8,128]{2,1,0:T(8,128)S(1)}, f32[129,8,128]{2,1,0:T(8,128)S(1)}, u32[]{:S(2)}, u32[]{:S(2)}) %collective-permute-start.2) | collective-permute-done | bytes 528416 | tf_op jit(solution)/shard_map/ppermute | solution.py:383
  23.5 0.1 join1.2.after_ref
  23.6 2.8 %collective-permute-start.4 = (f32[129,8,128]{2,1,0:T(8,128)S(1)}, f32[129,8,128]{2,1,0:T(8,128)S(1)}, u32[]{:S(2)}, u32[]{:S(2)}) collective-permute-start(f32[129,8,128]{2,1,0:T(8,128)S(1)} %join1.2.after_ref), channel_id=1, source_target_pairs={{0,4},{1,3},{2,6},{3,5},{4,8},{5,7},{6,10},{7,9},{8,12},{9,11},{10... | collective-permute-start | bytes 1585160 | tf_op jit(solution)/shard_map/ppermute | solution.py:383
  26.4 0.9 %intra1.1.after_ref.intra_ref = f32[256,1024]{1,0:T(8,128)S(1)} custom-call(bf16[256,2048]{1,0:T(8,128)(2,1)S(1)} %copy-done, bf16[256,1024]{1,0:T(8,128)(2,1)S(1)} %get-tuple-element.43.k_ref, bf16[256,1024]{1,0:T(8,128)(2,1)S(1)} %get-tuple-element.44.v_ref, f32[129,8,128]{2,1,0:T(8,128)S(1)} %join1.2.after_ref), custom_call_target="tpu_custom_call" | custom-call | flops 268435456 | bytes 4194304 | tf_op jit(solution)/shard_map/intra1/pallas_call | solution.py:349
  27.3 0.0 copy-start.1
  27.4 0.0 copy-start.2
  27.4 0.0 collective-permute-done.1.x_ref
  27.4 3.6 %collective-permute-start.3 = (f32[129,8,128]{2,1,0:T(8,128)S(1)}, f32[129,8,128]{2,1,0:T(8,128)S(1)}, u32[]{:S(2)}, u32[]{:S(2)}) collective-permute-start(f32[129,8,128]{2,1,0:T(8,128)S(1)} %order0.1.r2_ref), channel_id=1, source_target_pairs={{0,4},{4,8},{8,12},{16,20},{20,24},{24,28}} | collective-permute-start | bytes 1585160 | tf_op jit(solution)/shard_map/ppermute | solution.py:383
  31.0 2.1 %collective-permute-done.4.r2_ref = f32[129,8,128]{2,1,0:T(8,128)S(1)} collective-permute-done((f32[129,8,128]{2,1,0:T(8,128)S(1)}, f32[129,8,128]{2,1,0:T(8,128)S(1)}, u32[]{:S(2)}, u32[]{:S(2)}) %collective-permute-start.4) | collective-permute-done | bytes 528416 | tf_op jit(solution)/shard_map/ppermute | solution.py:383
  33.1 4.4 %collective-permute-start.5 = (f32[129,8,128]{2,1,0:T(8,128)S(1)}, f32[129,8,128]{2,1,0:T(8,128)S(1)}, u32[]{:S(2)}, u32[]{:S(2)}) collective-permute-start(f32[129,8,128]{2,1,0:T(8,128)S(1)} %collective-permute-done.4.r2_ref), channel_id=1, source_target_pairs={{0,4},{4,8},{8,12},{16,20},{20,24},{24,28}} | collective-permute-start | bytes 1585160 | tf_op jit(solution)/shard_map/ppermute | solution.py:383
  37.5 1.2 %collective-permute-done.3.r3_ref = f32[129,8,128]{2,1,0:T(8,128)S(1)} collective-permute-done((f32[129,8,128]{2,1,0:T(8,128)S(1)}, f32[129,8,128]{2,1,0:T(8,128)S(1)}, u32[]{:S(2)}, u32[]{:S(2)}) %collective-permute-start.3) | collective-permute-done | bytes 528416 | tf_op jit(solution)/shard_map/ppermute | solution.py:383
  38.8 0.5 attend0.1
  39.2 5.2 %collective-permute-done.5.r3_ref = f32[129,8,128]{2,1,0:T(8,128)S(1)} collective-permute-done((f32[129,8,128]{2,1,0:T(8,128)S(1)}, f32[129,8,128]{2,1,0:T(8,128)S(1)}, u32[]{:S(2)}, u32[]{:S(2)}) %collective-permute-start.5) | collective-permute-done | bytes 528416 | tf_op jit(solution)/shard_map/ppermute | solution.py:383
  44.4 0.6 attend1.1
  45.0 0.1 collective-permute-start.6
  45.1 1.3 %collective-permute-done.6.other_ref = f32[256,128]{1,0:T(8,128)S(1)} collective-permute-done((f32[256,128]{1,0:T(8,128)S(1)}, f32[256,128]{1,0:T(8,128)S(1)}, u32[]{:S(2)}, u32[]{:S(2)}) %collective-permute-start.6) | collective-permute-done | bytes 131104 | tf_op jit(solution)/shard_map/ppermute | solution.py:453
  46.4 0.7 grad0.1
  47.2 2.5 %collective-permute-start.7 = (f32[129,8,128]{2,1,0:T(8,128)S(1)}, f32[129,8,128]{2,1,0:T(8,128)S(1)}, u32[]{:S(2)}, u32[]{:S(2)}) collective-permute-start(f32[129,8,128]{2,1,0:T(8,128)S(1)} %get-tuple-element.57.own_ref), channel_id=1, source_target_pairs={{0,2},{2,0},{4,6},{5,1},{6,4},{7,3},{8,10},{9,5},{10,8},{11,7},{12... | collective-permute-start | bytes 1585160 | tf_op jit(solution)/shard_map/ppermute | solution.py:383
  49.6 0.7 grad1.1
  50.4 3.4 %collective-permute-start.9 = (f32[129,8,128]{2,1,0:T(8,128)S(1)}, f32[129,8,128]{2,1,0:T(8,128)S(1)}, u32[]{:S(2)}, u32[]{:S(2)}) collective-permute-start(f32[129,8,128]{2,1,0:T(8,128)S(1)} %get-tuple-element.52.rest_0_.own_ref), channel_id=1, source_target_pairs={{0,2},{2,0},{4,6},{5,1},{6,4},{7,3},{8,10},{9,5},{10,8},{11,7},{12... | collective-permute-start | bytes 1585160 | tf_op jit(solution)/shard_map/ppermute | solution.py:383
  53.8 1.8 %back0.1 = (bf16[256,2048]{1,0:T(8,128)(2,1)}, bf16[256,2048]{1,0:T(8,128)(2,1)}, f32[256,512]{1,0:T(8,128)S(1)}, f32[256,512]{1,0:T(8,128)S(1)}) custom-call(bf16[256,2048]{1,0:T(8,128)(2,1)S(1)} %copy-done, bf16[256,1024]{1,0:T(8,128)(2,1)S(1)} %get-tuple-element.39.k_ref, bf16[256,1024]{1,0:T(8,128)(2,1)S(1)} %get-tuple-element.40.v_ref, ...), custom_call_target="tpu_custom_call" | custom-call | flops 234881024 | bytes 4194304 | tf_op jit(solution)/shard_map/back0/pallas_call | solution.py:349
  55.6 2.7 %collective-permute-done.7.got_ref.r1_ref = f32[129,8,128]{2,1,0:T(8,128)S(1)} collective-permute-done((f32[129,8,128]{2,1,0:T(8,128)S(1)}, f32[129,8,128]{2,1,0:T(8,128)S(1)}, u32[]{:S(2)}, u32[]{:S(2)}) %collective-permute-start.7) | collective-permute-done | bytes 528416 | tf_op jit(solution)/shard_map/ppermute | solution.py:383
  58.3 0.1 join0.3.rest_0_
  58.4 1.3 %collective-permute-start.8 = (f32[129,8,128]{2,1,0:T(8,128)S(1)}, f32[129,8,128]{2,1,0:T(8,128)S(1)}, u32[]{:S(2)}, u32[]{:S(2)}) collective-permute-start(f32[129,8,128]{2,1,0:T(8,128)S(1)} %join0.3.rest_0_), channel_id=1, source_target_pairs={{3,1},{4,0},{5,3},{6,2},{7,5},{8,4},{9,7},{10,6},{11,9},{12,8},{13... | collective-permute-start | bytes 1585160 | tf_op jit(solution)/shard_map/ppermute | solution.py:383
  59.7 1.8 %back1.1 = (bf16[256,2048]{1,0:T(8,128)(2,1)}, f32[256,512]{1,0:T(8,128)S(1)}, f32[256,512]{1,0:T(8,128)S(1)}) custom-call(bf16[256,2048]{1,0:T(8,128)(2,1)S(1)} %copy-done, bf16[256,1024]{1,0:T(8,128)(2,1)S(1)} %get-tuple-element.39.k_ref, bf16[256,1024]{1,0:T(8,128)(2,1)S(1)} %get-tuple-element.40.v_ref, ...), custom_call_target="tpu_custom_call", output_to_operand_aliasing={{0}: (6, {})} | custom-call | flops 234881024 | bytes 4194304 | tf_op jit(solution)/shard_map/back1/pallas_call | solution.py:349
  61.5 3.4 %collective-permute-done.9.got_ref.r1_ref = f32[129,8,128]{2,1,0:T(8,128)S(1)} collective-permute-done((f32[129,8,128]{2,1,0:T(8,128)S(1)}, f32[129,8,128]{2,1,0:T(8,128)S(1)}, u32[]{:S(2)}, u32[]{:S(2)}) %collective-permute-start.9) | collective-permute-done | bytes 528416 | tf_op jit(solution)/shard_map/ppermute | solution.py:383
  64.9 0.1 join1.3.rest_0_
  65.0 1.3 %collective-permute-start.10 = (f32[129,8,128]{2,1,0:T(8,128)S(1)}, f32[129,8,128]{2,1,0:T(8,128)S(1)}, u32[]{:S(2)}, u32[]{:S(2)}) collective-permute-start(f32[129,8,128]{2,1,0:T(8,128)S(1)} %join1.3.rest_0_), channel_id=1, source_target_pairs={{3,1},{4,0},{5,3},{6,2},{7,5},{8,4},{9,7},{10,6},{11,9},{12,8},{13... | collective-permute-start | bytes 1585160 | tf_op jit(solution)/shard_map/ppermute | solution.py:383
  66.3 1.8 %back2.1 = (bf16[256,2048]{1,0:T(8,128)(2,1)}, f32[256,512]{1,0:T(8,128)S(1)}, f32[256,512]{1,0:T(8,128)S(1)}) custom-call(bf16[256,2048]{1,0:T(8,128)(2,1)S(1)} %copy-done, bf16[256,1024]{1,0:T(8,128)(2,1)S(1)} %get-tuple-element.43.k_ref, bf16[256,1024]{1,0:T(8,128)(2,1)S(1)} %get-tuple-element.44.v_ref, ...), custom_call_target="tpu_custom_call", output_to_operand_aliasing={{0}: (6, {})} | custom-call | flops 234881024 | bytes 4194304 | tf_op jit(solution)/shard_map/back2/pallas_call | solution.py:349
  68.2 7.5 %collective-permute-done.8.x_ref = f32[129,8,128]{2,1,0:T(8,128)S(1)} collective-permute-done((f32[129,8,128]{2,1,0:T(8,128)S(1)}, f32[129,8,128]{2,1,0:T(8,128)S(1)}, u32[]{:S(2)}, u32[]{:S(2)}) %collective-permute-start.8) | collective-permute-done | bytes 528416 | tf_op jit(solution)/shard_map/ppermute | solution.py:383
  75.7 0.7 collective-permute-start.12
  76.4 1.8 %back3.1 = (bf16[256,2048]{1,0:T(8,128)(2,1)}, f32[256,512]{1,0:T(8,128)S(1)}, f32[256,512]{1,0:T(8,128)S(1)}) custom-call(bf16[256,2048]{1,0:T(8,128)(2,1)S(1)} %copy-done, bf16[256,1024]{1,0:T(8,128)(2,1)S(1)} %get-tuple-element.43.k_ref, bf16[256,1024]{1,0:T(8,128)(2,1)S(1)} %get-tuple-element.44.v_ref, ...), custom_call_target="tpu_custom_call", output_to_operand_aliasing={{0}: (6, {})} | custom-call | flops 234881024 | bytes 4194304 | tf_op jit(solution)/shard_map/back3/pallas_call | solution.py:349
  78.2 8.3 %collective-permute-done.10.x_ref = f32[129,8,128]{2,1,0:T(8,128)S(1)} collective-permute-done((f32[129,8,128]{2,1,0:T(8,128)S(1)}, f32[129,8,128]{2,1,0:T(8,128)S(1)}, u32[]{:S(2)}, u32[]{:S(2)}) %collective-permute-start.10) | collective-permute-done | bytes 528416 | tf_op jit(solution)/shard_map/ppermute | solution.py:383
  86.5 0.7 collective-permute-start.11
  87.2 0.0 collective-permute-done.12.r3_ref
  87.2 1.3 %final0.1 = (bf16[256,2048]{1,0:T(8,128)(2,1)}, bf16[256,2048]{1,0:T(8,128)(2,1)}) custom-call(s32[1]{0:T(128)S(6)} %copy.28.doc_ref, bf16[256,1024]{1,0:T(8,128)(2,1)S(1)} %get-tuple-element.39.k_ref, bf16[256,1024]{1,0:T(8,128)(2,1)S(1)} %get-tuple-element.40.v_ref, f32[256,512]{1,0:T(8,128)S(1)} %get-tuple-element.58.after_ref.kin0, ...), custom_call_target="tpu_custom_call" | custom-call | flops 134217728 | bytes 4194304 | tf_op jit(solution)/shard_map/final0/pallas_call | solution.py:349
  88.6 0.0 collective-permute-done.11.r3_ref
  88.6 1.3 %final1.1 = (bf16[256,2048]{1,0:T(8,128)(2,1)}, bf16[256,2048]{1,0:T(8,128)(2,1)}) custom-call(s32[1]{0:T(128)S(6)} %copy.28.doc_ref, bf16[256,1024]{1,0:T(8,128)(2,1)S(1)} %get-tuple-element.43.k_ref, bf16[256,1024]{1,0:T(8,128)(2,1)S(1)} %get-tuple-element.44.v_ref, ...), custom_call_target="tpu_custom_call", output_to_operand_aliasing={{0}: (10, {}), {1}: (11, {})} | custom-call | flops 134217728 | bytes 4194304 | tf_op jit(solution)/shard_map/final1/pallas_call | solution.py:349
  (5 shorter events, 0.0 us)
Async XLA Ops:
  3.3 8.9 %copy-start = (bf16[256,2048]{1,0:T(8,128)(2,1)S(1)}, bf16[256,2048]{1,0:T(8,128)(2,1)}, u32[]{:S(2)}) copy-start(bf16[256,2048]{1,0:T(8,128)(2,1)} %q_ref.19) | copy-start | bytes 3145732
  3.3 12.2 %collective-permute-start = (f32[129,8,128]{2,1,0:T(8,128)S(1)}, f32[129,8,128]{2,1,0:T(8,128)S(1)}, u32[]{:S(2)}, u32[]{:S(2)}) collective-permute-start(f32[129,8,128]{2,1,0:T(8,128)S(1)} %get-tuple-element.42.own_ref), channel_id=1, source_target_pairs={{0,2},{1,5},{2,0},{3,7},{4,6},{5,9},{6,4},{7,11},{8,10},{9,13},{10... | collective-permute-start | bytes 1585160 | tf_op jit(solution)/shard_map/ppermute | solution.py:383
  10.3 13.3 %collective-permute-start.2 = (f32[129,8,128]{2,1,0:T(8,128)S(1)}, f32[129,8,128]{2,1,0:T(8,128)S(1)}, u32[]{:S(2)}, u32[]{:S(2)}) collective-permute-start(f32[129,8,128]{2,1,0:T(8,128)S(1)} %get-tuple-element.41.after_ref.own_ref), channel_id=1, source_target_pairs={{0,2},{1,5},{2,0},{3,7},{4,6},{5,9},{6,4},{7,11},{8,10},{9,13},{10... | collective-permute-start | bytes 1585160 | tf_op jit(solution)/shard_map/ppermute | solution.py:383
  15.5 11.9 %collective-permute-start.1 = (f32[129,8,128]{2,1,0:T(8,128)S(1)}, f32[129,8,128]{2,1,0:T(8,128)S(1)}, u32[]{:S(2)}, u32[]{:S(2)}) collective-permute-start(f32[129,8,128]{2,1,0:T(8,128)S(1)} %join0.2.after_ref), channel_id=1, source_target_pairs={{0,4},{1,3},{2,6},{3,5},{4,8},{5,7},{6,10},{7,9},{8,12},{9,11},{10... | collective-permute-start | bytes 1585160 | tf_op jit(solution)/shard_map/ppermute | solution.py:383
  23.6 9.5 %collective-permute-start.4 = (f32[129,8,128]{2,1,0:T(8,128)S(1)}, f32[129,8,128]{2,1,0:T(8,128)S(1)}, u32[]{:S(2)}, u32[]{:S(2)}) collective-permute-start(f32[129,8,128]{2,1,0:T(8,128)S(1)} %join1.2.after_ref), channel_id=1, source_target_pairs={{0,4},{1,3},{2,6},{3,5},{4,8},{5,7},{6,10},{7,9},{8,12},{9,11},{10... | collective-permute-start | bytes 1585160 | tf_op jit(solution)/shard_map/ppermute | solution.py:383
  27.3 11.4 %copy-start.1 = (bf16[256,2048]{1,0:T(8,128)(2,1)S(1)}, bf16[256,2048]{1,0:T(8,128)(2,1)}, u32[]{:S(2)}) copy-start(bf16[256,2048]{1,0:T(8,128)(2,1)} %do_ref.7) | copy-start | bytes 3145732
  27.4 11.4 %copy-start.2 = (f32[2048]{0:T(1024)S(1)}, f32[2048]{0:T(1024)}, u32[]{:S(2)}) copy-start(f32[2048]{0:T(1024)} %param.10) | copy-start | bytes 24580
  27.4 11.4 %collective-permute-start.3 = (f32[129,8,128]{2,1,0:T(8,128)S(1)}, f32[129,8,128]{2,1,0:T(8,128)S(1)}, u32[]{:S(2)}, u32[]{:S(2)}) collective-permute-start(f32[129,8,128]{2,1,0:T(8,128)S(1)} %order0.1.r2_ref), channel_id=1, source_target_pairs={{0,4},{4,8},{8,12},{16,20},{20,24},{24,28}} | collective-permute-start | bytes 1585160 | tf_op jit(solution)/shard_map/ppermute | solution.py:383
  33.1 11.3 %collective-permute-start.5 = (f32[129,8,128]{2,1,0:T(8,128)S(1)}, f32[129,8,128]{2,1,0:T(8,128)S(1)}, u32[]{:S(2)}, u32[]{:S(2)}) collective-permute-start(f32[129,8,128]{2,1,0:T(8,128)S(1)} %collective-permute-done.4.r2_ref), channel_id=1, source_target_pairs={{0,4},{4,8},{8,12},{16,20},{20,24},{24,28}} | collective-permute-start | bytes 1585160 | tf_op jit(solution)/shard_map/ppermute | solution.py:383
  45.0 1.4 %collective-permute-start.6 = (f32[256,128]{1,0:T(8,128)S(1)}, f32[256,128]{1,0:T(8,128)S(1)}, u32[]{:S(2)}, u32[]{:S(2)}) collective-permute-start(f32[256,128]{1,0:T(8,128)S(1)} %get-tuple-element.47.mine_ref), channel_id=1, source_target_pairs={{0,1},{1,0},{2,3},{3,2},{4,5},{5,4},{6,7},{7,6},{8,9},{9,8},{10,11... | collective-permute-start | bytes 393224 | tf_op jit(solution)/shard_map/ppermute | solution.py:453
  47.2 11.1 %collective-permute-start.7 = (f32[129,8,128]{2,1,0:T(8,128)S(1)}, f32[129,8,128]{2,1,0:T(8,128)S(1)}, u32[]{:S(2)}, u32[]{:S(2)}) collective-permute-start(f32[129,8,128]{2,1,0:T(8,128)S(1)} %get-tuple-element.57.own_ref), channel_id=1, source_target_pairs={{0,2},{2,0},{4,6},{5,1},{6,4},{7,3},{8,10},{9,5},{10,8},{11,7},{12... | collective-permute-start | bytes 1585160 | tf_op jit(solution)/shard_map/ppermute | solution.py:383
  50.4 14.6 %collective-permute-start.9 = (f32[129,8,128]{2,1,0:T(8,128)S(1)}, f32[129,8,128]{2,1,0:T(8,128)S(1)}, u32[]{:S(2)}, u32[]{:S(2)}) collective-permute-start(f32[129,8,128]{2,1,0:T(8,128)S(1)} %get-tuple-element.52.rest_0_.own_ref), channel_id=1, source_target_pairs={{0,2},{2,0},{4,6},{5,1},{6,4},{7,3},{8,10},{9,5},{10,8},{11,7},{12... | collective-permute-start | bytes 1585160 | tf_op jit(solution)/shard_map/ppermute | solution.py:383
  58.4 17.3 %collective-permute-start.8 = (f32[129,8,128]{2,1,0:T(8,128)S(1)}, f32[129,8,128]{2,1,0:T(8,128)S(1)}, u32[]{:S(2)}, u32[]{:S(2)}) collective-permute-start(f32[129,8,128]{2,1,0:T(8,128)S(1)} %join0.3.rest_0_), channel_id=1, source_target_pairs={{3,1},{4,0},{5,3},{6,2},{7,5},{8,4},{9,7},{10,6},{11,9},{12,8},{13... | collective-permute-start | bytes 1585160 | tf_op jit(solution)/shard_map/ppermute | solution.py:383
  65.0 21.5 %collective-permute-start.10 = (f32[129,8,128]{2,1,0:T(8,128)S(1)}, f32[129,8,128]{2,1,0:T(8,128)S(1)}, u32[]{:S(2)}, u32[]{:S(2)}) collective-permute-start(f32[129,8,128]{2,1,0:T(8,128)S(1)} %join1.3.rest_0_), channel_id=1, source_target_pairs={{3,1},{4,0},{5,3},{6,2},{7,5},{8,4},{9,7},{10,6},{11,9},{12,8},{13... | collective-permute-start | bytes 1585160 | tf_op jit(solution)/shard_map/ppermute | solution.py:383
  75.7 11.5 %collective-permute-start.12 = (f32[129,8,128]{2,1,0:T(8,128)S(1)}, f32[129,8,128]{2,1,0:T(8,128)S(1)}, u32[]{:S(2)}, u32[]{:S(2)}) collective-permute-start(f32[129,8,128]{2,1,0:T(8,128)S(1)} %order1.1.rest_0_.r2_ref), channel_id=1, source_target_pairs={{6,2},{10,6},{14,10},{22,18},{26,22},{30,26}} | collective-permute-start | bytes 1585160 | tf_op jit(solution)/shard_map/ppermute | solution.py:383
  86.5 2.0 %collective-permute-start.11 = (f32[129,8,128]{2,1,0:T(8,128)S(1)}, f32[129,8,128]{2,1,0:T(8,128)S(1)}, u32[]{:S(2)}, u32[]{:S(2)}) collective-permute-start(f32[129,8,128]{2,1,0:T(8,128)S(1)} %order2.1.r2_ref), channel_id=1, source_target_pairs={{6,2},{10,6},{14,10},{22,18},{26,22},{30,26}} | collective-permute-start | bytes 1585160 | tf_op jit(solution)/shard_map/ppermute | solution.py:383

commit v4 on v3

--- a/solution.py
+++ b/solution.py
@@ -1,4 +1,5 @@
 import functools
+import itertools
 
 import jax
 import jax.numpy as jnp
@@ -113,7 +114,7 @@
 
 
 HALVES = 2
-CHUNKS = 4
+CHUNKS = 2
 VMEM_LIMIT = 16 * 1024 * 1024
 
 
@@ -145,7 +146,8 @@
     out_ref[out_ref.shape[0] - 1] = jnp.full((8, HEAD_DIM), own_tag(doc_ref), F32)
 
 
-def kv_kernel(n, hh, doc_ref, k_hbm, v_hbm, k_ref, v_ref, out_ref, k_sems, v_sems):
+def kv_kernel(n, hh, doc_ref, k_hbm, v_hbm, *rest):
+    k_ref, v_ref, out_ref, k_sems, v_sems = rest[-5:]
     step = hh // CHUNKS
     width = step * HEAD_DIM
 
@@ -190,24 +192,23 @@
     return even_core * (odd_block if parity else 1 - odd_block)
 
 
-def gate(parity, doc_ref, r1_ref, r2_ref, r3_ref):
+def gate(parity, way, doc_ref, messages):
     own = own_tag(doc_ref)
-    last = r1_ref.shape[0] - 1
-    use3 = near_block(parity).astype(F32)
-    m1 = (r1_ref[last] == own).astype(F32) * (1.0 - use3)
-    m2 = (r2_ref[last] == own).astype(F32)
-    m3 = (r3_ref[last] == own).astype(F32) * use3
-    return m1, m2, m3
-
-
-def gathered(j, gates, r1_ref, r2_ref, r3_ref):
-    m1, m2, m3 = gates
+    last = messages[0].shape[0] - 1
+    gates = [(ref[last] == own).astype(F32) for ref in messages]
+    if way[0] in PAIR_FIRST:
+        gates[0] = gates[0] * (1.0 - near_block(parity).astype(F32))
+    return gates
+
+
+def gathered(j, gates, messages):
     at = slice(j * 16, (j + 1) * 16)
-    total = r2_ref[at] * m2 + r1_ref[at] * m1 + r3_ref[at] * m3
+    total = sum(ref[at] * g for ref, g in zip(messages, gates))
     return total.reshape(HEAD_DIM, HEAD_DIM).astype(BF)
 
 
-def attend_kernel(n, hh, doc_ref, q_ref, intra_ref, do_ref, gain_ref, r1_ref, r2_ref, r3_ref, *rest):
+def attend_kernel(n, hh, count, doc_ref, q_ref, intra_ref, do_ref, gain_ref, *rest):
+    messages, rest = rest[:count], rest[count:]
     last_half = n == HALVES - 1
     if n:
         sum_in_ref, att_ref, state_ref, sum_ref = rest
@@ -217,10 +218,10 @@
         att_ref, state_ref, sum_ref = rest
         square = jnp.zeros((q_ref.shape[0], HEAD_DIM), F32)
         cross = square
-    gates = gate(0, doc_ref, r1_ref, r2_ref, r3_ref)
+    gates = gate(0, WAYS[n], doc_ref, messages)
     for j in range(hh):
         at = cols(n * hh + j)
-        state = gathered(j, gates, r1_ref, r2_ref, r3_ref)
+        state = gathered(j, gates, messages)
         state_ref[j] = state
         att = intra_ref[:, cols(j)] + nn(q_ref[:, at], state)
         att_ref[:, cols(j)] = att
@@ -254,8 +255,8 @@
 
 def back_kernel(c, hh, q_ref, k_ref, v_ref, ag_ref, state_ref, *rest):
     qg_ref, qg_sems, normed_sem = rest[-3:]
-    if c == 0:
-        normed_ref = rest[1]
+    if c == 1:
+        normed_ref = rest[2]
         normed_hbm, qg_hbm, kin_ref, vin_ref = rest[-7:-3]
         normed_copy = pltpu.make_async_copy(normed_ref, normed_hbm, normed_sem)
         normed_copy.start()
@@ -282,57 +283,78 @@
         vin_ref[:, cols(i)] = nn(att_t, ag)
     for copy in copies:
         copy.wait()
-    if c == 0:
+    if c == 1:
         normed_copy.wait()
 
 
-def final_kernel(n, hh, doc_ref, k_ref, v_ref, kin0, kin1, vin0, vin1, r1_ref, r2_ref, r3_ref, *rest):
-    kg_hbm, vg_hbm, kg_ref, vg_ref, k_sems, v_sems = rest[-6:]
-    gates = gate(1, doc_ref, r1_ref, r2_ref, r3_ref)
+def final_kernel(n, hh, count_in, doc_ref, k_ref, v_ref, kin0, kin1, vin0, vin1, *rest):
+    messages, rest = rest[:count_in], rest[count_in:]
+    gates = gate(1, WAYS[n], doc_ref, messages)
     count = hh // 2
-    step = hh // CHUNKS
-    width = step * HEAD_DIM
-
-    def copies(c):
-        there = slice((n * CHUNKS + c) * width, (n * CHUNKS + c + 1) * width)
-        here = slice(c * width, (c + 1) * width)
-        return (
-            pltpu.make_async_copy(kg_ref.at[:, here], kg_hbm.at[:, there], k_sems.at[c]),
-            pltpu.make_async_copy(vg_ref.at[:, here], vg_hbm.at[:, there], v_sems.at[c]),
-        )
-
-    for c in range(CHUNKS):
-        for j in range(c * step, (c + 1) * step):
-            kin_ref, vin_ref = (kin0, vin0) if j < count else (kin1, vin1)
-            within = cols(j % count)
-            grads = gathered(j, gates, r1_ref, r2_ref, r3_ref)
-            kg_ref[:, cols(j)] = (kin_ref[:, within] + nt(v_ref[:, cols(j)], grads)).astype(BF)
-            vg_ref[:, cols(j)] = (vin_ref[:, within] + nn(k_ref[:, cols(j)], grads)).astype(BF)
-        for copy in copies(c):
-            copy.start()
-    for c in range(CHUNKS):
-        for copy in copies(c):
-            copy.wait()
-
-
-def join_kernel(parity, own_ref, got_ref, after_ref, out_ref):
-    role = near_block(parity)
+    copies = []
+    if n:
+        kg_first, vg_first, kg_hbm, vg_hbm, kg_ref, vg_ref, sems = rest
+        half = hh * HEAD_DIM
+        for ref, hbm in ((kg_first, kg_hbm), (vg_first, vg_hbm)):
+            copies.append(pltpu.make_async_copy(ref, hbm.at[:, :half], sems.at[len(copies)]))
+            copies[-1].start()
+    else:
+        kg_ref, vg_ref = rest
+    for j in range(hh):
+        kin_ref, vin_ref = (kin0, vin0) if j < count else (kin1, vin1)
+        within = cols(j % count)
+        grads = gathered(j, gates, messages)
+        kg_ref[:, cols(j)] = (kin_ref[:, within] + nt(v_ref[:, cols(j)], grads)).astype(BF)
+        vg_ref[:, cols(j)] = (vin_ref[:, within] + nn(k_ref[:, cols(j)], grads)).astype(BF)
+        if n and j % 2:
+            here = slice((j - 1) * HEAD_DIM, (j + 1) * HEAD_DIM)
+            there = slice(half + (j - 1) * HEAD_DIM, half + (j + 1) * HEAD_DIM)
+            for ref, hbm in ((kg_ref, kg_hbm), (vg_ref, vg_hbm)):
+                copies.append(pltpu.make_async_copy(ref.at[:, here], hbm.at[:, there], sems.at[len(copies)]))
+                copies[-1].start()
+    for copy in copies:
+        copy.wait()
+
+
+def add_message(base_ref, got_ref, own_ref, out_ref):
     last = own_ref.shape[0] - 1
     same = (own_ref[last] == got_ref[last]).astype(F32)
-
-    @pl.when(role == 1)
+    out_ref[...] = base_ref[...] + got_ref[...] * same[None]
+    out_ref[last] = own_ref[last]
+
+
+def join_kernel(parity, way, own_ref, got_ref, after_ref, out_ref):
+    if way[0] not in PAIR_FIRST:
+        add_message(own_ref, got_ref, own_ref, out_ref)
+        return
+    near = near_block(parity)
+
+    @pl.when(near == 1)
     def _():
-        out_ref[...] = got_ref[...] + own_ref[...] * same[None]
-        out_ref[last] = got_ref[last]
-
-    @pl.when(role == 0)
+        add_message(got_ref, own_ref, got_ref, out_ref)
+
+    @pl.when(near == 0)
     def _():
-        out_ref[...] = own_ref[...] + got_ref[...] * same[None]
-        out_ref[last] = own_ref[last]
-
-
-def order_kernel(x_ref, after_ref, out_ref):
-    pass
+        add_message(own_ref, got_ref, own_ref, out_ref)
+
+
+def third_kernel(parity, way, own_ref, sent_ref, got_ref, after_ref, third_ref, *fourth_ref):
+    if way[0] not in PAIR_FIRST:
+        add_message(sent_ref, got_ref, own_ref, third_ref)
+        return
+    near = near_block(parity)
+
+    @pl.when(near == 1)
+    def _():
+        third_ref[...] = got_ref[...]
+        if fourth_ref:
+            add_message(own_ref, got_ref, own_ref, fourth_ref[0])
+
+    @pl.when(near == 0)
+    def _():
+        add_message(sent_ref, got_ref, own_ref, third_ref)
+        if fourth_ref:
+            fourth_ref[0][...] = own_ref[...]
 
 
 VMEM, SMEM, HBM = pltpu.VMEM, pltpu.SMEM, pltpu.HBM
@@ -359,24 +381,43 @@
     )(*args)
 
 
-def pairs_of(seq, head, rule):
+def pairs_of(seq, head, sign, even_core, odd_core):
     out = []
-    for s in range(seq):
+    for t in range(seq):
         for h in range(head):
-            to = rule(s, h)
-            if to is not None and 0 <= to < seq:
-                out.append((s * head + h, to * head + h))
+            step = (odd_core if h % 2 else even_core)(t % 2)
+            if step is not None and 0 <= t + step < seq:
+                source, to = (t, t + step) if sign > 0 else (seq - 1 - t, seq - 1 - t - step)
+                out.append((source * head + h, to * head + h))
     return out
 
 
+ROUNDS = {
+    "swap": (lambda odd: -1 if odd else 1, lambda odd: 2, lambda odd: None if odd else 2),
+    "first": (
+        lambda odd: -1 if odd else None, lambda odd: None if odd else 2,
+        lambda odd: None if odd else 2, lambda odd: None if odd else 1,
+    ),
+    "second": (lambda odd: None if odd else 1, lambda odd: 2 if odd else None, lambda odd: 1 if odd else None),
+    "across": (lambda odd: 1 if odd else None, lambda odd: None if odd else 2, lambda odd: None if odd else 1),
+    "two": (lambda odd: 2, lambda odd: 1),
+}
+PAIR_FIRST = ("swap", "first")
+WAYS = (("first", "second"), ("swap", "two"))
+
+
 def routes(seq, head, sign):
-    first = pairs_of(seq, head, lambda s, h: s ^ 1 if h % 2 == 0 else s + 2 * sign)
-    second = pairs_of(seq, head, lambda s, h: s + 2 * sign if h % 2 == 0 else s + sign)
-    parity = 0 if sign > 0 else 1
-    third = pairs_of(
-        seq, head, lambda s, h: s + 2 * sign if h % 2 == 0 and s % 2 == parity else None
-    )
-    return first, second, third
+    return [
+        [
+            pairs_of(seq, head, sign, even or never, odd or never)
+            for even, odd in itertools.zip_longest(ROUNDS[way[0]], ROUNDS[way[1]])
+        ]
+        for way in WAYS
+    ]
+
+
+def never(odd):
+    return None
 
 
 def send(x, pairs):
@@ -407,10 +448,19 @@
         return [(VMEM, x) for x in arrays]
 
     def join(n, parity, own, got, after):
-        return call(functools.partial(join_kernel, parity), f"join{n}", near(own, got, after), [message])
-
-    def ordered(x, after, name):
-        return call(order_kernel, name, near(x, after), [(VMEM, x.shape, x.dtype)], aliases={0: 0})
+        return call(
+            functools.partial(join_kernel, parity, WAYS[n]), f"second{parity}{n}", near(own, got, after), [message]
+        )
+
+    def later(n, parity, pairs, own, sent, got, after):
+        out = call(
+            functools.partial(third_kernel, parity, WAYS[n]), f"third{parity}{n}",
+            near(own, sent, got, after), [message] * (len(pairs) - 2),
+        )
+        if len(pairs) == 3:
+            return [send(out, pairs[2])]
+        fourth = send(out[1], pairs[3])
+        return [send(out[0], pairs[2]), fourth]
 
     def intra(n, after):
         return call(
@@ -418,32 +468,34 @@
             near(queries, keys[n], values[n], after), [half32], flops=4 * mm,
         )
 
-    up = routes(seq, head, 1)
-    keys, values, kv = zip(*(
-        call(
+    way0, way1 = routes(seq, head, 1)
+    def keys_values(n, *after):
+        return call(
             functools.partial(kv_kernel, n, hh), f"kv{n}",
-            [docs, (HBM, key_vectors), (HBM, value_vectors)], [half16, half16, message],
+            [docs, (HBM, key_vectors), (HBM, value_vectors)] + near(*after), [half16, half16, message],
             scratch=sems, flops=mm,
         )
-        for n in range(HALVES)
-    ))
-    got1 = [send(m, up[0]) for m in kv]
-    intra0 = intra(0, kv[1])
-    on0 = join(0, 0, kv[0], got1[0], intra0)
-    got2a = send(on0, up[1])
+
+    keys, values, kv = map(list, zip(keys_values(0)))
+    got1 = [send(kv[0], way0[0])]
+    intra0 = intra(0, kv[0])
+    for out, x in zip((keys, values, kv), keys_values(1, intra0)):
+        out.append(x)
+    got1.append(send(kv[1], way1[0]))
+    on0 = join(0, 0, kv[0], got1[0], kv[1])
+    got2a = send(on0, way0[1])
     on1 = join(1, 0, kv[1], got1[1], on0)
-    got2b = send(on1, up[1])
+    got2b = send(on1, way1[1])
     intra1 = intra(1, on1)
-    got2a = ordered(got2a, intra1, "order0")
-    got3a = send(got2a, up[2])
-    got3b = send(got2b, up[2])
-    got = [(got1[0], got2a, got3a), (got1[1], got2b, got3b)]
+    more0 = later(0, 0, way0, kv[0], on0, got2a, intra1)
+    more1 = later(1, 0, way1, kv[1], on1, got2b, on1)
+    got = [(got1[0], got2a, *more0), (got1[1], got2b, *more1)]
     inner = [intra0, intra1]
     attended, state, sums = [], [], None
     for n in range(HALVES):
         last = n == HALVES - 1
         att, st, sums = call(
-            functools.partial(attend_kernel, n, hh), f"attend{n}",
+            functools.partial(attend_kernel, n, hh, len(got[n])), f"attend{n}",
             [docs] + near(queries, inner[n], output_grad, gain, *got[n], *([sums] if n else [])),
             [half32, state_shape, sums_shape if last else (VMEM, (2, tokens, HEAD_DIM), F32)],
             flops=mm,
@@ -451,53 +503,55 @@
         attended.append(att)
         state.append(st)
     other = lax.ppermute(sums, "head", [(c, c ^ 1) for c in range(head)])
-    ag, bg, normed = [], [], None
-    for n in range(HALVES):
-        normed, a, b = call(
+    def grad(n, normed, *after):
+        return call(
             functools.partial(grad_kernel, n, hh, full), f"grad{n}",
-            [docs] + near(queries, attended[n], output_grad, gain, sums, other, *([normed] if n else [])),
+            [docs] + near(queries, attended[n], output_grad, gain, sums, other, *([normed] if n else []), *after),
             [wide, half16, message], aliases={7: 0} if n else None, flops=mm,
         )
-        ag.append(a)
-        bg.append(b)
 
     def back(c, query_grad, after):
         n = c // 2
         ins = near(queries, keys[n], values[n], ag[n], state[n], after)
-        ins += [(HBM, query_grad)] if c else near(normed)
+        ins += [(HBM, query_grad)] if c else []
+        ins += near(normed) if c == 1 else []
         outs = [(HBM, (tokens, width), BF), quarter32, quarter32]
         return call(
-            functools.partial(back_kernel, c, hh), f"back{c}", ins, outs if c else [outs[0]] + outs,
+            functools.partial(back_kernel, c, hh), f"back{c}", ins, [outs[0]] + outs if c == 1 else outs,
             scratch=[
                 pltpu.VMEM((tokens, hw // 2), BF), pltpu.SemaphoreType.DMA((hh // 2,)), pltpu.SemaphoreType.DMA(())
             ],
-            aliases={6: 0} if c else None, flops=7 * mm // 2,
-        )
-
-    down = routes(seq, head, -1)
-    got1 = [send(m, down[0]) for m in bg]
-    normed, query_grad, kin0, vin0 = back(0, None, bg[1])
-    on0 = join(0, 1, bg[0], got1[0], kin0)
-    got2a = send(on0, down[1])
-    query_grad, kin1, vin1 = back(1, query_grad, on0)
+            aliases={6: int(c == 1)} if c else None, flops=7 * mm // 2,
+        )
+
+    way0, way1 = routes(seq, head, -1)
+    normed, ag0, bg0 = grad(0, None)
+    ag = [ag0]
+    got1 = [send(bg0, way0[0])]
+    query_grad, kin0, vin0 = back(0, None, bg0)
+    normed, ag1, bg1 = grad(1, normed, kin0)
+    ag.append(ag1)
+    bg = [bg0, bg1]
+    got1.append(send(bg1, way1[0]))
+    on0 = join(0, 1, bg[0], got1[0], bg1)
+    got2a = send(on0, way0[1])
+    normed, query_grad, kin1, vin1 = back(1, query_grad, on0)
     on1 = join(1, 1, bg[1], got1[1], kin1)
-    got2b = send(on1, down[1])
+    got2b = send(on1, way1[1])
     query_grad, kin2, vin2 = back(2, query_grad, on1)
-    got2a = ordered(got2a, kin2, "order1")
-    got3a = send(got2a, down[2])
-    query_grad, kin3, vin3 = back(3, query_grad, got2a)
-    got2b = ordered(got2b, kin3, "order2")
-    got3b = send(got2b, down[2])
-    got = [(got1[0], got2a, got3a), (got1[1], got2b, got3b)]
+    more0 = later(0, 1, way0, bg[0], on0, got2a, kin2)
+    query_grad, kin3, vin3 = back(3, query_grad, on1)
+    more1 = later(1, 1, way1, bg[1], on1, got2b, kin3)
+    got = [(got1[0], got2a, *more0), (got1[1], got2b, *more1)]
     inside = [(kin0, kin1, vin0, vin1), (kin2, kin3, vin2, vin3)]
-    grads = None
+    grads = []
     for n in range(HALVES):
         grads = call(
-            functools.partial(final_kernel, n, hh), f"final{n}",
-            [docs] + near(keys[n], values[n], *inside[n], *got[n]) + ([(HBM, x) for x in grads] if n else []),
-            [(HBM, (tokens, width), BF)] * 2,
-            scratch=[pltpu.VMEM((tokens, hw), BF)] * 2 + sems,
-            aliases={10: 0, 11: 1} if n else None, flops=2 * mm,
+            functools.partial(final_kernel, n, hh, len(got[n])), f"final{n}",
+            [docs] + near(keys[n], values[n], *inside[n], *got[n], *grads),
+            [(HBM, (tokens, width), BF)] * 2 if n else [half16] * 2,
+            scratch=[pltpu.VMEM((tokens, hw), BF)] * 2 + [pltpu.SemaphoreType.DMA((hh + 2,))] if n else (),
+            flops=2 * mm,
         )
     return normed, query_grad, *grads
 

time: 90.3 us -> 86.1 us (0.953)
  the two profiles are of different devices: /device:TPU:0 before, /device:TPU:19 now
where the time goes in v4:
time: 86.1 us; the launch traced here: 85.7 us
  waiting for transfers between devices  37.7 us (44%)
  starting transfers between devices  28.4 us (33%)
  Pallas kernels  17.8 us (21%)
  between operations  1.73 us (2%)
    ppermute x14, waiting for transfers between devices, send(): return lax.ppermute(x, ('seq', 'head'), pairs)  36.4 us
    ppermute x14, starting transfers between devices, send(): return lax.ppermute(x, ('seq', 'head'), pairs)  28.3 us
    pallas_call x22, Pallas kernels, call(): pl.pallas_call(kernel, in_specs=[spec(m) for m, _ in ins], out_specs=out_...  17.8 us
  transfers between devices with their start and end apart: 15, of which 9 were waited for; matrix products, arithmetic and copies ran while one was open for 0% of the time, Pallas kernels for 16%

profile of v4, /device:TPU:19, one launch (start us, length us, event | category | flops | bytes accessed | tf_op | source)
XLA Modules:
  0.0 85.7 jit_solution(894517104074728516)
XLA Ops:
  1.3 1.7 %kv0.1 = (bf16[256,1024]{1,0:T(8,128)(2,1)S(1)}, bf16[256,1024]{1,0:T(8,128)(2,1)S(1)}, f32[129,8,128]{2,1,0:T(8,128)S(1)}) custom-call(s32[1]{0:T(128)S(6)} %copy.18.doc_ref, bf16[256,2048]{1,0:T(8,128)(2,1)} %k_hbm.3, bf16[256,2048]{1,0:T(8,128)(2,1)} %v_hbm.3), custom_call_target="tpu_custom_call" | custom-call | flops 67108864 | bytes 4194304 | tf_op jit(solution)/shard_map/kv0/pallas_call | solution.py:371
  3.0 1.3 %collective-permute-start = (f32[129,8,128]{2,1,0:T(8,128)S(1)}, f32[129,8,128]{2,1,0:T(8,128)S(1)}, u32[]{:S(2)}, u32[]{:S(2)}) collective-permute-start(f32[129,8,128]{2,1,0:T(8,128)S(1)} %get-tuple-element.45.after_ref.own_ref), channel_id=1, source_target_pairs={{1,3},{2,0},{5,7},{6,4},{9,11},{10,8},{13,15},{14,12},{17,19},{18,... | collective-permute-start | bytes 1585160 | tf_op jit(solution)/shard_map/ppermute | solution.py:424
  4.3 0.9 %intra0.1.rest_0_.intra_ref = f32[256,1024]{1,0:T(8,128)S(1)} custom-call(bf16[256,2048]{1,0:T(8,128)(2,1)S(1)} %copy-done, bf16[256,1024]{1,0:T(8,128)(2,1)S(1)} %get-tuple-element.43.k_ref, bf16[256,1024]{1,0:T(8,128)(2,1)S(1)} %get-tuple-element.44.v_ref, f32[129,8,128]{2,1,0:T(8,128)S(1)} %get-tuple-element.45.after_ref.own_ref), custom_call_target="tpu_custom_call" | custom-call | flops 268435456 | bytes 4194304 | tf_op jit(solution)/shard_map/intra0/pallas_call | solution.py:371
  5.2 1.6 %kv1.1 = (bf16[256,1024]{1,0:T(8,128)(2,1)S(1)}, bf16[256,1024]{1,0:T(8,128)(2,1)S(1)}, f32[129,8,128]{2,1,0:T(8,128)S(1)}) custom-call(s32[1]{0:T(128)S(6)} %copy.18.doc_ref, bf16[256,2048]{1,0:T(8,128)(2,1)} %k_hbm.3, bf16[256,2048]{1,0:T(8,128)(2,1)} %v_hbm.3, f32[256,1024]{1,0:T(8,128)S(1)} %intra0.1.rest_0_.intra_ref), custom_call_target="tpu_custom_call" | custom-call | flops 67108864 | bytes 4194304 | tf_op jit(solution)/shard_map/kv1/pallas_call | solution.py:371
  6.9 3.2 %collective-permute-start.2 = (f32[129,8,128]{2,1,0:T(8,128)S(1)}, f32[129,8,128]{2,1,0:T(8,128)S(1)}, u32[]{:S(2)}, u32[]{:S(2)}) collective-permute-start(f32[129,8,128]{2,1,0:T(8,128)S(1)} %get-tuple-element.46.after_ref.own_ref), channel_id=1, source_target_pairs={{0,2},{1,5},{2,0},{3,7},{4,6},{5,9},{6,4},{7,11},{8,10},{9,13},{10... | collective-permute-start | bytes 1585160 | tf_op jit(solution)/shard_map/ppermute | solution.py:424
  10.1 2.9 %collective-permute-done.got_ref.rest_0_ = f32[129,8,128]{2,1,0:T(8,128)S(1)} collective-permute-done((f32[129,8,128]{2,1,0:T(8,128)S(1)}, f32[129,8,128]{2,1,0:T(8,128)S(1)}, u32[]{:S(2)}, u32[]{:S(2)}) %collective-permute-start) | collective-permute-done | bytes 528416 | tf_op jit(solution)/shard_map/ppermute | solution.py:424
  13.0 0.1 second00.1.after_ref.sent_ref
  13.0 3.2 %collective-permute-start.1 = (f32[129,8,128]{2,1,0:T(8,128)S(1)}, f32[129,8,128]{2,1,0:T(8,128)S(1)}, u32[]{:S(2)}, u32[]{:S(2)}) collective-permute-start(f32[129,8,128]{2,1,0:T(8,128)S(1)} %second00.1.after_ref.sent_ref), channel_id=1, source_target_pairs={{0,4},{3,7},{4,8},{7,11},{8,12},{11,15},{16,20},{19,23},{20,24},{2... | collective-permute-start | bytes 1585160 | tf_op jit(solution)/shard_map/ppermute | solution.py:424
  16.3 0.9 %collective-permute-done.2.got_ref.rest_0_ = f32[129,8,128]{2,1,0:T(8,128)S(1)} collective-permute-done((f32[129,8,128]{2,1,0:T(8,128)S(1)}, f32[129,8,128]{2,1,0:T(8,128)S(1)}, u32[]{:S(2)}, u32[]{:S(2)}) %collective-permute-start.2) | collective-permute-done | bytes 528416 | tf_op jit(solution)/shard_map/ppermute | solution.py:424
  17.1 0.1 second01.1.after_ref.sent_ref
  17.2 5.0 %collective-permute-start.5 = (f32[129,8,128]{2,1,0:T(8,128)S(1)}, f32[129,8,128]{2,1,0:T(8,128)S(1)}, u32[]{:S(2)}, u32[]{:S(2)}) collective-permute-start(f32[129,8,128]{2,1,0:T(8,128)S(1)} %second01.1.after_ref.sent_ref), channel_id=1, source_target_pairs={{0,4},{1,3},{2,6},{3,5},{4,8},{5,7},{6,10},{7,9},{8,12},{9,11},{10... | collective-permute-start | bytes 1585160 | tf_op jit(solution)/shard_map/ppermute | solution.py:424
  22.3 0.9 %intra1.1.after_ref.intra_ref = f32[256,1024]{1,0:T(8,128)S(1)} custom-call(bf16[256,2048]{1,0:T(8,128)(2,1)S(1)} %copy-done, bf16[256,1024]{1,0:T(8,128)(2,1)S(1)} %get-tuple-element.47.k_ref, bf16[256,1024]{1,0:T(8,128)(2,1)S(1)} %get-tuple-element.48.v_ref, f32[129,8,128]{2,1,0:T(8,128)S(1)} %second01.1.after_ref.sent_ref), custom_call_target="tpu_custom_call" | custom-call | flops 268435456 | bytes 4194304 | tf_op jit(solution)/shard_map/intra1/pallas_call | solution.py:371
  23.2 0.1 third00.1
  23.3 1.9 %collective-permute-start.3 = (f32[129,8,128]{2,1,0:T(8,128)S(1)}, f32[129,8,128]{2,1,0:T(8,128)S(1)}, u32[]{:S(2)}, u32[]{:S(2)}) collective-permute-start(f32[129,8,128]{2,1,0:T(8,128)S(1)} %get-tuple-element.49), channel_id=1, source_target_pairs={{0,4},{3,5},{4,8},{7,9},{8,12},{11,13},{16,20},{19,21},{20,24},{23... | collective-permute-start | bytes 1585160 | tf_op jit(solution)/shard_map/ppermute | solution.py:424
  25.3 0.0 copy-start.1
  25.3 0.0 copy-start.2
  25.3 0.8 collective-permute-start.4
  26.2 6.5 %collective-permute-done.5.got_ref.rest_1_ = f32[129,8,128]{2,1,0:T(8,128)S(1)} collective-permute-done((f32[129,8,128]{2,1,0:T(8,128)S(1)}, f32[129,8,128]{2,1,0:T(8,128)S(1)}, u32[]{:S(2)}, u32[]{:S(2)}) %collective-permute-start.5) | collective-permute-done | bytes 528416 | tf_op jit(solution)/shard_map/ppermute | solution.py:424
  32.7 0.1 third01.1
  32.8 0.7 collective-permute-start.6
  33.5 6.3 %collective-permute-done.3.rest_2_ = f32[129,8,128]{2,1,0:T(8,128)S(1)} collective-permute-done((f32[129,8,128]{2,1,0:T(8,128)S(1)}, f32[129,8,128]{2,1,0:T(8,128)S(1)}, u32[]{:S(2)}, u32[]{:S(2)}) %collective-permute-start.3) | collective-permute-done | bytes 528416 | tf_op jit(solution)/shard_map/ppermute | solution.py:424
  39.7 0.5 attend0.1
  40.2 0.6 attend1.1
  40.8 0.1 collective-permute-start.7
  40.9 1.3 %collective-permute-done.7.other_ref = f32[256,128]{1,0:T(8,128)S(1)} collective-permute-done((f32[256,128]{1,0:T(8,128)S(1)}, f32[256,128]{1,0:T(8,128)S(1)}, u32[]{:S(2)}, u32[]{:S(2)}) %collective-permute-start.7) | collective-permute-done | bytes 131104 | tf_op jit(solution)/shard_map/ppermute | solution.py:505
  42.3 0.7 grad0.1
  43.0 4.6 %collective-permute-start.8 = (f32[129,8,128]{2,1,0:T(8,128)S(1)}, f32[129,8,128]{2,1,0:T(8,128)S(1)}, u32[]{:S(2)}, u32[]{:S(2)}) collective-permute-start(f32[129,8,128]{2,1,0:T(8,128)S(1)} %get-tuple-element.56.rest_0_.own_ref), channel_id=1, source_target_pairs={{15,13},{12,14},{11,9},{8,10},{7,5},{4,6},{3,1},{0,2},{31,29},{28,... | collective-permute-start | bytes 1585160 | tf_op jit(solution)/shard_map/ppermute | solution.py:424
  47.6 1.8 %back0.1 = (bf16[256,2048]{1,0:T(8,128)(2,1)}, f32[256,512]{1,0:T(8,128)S(1)}, f32[256,512]{1,0:T(8,128)S(1)}) custom-call(bf16[256,2048]{1,0:T(8,128)(2,1)S(1)} %copy-done, bf16[256,1024]{1,0:T(8,128)(2,1)S(1)} %get-tuple-element.43.k_ref, bf16[256,1024]{1,0:T(8,128)(2,1)S(1)} %get-tuple-element.44.v_ref, bf16[256,1024]{1,0:T(8,128)(2,1)S(1)} %get-tuple-element.54.ag_ref, ...), custom_call_target="tpu_custom_call" | custom-call | flops 234881024 | bytes 4194304 | tf_op jit(solution)/shard_map/back0/pallas_call | solution.py:371
  49.4 0.7 grad1.1
  50.1 2.1 %collective-permute-start.9 = (f32[129,8,128]{2,1,0:T(8,128)S(1)}, f32[129,8,128]{2,1,0:T(8,128)S(1)}, u32[]{:S(2)}, u32[]{:S(2)}) collective-permute-start(f32[129,8,128]{2,1,0:T(8,128)S(1)} %get-tuple-element.60.after_ref.own_ref), channel_id=1, source_target_pairs={{14,12},{15,11},{12,14},{13,9},{10,8},{11,7},{8,10},{9,5},{6,4},{7... | collective-permute-start | bytes 1585160 | tf_op jit(solution)/shard_map/ppermute | solution.py:424
  52.2 2.3 %collective-permute-done.8.got_ref.rest_0_ = f32[129,8,128]{2,1,0:T(8,128)S(1)} collective-permute-done((f32[129,8,128]{2,1,0:T(8,128)S(1)}, f32[129,8,128]{2,1,0:T(8,128)S(1)}, u32[]{:S(2)}, u32[]{:S(2)}) %collective-permute-start.8) | collective-permute-done | bytes 528416 | tf_op jit(solution)/shard_map/ppermute | solution.py:424
  54.5 0.1 second10.1.rest_0_.sent_ref
  54.6 0.7 collective-permute-start.12
  55.3 1.9 %back1.1 = (bf16[256,2048]{1,0:T(8,128)(2,1)}, bf16[256,2048]{1,0:T(8,128)(2,1)}, f32[256,512]{1,0:T(8,128)S(1)}, f32[256,512]{1,0:T(8,128)S(1)}) custom-call(bf16[256,2048]{1,0:T(8,128)(2,1)S(1)} %copy-done, bf16[256,1024]{1,0:T(8,128)(2,1)S(1)} %get-tuple-element.43.k_ref, ...), custom_call_target="tpu_custom_call", output_to_operand_aliasing={{1}: (6, {})} | custom-call | flops 234881024 | bytes 4194304 | tf_op jit(solution)/shard_map/back1/pallas_call | solution.py:371
  57.2 3.7 %collective-permute-done.9.got_ref.rest_0_ = f32[129,8,128]{2,1,0:T(8,128)S(1)} collective-permute-done((f32[129,8,128]{2,1,0:T(8,128)S(1)}, f32[129,8,128]{2,1,0:T(8,128)S(1)}, u32[]{:S(2)}, u32[]{:S(2)}) %collective-permute-start.9) | collective-permute-done | bytes 528416 | tf_op jit(solution)/shard_map/ppermute | solution.py:424
  60.9 0.1 second11.1.rest_0_.sent_ref
  60.9 1.9 %collective-permute-start.10 = (f32[129,8,128]{2,1,0:T(8,128)S(1)}, f32[129,8,128]{2,1,0:T(8,128)S(1)}, u32[]{:S(2)}, u32[]{:S(2)}) collective-permute-start(f32[129,8,128]{2,1,0:T(8,128)S(1)} %second11.1.rest_0_.sent_ref), channel_id=1, source_target_pairs={{14,10},{15,13},{12,8},{13,11},{10,6},{11,9},{8,4},{9,7},{6,2},{7,... | collective-permute-start | bytes 1585160 | tf_op jit(solution)/shard_map/ppermute | solution.py:424
  62.9 1.8 %back2.1 = (bf16[256,2048]{1,0:T(8,128)(2,1)}, f32[256,512]{1,0:T(8,128)S(1)}, f32[256,512]{1,0:T(8,128)S(1)}) custom-call(bf16[256,2048]{1,0:T(8,128)(2,1)S(1)} %copy-done, bf16[256,1024]{1,0:T(8,128)(2,1)S(1)} %get-tuple-element.47.k_ref, bf16[256,1024]{1,0:T(8,128)(2,1)S(1)} %get-tuple-element.48.v_ref, ...), custom_call_target="tpu_custom_call", output_to_operand_aliasing={{0}: (6, {})} | custom-call | flops 234881024 | bytes 4194304 | tf_op jit(solution)/shard_map/back2/pallas_call | solution.py:371
  64.7 0.1 third10.1
  64.9 1.3 %collective-permute-start.13 = (f32[129,8,128]{2,1,0:T(8,128)S(1)}, f32[129,8,128]{2,1,0:T(8,128)S(1)}, u32[]{:S(2)}, u32[]{:S(2)}) collective-permute-start(f32[129,8,128]{2,1,0:T(8,128)S(1)} %get-tuple-element.76), channel_id=1, source_target_pairs={{14,10},{13,11},{10,6},{9,7},{6,2},{5,3},{30,26},{29,27},{26,22},{... | collective-permute-start | bytes 1585160 | tf_op jit(solution)/shard_map/ppermute | solution.py:424
  66.2 0.9 %collective-permute-start.14 = (f32[129,8,128]{2,1,0:T(8,128)S(1)}, f32[129,8,128]{2,1,0:T(8,128)S(1)}, u32[]{:S(2)}, u32[]{:S(2)}) collective-permute-start(f32[129,8,128]{2,1,0:T(8,128)S(1)} %get-tuple-element.77), channel_id=1, source_target_pairs={{14,12},{10,8},{6,4},{2,0},{30,28},{26,24},{22,20},{18,16}} | collective-permute-start | bytes 1585160 | tf_op jit(solution)/shard_map/ppermute | solution.py:424
  67.0 1.9 %back3.1 = (bf16[256,2048]{1,0:T(8,128)(2,1)}, f32[256,512]{1,0:T(8,128)S(1)}, f32[256,512]{1,0:T(8,128)S(1)}) custom-call(bf16[256,2048]{1,0:T(8,128)(2,1)S(1)} %copy-done, bf16[256,1024]{1,0:T(8,128)(2,1)S(1)} %get-tuple-element.47.k_ref, bf16[256,1024]{1,0:T(8,128)(2,1)S(1)} %get-tuple-element.48.v_ref, ...), custom_call_target="tpu_custom_call", output_to_operand_aliasing={{0}: (6, {})} | custom-call | flops 234881024 | bytes 4194304 | tf_op jit(solution)/shard_map/back3/pallas_call | solution.py:371
  68.9 8.9 %collective-permute-done.10.got_ref.rest_1_ = f32[129,8,128]{2,1,0:T(8,128)S(1)} collective-permute-done((f32[129,8,128]{2,1,0:T(8,128)S(1)}, f32[129,8,128]{2,1,0:T(8,128)S(1)}, u32[]{:S(2)}, u32[]{:S(2)}) %collective-permute-start.10) | collective-permute-done | bytes 528416 | tf_op jit(solution)/shard_map/ppermute | solution.py:424
  77.8 0.1 third11.1
  77.9 0.7 collective-permute-start.11
  78.6 4.9 %collective-permute-done.13.rest_2_ = f32[129,8,128]{2,1,0:T(8,128)S(1)} collective-permute-done((f32[129,8,128]{2,1,0:T(8,128)S(1)}, f32[129,8,128]{2,1,0:T(8,128)S(1)}, u32[]{:S(2)}, u32[]{:S(2)}) %collective-permute-start.13) | collective-permute-done | bytes 528416 | tf_op jit(solution)/shard_map/ppermute | solution.py:424
  83.5 0.6 final0.1
  84.1 1.4 %final1.1 = (bf16[256,2048]{1,0:T(8,128)(2,1)}, bf16[256,2048]{1,0:T(8,128)(2,1)}) custom-call(s32[1]{0:T(128)S(6)} %copy.18.doc_ref, bf16[256,1024]{1,0:T(8,128)(2,1)S(1)} %get-tuple-element.47.k_ref, bf16[256,1024]{1,0:T(8,128)(2,1)S(1)} %get-tuple-element.48.v_ref, f32[256,512]{1,0:T(8,128)S(1)} %get-tuple-element.70.after_ref.kin0, ...), custom_call_target="tpu_custom_call" | custom-call | flops 134217728 | bytes 4194304 | tf_op jit(solution)/shard_map/final1/pallas_call | solution.py:371
  (10 shorter events, 0.0 us)
Async XLA Ops:
  1.3 3.0 %copy-start = (bf16[256,2048]{1,0:T(8,128)(2,1)S(1)}, bf16[256,2048]{1,0:T(8,128)(2,1)}, u32[]{:S(2)}) copy-start(bf16[256,2048]{1,0:T(8,128)(2,1)} %q_ref.19) | copy-start | bytes 3145732
  3.0 10.0 %collective-permute-start = (f32[129,8,128]{2,1,0:T(8,128)S(1)}, f32[129,8,128]{2,1,0:T(8,128)S(1)}, u32[]{:S(2)}, u32[]{:S(2)}) collective-permute-start(f32[129,8,128]{2,1,0:T(8,128)S(1)} %get-tuple-element.45.after_ref.own_ref), channel_id=1, source_target_pairs={{1,3},{2,0},{5,7},{6,4},{9,11},{10,8},{13,15},{14,12},{17,19},{18,... | collective-permute-start | bytes 1585160 | tf_op jit(solution)/shard_map/ppermute | solution.py:424
  6.9 10.3 %collective-permute-start.2 = (f32[129,8,128]{2,1,0:T(8,128)S(1)}, f32[129,8,128]{2,1,0:T(8,128)S(1)}, u32[]{:S(2)}, u32[]{:S(2)}) collective-permute-start(f32[129,8,128]{2,1,0:T(8,128)S(1)} %get-tuple-element.46.after_ref.own_ref), channel_id=1, source_target_pairs={{0,2},{1,5},{2,0},{3,7},{4,6},{5,9},{6,4},{7,11},{8,10},{9,13},{10... | collective-permute-start | bytes 1585160 | tf_op jit(solution)/shard_map/ppermute | solution.py:424
  13.0 10.2 %collective-permute-start.1 = (f32[129,8,128]{2,1,0:T(8,128)S(1)}, f32[129,8,128]{2,1,0:T(8,128)S(1)}, u32[]{:S(2)}, u32[]{:S(2)}) collective-permute-start(f32[129,8,128]{2,1,0:T(8,128)S(1)} %second00.1.after_ref.sent_ref), channel_id=1, source_target_pairs={{0,4},{3,7},{4,8},{7,11},{8,12},{11,15},{16,20},{19,23},{20,24},{2... | collective-permute-start | bytes 1585160 | tf_op jit(solution)/shard_map/ppermute | solution.py:424
  17.2 15.5 %collective-permute-start.5 = (f32[129,8,128]{2,1,0:T(8,128)S(1)}, f32[129,8,128]{2,1,0:T(8,128)S(1)}, u32[]{:S(2)}, u32[]{:S(2)}) collective-permute-start(f32[129,8,128]{2,1,0:T(8,128)S(1)} %second01.1.after_ref.sent_ref), channel_id=1, source_target_pairs={{0,4},{1,3},{2,6},{3,5},{4,8},{5,7},{6,10},{7,9},{8,12},{9,11},{10... | collective-permute-start | bytes 1585160 | tf_op jit(solution)/shard_map/ppermute | solution.py:424
  23.3 16.4 %collective-permute-start.3 = (f32[129,8,128]{2,1,0:T(8,128)S(1)}, f32[129,8,128]{2,1,0:T(8,128)S(1)}, u32[]{:S(2)}, u32[]{:S(2)}) collective-permute-start(f32[129,8,128]{2,1,0:T(8,128)S(1)} %get-tuple-element.49), channel_id=1, source_target_pairs={{0,4},{3,5},{4,8},{7,9},{8,12},{11,13},{16,20},{19,21},{20,24},{23... | collective-permute-start | bytes 1585160 | tf_op jit(solution)/shard_map/ppermute | solution.py:424
  25.3 14.4 %copy-start.1 = (bf16[256,2048]{1,0:T(8,128)(2,1)S(1)}, bf16[256,2048]{1,0:T(8,128)(2,1)}, u32[]{:S(2)}) copy-start(bf16[256,2048]{1,0:T(8,128)(2,1)} %do_ref.7) | copy-start | bytes 3145732
  25.3 14.4 %copy-start.2 = (f32[2048]{0:T(1024)S(1)}, f32[2048]{0:T(1024)}, u32[]{:S(2)}) copy-start(f32[2048]{0:T(1024)} %param.10) | copy-start | bytes 24580
  25.3 14.4 %collective-permute-start.4 = (f32[129,8,128]{2,1,0:T(8,128)S(1)}, f32[129,8,128]{2,1,0:T(8,128)S(1)}, u32[]{:S(2)}, u32[]{:S(2)}) collective-permute-start(f32[129,8,128]{2,1,0:T(8,128)S(1)} %get-tuple-element.50), channel_id=1, source_target_pairs={{0,2},{4,6},{8,10},{12,14},{16,18},{20,22},{24,26},{28,30}} | collective-permute-start | bytes 1585160 | tf_op jit(solution)/shard_map/ppermute | solution.py:424
  32.8 7.5 %collective-permute-start.6 = (f32[129,8,128]{2,1,0:T(8,128)S(1)}, f32[129,8,128]{2,1,0:T(8,128)S(1)}, u32[]{:S(2)}, u32[]{:S(2)}) collective-permute-start(f32[129,8,128]{2,1,0:T(8,128)S(1)} %third01.1), channel_id=1, source_target_pairs={{0,4},{4,8},{8,12},{16,20},{20,24},{24,28}} | collective-permute-start | bytes 1585160 | tf_op jit(solution)/shard_map/ppermute | solution.py:424
  40.8 1.4 %collective-permute-start.7 = (f32[256,128]{1,0:T(8,128)S(1)}, f32[256,128]{1,0:T(8,128)S(1)}, u32[]{:S(2)}, u32[]{:S(2)}) collective-permute-start(f32[256,128]{1,0:T(8,128)S(1)} %get-tuple-element.53.mine_ref), channel_id=1, source_target_pairs={{0,1},{1,0},{2,3},{3,2},{4,5},{5,4},{6,7},{7,6},{8,9},{9,8},{10,11... | collective-permute-start | bytes 393224 | tf_op jit(solution)/shard_map/ppermute | solution.py:505
  43.0 11.6 %collective-permute-start.8 = (f32[129,8,128]{2,1,0:T(8,128)S(1)}, f32[129,8,128]{2,1,0:T(8,128)S(1)}, u32[]{:S(2)}, u32[]{:S(2)}) collective-permute-start(f32[129,8,128]{2,1,0:T(8,128)S(1)} %get-tuple-element.56.rest_0_.own_ref), channel_id=1, source_target_pairs={{15,13},{12,14},{11,9},{8,10},{7,5},{4,6},{3,1},{0,2},{31,29},{28,... | collective-permute-start | bytes 1585160 | tf_op jit(solution)/shard_map/ppermute | solution.py:424
  50.1 10.7 %collective-permute-start.9 = (f32[129,8,128]{2,1,0:T(8,128)S(1)}, f32[129,8,128]{2,1,0:T(8,128)S(1)}, u32[]{:S(2)}, u32[]{:S(2)}) collective-permute-start(f32[129,8,128]{2,1,0:T(8,128)S(1)} %get-tuple-element.60.after_ref.own_ref), channel_id=1, source_target_pairs={{14,12},{15,11},{12,14},{13,9},{10,8},{11,7},{8,10},{9,5},{6,4},{7... | collective-permute-start | bytes 1585160 | tf_op jit(solution)/shard_map/ppermute | solution.py:424
  54.6 10.1 %collective-permute-start.12 = (f32[129,8,128]{2,1,0:T(8,128)S(1)}, f32[129,8,128]{2,1,0:T(8,128)S(1)}, u32[]{:S(2)}, u32[]{:S(2)}) collective-permute-start(f32[129,8,128]{2,1,0:T(8,128)S(1)} %second10.1.rest_0_.sent_ref), channel_id=1, source_target_pairs={{14,10},{13,9},{10,6},{9,5},{6,2},{5,1},{30,26},{29,25},{26,22},{2... | collective-permute-start | bytes 1585160 | tf_op jit(solution)/shard_map/ppermute | solution.py:424
  60.9 16.9 %collective-permute-start.10 = (f32[129,8,128]{2,1,0:T(8,128)S(1)}, f32[129,8,128]{2,1,0:T(8,128)S(1)}, u32[]{:S(2)}, u32[]{:S(2)}) collective-permute-start(f32[129,8,128]{2,1,0:T(8,128)S(1)} %second11.1.rest_0_.sent_ref), channel_id=1, source_target_pairs={{14,10},{15,13},{12,8},{13,11},{10,6},{11,9},{8,4},{9,7},{6,2},{7,... | collective-permute-start | bytes 1585160 | tf_op jit(solution)/shard_map/ppermute | solution.py:424
  64.9 18.6 %collective-permute-start.13 = (f32[129,8,128]{2,1,0:T(8,128)S(1)}, f32[129,8,128]{2,1,0:T(8,128)S(1)}, u32[]{:S(2)}, u32[]{:S(2)}) collective-permute-start(f32[129,8,128]{2,1,0:T(8,128)S(1)} %get-tuple-element.76), channel_id=1, source_target_pairs={{14,10},{13,11},{10,6},{9,7},{6,2},{5,3},{30,26},{29,27},{26,22},{... | collective-permute-start | bytes 1585160 | tf_op jit(solution)/shard_map/ppermute | solution.py:424
  66.2 17.3 %collective-permute-start.14 = (f32[129,8,128]{2,1,0:T(8,128)S(1)}, f32[129,8,128]{2,1,0:T(8,128)S(1)}, u32[]{:S(2)}, u32[]{:S(2)}) collective-permute-start(f32[129,8,128]{2,1,0:T(8,128)S(1)} %get-tuple-element.77), channel_id=1, source_target_pairs={{14,12},{10,8},{6,4},{2,0},{30,28},{26,24},{22,20},{18,16}} | collective-permute-start | bytes 1585160 | tf_op jit(solution)/shard_map/ppermute | solution.py:424
  77.9 6.2 %collective-permute-start.11 = (f32[129,8,128]{2,1,0:T(8,128)S(1)}, f32[129,8,128]{2,1,0:T(8,128)S(1)}, u32[]{:S(2)}, u32[]{:S(2)}) collective-permute-start(f32[129,8,128]{2,1,0:T(8,128)S(1)} %third11.1), channel_id=1, source_target_pairs={{14,10},{10,6},{6,2},{30,26},{26,22},{22,18}} | collective-permute-start | bytes 1585160 | tf_op jit(solution)/shard_map/ppermute | solution.py:424

commit v5 on v4

--- a/solution.py
+++ b/solution.py
@@ -114,7 +114,7 @@
 
 
 HALVES = 2
-CHUNKS = 2
+CHUNKS = 1
 VMEM_LIMIT = 16 * 1024 * 1024
 
 
@@ -275,8 +275,10 @@
         ag = ag_ref[:, cols(j)]
         gw = jnp.where(mask, nt(ag, v), 0.0).astype(BF)
         qg_ref[:, cols(i)] = (nn(gw, k) + nt(ag, state_ref[j])).astype(BF)
-        copies.append(pltpu.make_async_copy(qg_ref.at[:, cols(i)], qg_hbm.at[:, at], qg_sems.at[i]))
-        copies[-1].start()
+        if i == count - 1:
+            there = slice(c * count * HEAD_DIM, (c + 1) * count * HEAD_DIM)
+            copies.append(pltpu.make_async_copy(qg_ref, qg_hbm.at[:, there], qg_sems.at[0]))
+            copies[-1].start()
         gw_t = jnp.where(mask_t, nt(v, ag), 0.0).astype(BF)
         kin_ref[:, cols(i)] = nn(gw_t, q)
         att_t = jnp.where(mask_t, nt(k, q), 0.0).astype(BF)
@@ -306,9 +308,9 @@
         grads = gathered(j, gates, messages)
         kg_ref[:, cols(j)] = (kin_ref[:, within] + nt(v_ref[:, cols(j)], grads)).astype(BF)
         vg_ref[:, cols(j)] = (vin_ref[:, within] + nn(k_ref[:, cols(j)], grads)).astype(BF)
-        if n and j % 2:
-            here = slice((j - 1) * HEAD_DIM, (j + 1) * HEAD_DIM)
-            there = slice(half + (j - 1) * HEAD_DIM, half + (j + 1) * HEAD_DIM)
+        if n and (j + 1) % count == 0:
+            here = slice((j + 1 - count) * HEAD_DIM, (j + 1) * HEAD_DIM)
+            there = slice(half + here.start, half + here.stop)
             for ref, hbm in ((kg_ref, kg_hbm), (vg_ref, vg_hbm)):
                 copies.append(pltpu.make_async_copy(ref.at[:, here], hbm.at[:, there], sems.at[len(copies)]))
                 copies[-1].start()
@@ -540,8 +542,8 @@
     got2b = send(on1, way1[1])
     query_grad, kin2, vin2 = back(2, query_grad, on1)
     more0 = later(0, 1, way0, bg[0], on0, got2a, kin2)
-    query_grad, kin3, vin3 = back(3, query_grad, on1)
-    more1 = later(1, 1, way1, bg[1], on1, got2b, kin3)
+    more1 = later(1, 1, way1, bg[1], on1, got2b, on1)
+    query_grad, kin3, vin3 = back(3, query_grad, got2b)
     got = [(got1[0], got2a, *more0), (got1[1], got2b, *more1)]
     inside = [(kin0, kin1, vin0, vin1), (kin2, kin3, vin2, vin3)]
     grads = []

time: 86.1 us -> 85.9 us (level)
  no operation moved by 1% of the time
where the time goes in v5:
time: 85.9 us; the launch traced here: 85.5 us
  waiting for transfers between devices  37.5 us (44%)
  starting transfers between devices  28.3 us (33%)
  Pallas kernels  18.2 us (21%)
  between operations  1.57 us (2%)
    ppermute x14, waiting for transfers between devices, send(): return lax.ppermute(x, ('seq', 'head'), pairs)  36.1 us
    ppermute x14, starting transfers between devices, send(): return lax.ppermute(x, ('seq', 'head'), pairs)  28.2 us
    pallas_call x22, Pallas kernels, call(): pl.pallas_call(kernel, in_specs=[spec(m) for m, _ in ins], out_specs=out_...  18.2 us
  transfers between devices with their start and end apart: 15, of which 9 were waited for; matrix products, arithmetic and copies ran while one was open for 0% of the time, Pallas kernels for 16%

profile of v5, /device:TPU:19, one launch (start us, length us, event | category | flops | bytes accessed | tf_op | source)
XLA Modules:
  0.0 85.5 jit_solution(455684250533091173)
XLA Ops:
  1.3 1.7 %kv0.1 = (bf16[256,1024]{1,0:T(8,128)(2,1)S(1)}, bf16[256,1024]{1,0:T(8,128)(2,1)S(1)}, f32[129,8,128]{2,1,0:T(8,128)S(1)}) custom-call(s32[1]{0:T(128)S(6)} %copy.18.doc_ref, bf16[256,2048]{1,0:T(8,128)(2,1)} %k_hbm.3, bf16[256,2048]{1,0:T(8,128)(2,1)} %v_hbm.3), custom_call_target="tpu_custom_call" | custom-call | flops 67108864 | bytes 4194304 | tf_op jit(solution)/shard_map/kv0/pallas_call | solution.py:373
  3.0 1.3 %collective-permute-start = (f32[129,8,128]{2,1,0:T(8,128)S(1)}, f32[129,8,128]{2,1,0:T(8,128)S(1)}, u32[]{:S(2)}, u32[]{:S(2)}) collective-permute-start(f32[129,8,128]{2,1,0:T(8,128)S(1)} %get-tuple-element.45.after_ref.own_ref), channel_id=1, source_target_pairs={{1,3},{2,0},{5,7},{6,4},{9,11},{10,8},{13,15},{14,12},{17,19},{18,... | collective-permute-start | bytes 1585160 | tf_op jit(solution)/shard_map/ppermute | solution.py:426
  4.3 0.9 %intra0.1.rest_0_.intra_ref = f32[256,1024]{1,0:T(8,128)S(1)} custom-call(bf16[256,2048]{1,0:T(8,128)(2,1)S(1)} %copy-done, bf16[256,1024]{1,0:T(8,128)(2,1)S(1)} %get-tuple-element.43.k_ref, bf16[256,1024]{1,0:T(8,128)(2,1)S(1)} %get-tuple-element.44.v_ref, f32[129,8,128]{2,1,0:T(8,128)S(1)} %get-tuple-element.45.after_ref.own_ref), custom_call_target="tpu_custom_call" | custom-call | flops 268435456 | bytes 4194304 | tf_op jit(solution)/shard_map/intra0/pallas_call | solution.py:373
  5.2 1.6 %kv1.1 = (bf16[256,1024]{1,0:T(8,128)(2,1)S(1)}, bf16[256,1024]{1,0:T(8,128)(2,1)S(1)}, f32[129,8,128]{2,1,0:T(8,128)S(1)}) custom-call(s32[1]{0:T(128)S(6)} %copy.18.doc_ref, bf16[256,2048]{1,0:T(8,128)(2,1)} %k_hbm.3, bf16[256,2048]{1,0:T(8,128)(2,1)} %v_hbm.3, f32[256,1024]{1,0:T(8,128)S(1)} %intra0.1.rest_0_.intra_ref), custom_call_target="tpu_custom_call" | custom-call | flops 67108864 | bytes 4194304 | tf_op jit(solution)/shard_map/kv1/pallas_call | solution.py:373
  6.8 3.2 %collective-permute-start.2 = (f32[129,8,128]{2,1,0:T(8,128)S(1)}, f32[129,8,128]{2,1,0:T(8,128)S(1)}, u32[]{:S(2)}, u32[]{:S(2)}) collective-permute-start(f32[129,8,128]{2,1,0:T(8,128)S(1)} %get-tuple-element.46.after_ref.own_ref), channel_id=1, source_target_pairs={{0,2},{1,5},{2,0},{3,7},{4,6},{5,9},{6,4},{7,11},{8,10},{9,13},{10... | collective-permute-start | bytes 1585160 | tf_op jit(solution)/shard_map/ppermute | solution.py:426
  10.0 2.9 %collective-permute-done.got_ref.rest_0_ = f32[129,8,128]{2,1,0:T(8,128)S(1)} collective-permute-done((f32[129,8,128]{2,1,0:T(8,128)S(1)}, f32[129,8,128]{2,1,0:T(8,128)S(1)}, u32[]{:S(2)}, u32[]{:S(2)}) %collective-permute-start) | collective-permute-done | bytes 528416 | tf_op jit(solution)/shard_map/ppermute | solution.py:426
  12.9 0.1 second00.1.after_ref.sent_ref
  13.0 3.2 %collective-permute-start.1 = (f32[129,8,128]{2,1,0:T(8,128)S(1)}, f32[129,8,128]{2,1,0:T(8,128)S(1)}, u32[]{:S(2)}, u32[]{:S(2)}) collective-permute-start(f32[129,8,128]{2,1,0:T(8,128)S(1)} %second00.1.after_ref.sent_ref), channel_id=1, source_target_pairs={{0,4},{3,7},{4,8},{7,11},{8,12},{11,15},{16,20},{19,23},{20,24},{2... | collective-permute-start | bytes 1585160 | tf_op jit(solution)/shard_map/ppermute | solution.py:426
  16.2 0.8 collective-permute-done.2.got_ref.rest_0_
  17.1 0.1 second01.1.after_ref.sent_ref
  17.1 5.0 %collective-permute-start.5 = (f32[129,8,128]{2,1,0:T(8,128)S(1)}, f32[129,8,128]{2,1,0:T(8,128)S(1)}, u32[]{:S(2)}, u32[]{:S(2)}) collective-permute-start(f32[129,8,128]{2,1,0:T(8,128)S(1)} %second01.1.after_ref.sent_ref), channel_id=1, source_target_pairs={{0,4},{1,3},{2,6},{3,5},{4,8},{5,7},{6,10},{7,9},{8,12},{9,11},{10... | collective-permute-start | bytes 1585160 | tf_op jit(solution)/shard_map/ppermute | solution.py:426
  22.2 0.9 %intra1.1.after_ref.intra_ref = f32[256,1024]{1,0:T(8,128)S(1)} custom-call(bf16[256,2048]{1,0:T(8,128)(2,1)S(1)} %copy-done, bf16[256,1024]{1,0:T(8,128)(2,1)S(1)} %get-tuple-element.47.k_ref, bf16[256,1024]{1,0:T(8,128)(2,1)S(1)} %get-tuple-element.48.v_ref, f32[129,8,128]{2,1,0:T(8,128)S(1)} %second01.1.after_ref.sent_ref), custom_call_target="tpu_custom_call" | custom-call | flops 268435456 | bytes 4194304 | tf_op jit(solution)/shard_map/intra1/pallas_call | solution.py:373
  23.1 0.1 third00.1
  23.3 1.9 %collective-permute-start.3 = (f32[129,8,128]{2,1,0:T(8,128)S(1)}, f32[129,8,128]{2,1,0:T(8,128)S(1)}, u32[]{:S(2)}, u32[]{:S(2)}) collective-permute-start(f32[129,8,128]{2,1,0:T(8,128)S(1)} %get-tuple-element.49), channel_id=1, source_target_pairs={{0,4},{3,5},{4,8},{7,9},{8,12},{11,13},{16,20},{19,21},{20,24},{23... | collective-permute-start | bytes 1585160 | tf_op jit(solution)/shard_map/ppermute | solution.py:426
  25.2 0.0 copy-start.1
  25.2 0.0 copy-start.2
  25.2 0.8 collective-permute-start.4
  26.1 6.5 %collective-permute-done.5.got_ref.rest_1_ = f32[129,8,128]{2,1,0:T(8,128)S(1)} collective-permute-done((f32[129,8,128]{2,1,0:T(8,128)S(1)}, f32[129,8,128]{2,1,0:T(8,128)S(1)}, u32[]{:S(2)}, u32[]{:S(2)}) %collective-permute-start.5) | collective-permute-done | bytes 528416 | tf_op jit(solution)/shard_map/ppermute | solution.py:426
  32.6 0.1 third01.1
  32.7 0.7 collective-permute-start.6
  33.4 6.3 %collective-permute-done.3.rest_2_ = f32[129,8,128]{2,1,0:T(8,128)S(1)} collective-permute-done((f32[129,8,128]{2,1,0:T(8,128)S(1)}, f32[129,8,128]{2,1,0:T(8,128)S(1)}, u32[]{:S(2)}, u32[]{:S(2)}) %collective-permute-start.3) | collective-permute-done | bytes 528416 | tf_op jit(solution)/shard_map/ppermute | solution.py:426
  39.7 0.5 attend0.1
  40.1 0.6 attend1.1
  40.7 0.1 collective-permute-start.7
  40.8 1.3 %collective-permute-done.7.other_ref = f32[256,128]{1,0:T(8,128)S(1)} collective-permute-done((f32[256,128]{1,0:T(8,128)S(1)}, f32[256,128]{1,0:T(8,128)S(1)}, u32[]{:S(2)}, u32[]{:S(2)}) %collective-permute-start.7) | collective-permute-done | bytes 131104 | tf_op jit(solution)/shard_map/ppermute | solution.py:507
  42.2 0.7 grad0.1
  42.9 4.6 %collective-permute-start.8 = (f32[129,8,128]{2,1,0:T(8,128)S(1)}, f32[129,8,128]{2,1,0:T(8,128)S(1)}, u32[]{:S(2)}, u32[]{:S(2)}) collective-permute-start(f32[129,8,128]{2,1,0:T(8,128)S(1)} %get-tuple-element.56.rest_0_.own_ref), channel_id=1, source_target_pairs={{15,13},{12,14},{11,9},{8,10},{7,5},{4,6},{3,1},{0,2},{31,29},{28,... | collective-permute-start | bytes 1585160 | tf_op jit(solution)/shard_map/ppermute | solution.py:426
  47.5 1.9 %back0.1 = (bf16[256,2048]{1,0:T(8,128)(2,1)}, f32[256,512]{1,0:T(8,128)S(1)}, f32[256,512]{1,0:T(8,128)S(1)}) custom-call(bf16[256,2048]{1,0:T(8,128)(2,1)S(1)} %copy-done, bf16[256,1024]{1,0:T(8,128)(2,1)S(1)} %get-tuple-element.43.k_ref, bf16[256,1024]{1,0:T(8,128)(2,1)S(1)} %get-tuple-element.44.v_ref, bf16[256,1024]{1,0:T(8,128)(2,1)S(1)} %get-tuple-element.54.ag_ref, ...), custom_call_target="tpu_custom_call" | custom-call | flops 234881024 | bytes 4194304 | tf_op jit(solution)/shard_map/back0/pallas_call | solution.py:373
  49.4 0.7 grad1.1
  50.2 2.1 %collective-permute-start.9 = (f32[129,8,128]{2,1,0:T(8,128)S(1)}, f32[129,8,128]{2,1,0:T(8,128)S(1)}, u32[]{:S(2)}, u32[]{:S(2)}) collective-permute-start(f32[129,8,128]{2,1,0:T(8,128)S(1)} %get-tuple-element.60.after_ref.own_ref), channel_id=1, source_target_pairs={{14,12},{15,11},{12,14},{13,9},{10,8},{11,7},{8,10},{9,5},{6,4},{7... | collective-permute-start | bytes 1585160 | tf_op jit(solution)/shard_map/ppermute | solution.py:426
  52.2 2.2 %collective-permute-done.8.got_ref.rest_0_ = f32[129,8,128]{2,1,0:T(8,128)S(1)} collective-permute-done((f32[129,8,128]{2,1,0:T(8,128)S(1)}, f32[129,8,128]{2,1,0:T(8,128)S(1)}, u32[]{:S(2)}, u32[]{:S(2)}) %collective-permute-start.8) | collective-permute-done | bytes 528416 | tf_op jit(solution)/shard_map/ppermute | solution.py:426
  54.4 0.1 second10.1.rest_0_.sent_ref
  54.5 0.7 collective-permute-start.12
  55.2 2.0 %back1.1 = (bf16[256,2048]{1,0:T(8,128)(2,1)}, bf16[256,2048]{1,0:T(8,128)(2,1)}, f32[256,512]{1,0:T(8,128)S(1)}, f32[256,512]{1,0:T(8,128)S(1)}) custom-call(bf16[256,2048]{1,0:T(8,128)(2,1)S(1)} %copy-done, bf16[256,1024]{1,0:T(8,128)(2,1)S(1)} %get-tuple-element.43.k_ref, ...), custom_call_target="tpu_custom_call", output_to_operand_aliasing={{1}: (6, {})} | custom-call | flops 234881024 | bytes 4194304 | tf_op jit(solution)/shard_map/back1/pallas_call | solution.py:373
  57.2 3.7 %collective-permute-done.9.got_ref.rest_0_ = f32[129,8,128]{2,1,0:T(8,128)S(1)} collective-permute-done((f32[129,8,128]{2,1,0:T(8,128)S(1)}, f32[129,8,128]{2,1,0:T(8,128)S(1)}, u32[]{:S(2)}, u32[]{:S(2)}) %collective-permute-start.9) | collective-permute-done | bytes 528416 | tf_op jit(solution)/shard_map/ppermute | solution.py:426
  60.9 0.1 second11.1.rest_0_.sent_ref.after_ref
  61.0 1.9 %collective-permute-start.10 = (f32[129,8,128]{2,1,0:T(8,128)S(1)}, f32[129,8,128]{2,1,0:T(8,128)S(1)}, u32[]{:S(2)}, u32[]{:S(2)}) collective-permute-start(f32[129,8,128]{2,1,0:T(8,128)S(1)} %second11.1.rest_0_.sent_ref.after_ref), channel_id=1, source_target_pairs={{14,10},{15,13},{12,8},{13,11},{10,6},{11,9},{8,4},{9,7},{6,2},{7,... | collective-permute-start | bytes 1585160 | tf_op jit(solution)/shard_map/ppermute | solution.py:426
  63.0 1.9 %back2.1 = (bf16[256,2048]{1,0:T(8,128)(2,1)}, f32[256,512]{1,0:T(8,128)S(1)}, f32[256,512]{1,0:T(8,128)S(1)}) custom-call(bf16[256,2048]{1,0:T(8,128)(2,1)S(1)} %copy-done, bf16[256,1024]{1,0:T(8,128)(2,1)S(1)} %get-tuple-element.47.k_ref, bf16[256,1024]{1,0:T(8,128)(2,1)S(1)} %get-tuple-element.48.v_ref, ...), custom_call_target="tpu_custom_call", output_to_operand_aliasing={{0}: (6, {})} | custom-call | flops 234881024 | bytes 4194304 | tf_op jit(solution)/shard_map/back2/pallas_call | solution.py:373
  64.9 0.1 third10.1
  65.0 1.3 %collective-permute-start.13 = (f32[129,8,128]{2,1,0:T(8,128)S(1)}, f32[129,8,128]{2,1,0:T(8,128)S(1)}, u32[]{:S(2)}, u32[]{:S(2)}) collective-permute-start(f32[129,8,128]{2,1,0:T(8,128)S(1)} %get-tuple-element.76), channel_id=1, source_target_pairs={{14,10},{13,11},{10,6},{9,7},{6,2},{5,3},{30,26},{29,27},{26,22},{... | collective-permute-start | bytes 1585160 | tf_op jit(solution)/shard_map/ppermute | solution.py:426
  66.3 0.7 collective-permute-start.14
  67.0 10.6 %collective-permute-done.10.rest_0_.got_ref.rest_1_ = f32[129,8,128]{2,1,0:T(8,128)S(1)} collective-permute-done((f32[129,8,128]{2,1,0:T(8,128)S(1)}, f32[129,8,128]{2,1,0:T(8,128)S(1)}, u32[]{:S(2)}, u32[]{:S(2)}) %collective-permute-start.10) | collective-permute-done | bytes 528416 | tf_op jit(solution)/shard_map/ppermute | solution.py:426
  77.6 0.1 third11.1
  77.6 0.7 collective-permute-start.11
  78.3 1.9 %back3.1 = (bf16[256,2048]{1,0:T(8,128)(2,1)}, f32[256,512]{1,0:T(8,128)S(1)}, f32[256,512]{1,0:T(8,128)S(1)}) custom-call(bf16[256,2048]{1,0:T(8,128)(2,1)S(1)} %copy-done, bf16[256,1024]{1,0:T(8,128)(2,1)S(1)} %get-tuple-element.47.k_ref, bf16[256,1024]{1,0:T(8,128)(2,1)S(1)} %get-tuple-element.48.v_ref, ...), custom_call_target="tpu_custom_call", output_to_operand_aliasing={{0}: (6, {})} | custom-call | flops 234881024 | bytes 4194304 | tf_op jit(solution)/shard_map/back3/pallas_call | solution.py:373
  80.3 3.1 %collective-permute-done.13.rest_2_ = f32[129,8,128]{2,1,0:T(8,128)S(1)} collective-permute-done((f32[129,8,128]{2,1,0:T(8,128)S(1)}, f32[129,8,128]{2,1,0:T(8,128)S(1)}, u32[]{:S(2)}, u32[]{:S(2)}) %collective-permute-start.13) | collective-permute-done | bytes 528416 | tf_op jit(solution)/shard_map/ppermute | solution.py:426
  83.4 0.6 final0.1
  84.0 1.4 %final1.1 = (bf16[256,2048]{1,0:T(8,128)(2,1)}, bf16[256,2048]{1,0:T(8,128)(2,1)}) custom-call(s32[1]{0:T(128)S(6)} %copy.18.doc_ref, bf16[256,1024]{1,0:T(8,128)(2,1)S(1)} %get-tuple-element.47.k_ref, bf16[256,1024]{1,0:T(8,128)(2,1)S(1)} %get-tuple-element.48.v_ref, f32[256,512]{1,0:T(8,128)S(1)} %get-tuple-element.70.after_ref.kin0, ...), custom_call_target="tpu_custom_call" | custom-call | flops 134217728 | bytes 4194304 | tf_op jit(solution)/shard_map/final1/pallas_call | solution.py:373
  (10 shorter events, 0.0 us)
Async XLA Ops:
  1.3 3.0 %copy-start = (bf16[256,2048]{1,0:T(8,128)(2,1)S(1)}, bf16[256,2048]{1,0:T(8,128)(2,1)}, u32[]{:S(2)}) copy-start(bf16[256,2048]{1,0:T(8,128)(2,1)} %q_ref.19) | copy-start | bytes 3145732
  3.0 10.0 %collective-permute-start = (f32[129,8,128]{2,1,0:T(8,128)S(1)}, f32[129,8,128]{2,1,0:T(8,128)S(1)}, u32[]{:S(2)}, u32[]{:S(2)}) collective-permute-start(f32[129,8,128]{2,1,0:T(8,128)S(1)} %get-tuple-element.45.after_ref.own_ref), channel_id=1, source_target_pairs={{1,3},{2,0},{5,7},{6,4},{9,11},{10,8},{13,15},{14,12},{17,19},{18,... | collective-permute-start | bytes 1585160 | tf_op jit(solution)/shard_map/ppermute | solution.py:426
  6.8 10.3 %collective-permute-start.2 = (f32[129,8,128]{2,1,0:T(8,128)S(1)}, f32[129,8,128]{2,1,0:T(8,128)S(1)}, u32[]{:S(2)}, u32[]{:S(2)}) collective-permute-start(f32[129,8,128]{2,1,0:T(8,128)S(1)} %get-tuple-element.46.after_ref.own_ref), channel_id=1, source_target_pairs={{0,2},{1,5},{2,0},{3,7},{4,6},{5,9},{6,4},{7,11},{8,10},{9,13},{10... | collective-permute-start | bytes 1585160 | tf_op jit(solution)/shard_map/ppermute | solution.py:426
  13.0 10.1 %collective-permute-start.1 = (f32[129,8,128]{2,1,0:T(8,128)S(1)}, f32[129,8,128]{2,1,0:T(8,128)S(1)}, u32[]{:S(2)}, u32[]{:S(2)}) collective-permute-start(f32[129,8,128]{2,1,0:T(8,128)S(1)} %second00.1.after_ref.sent_ref), channel_id=1, source_target_pairs={{0,4},{3,7},{4,8},{7,11},{8,12},{11,15},{16,20},{19,23},{20,24},{2... | collective-permute-start | bytes 1585160 | tf_op jit(solution)/shard_map/ppermute | solution.py:426
  17.1 15.5 %collective-permute-start.5 = (f32[129,8,128]{2,1,0:T(8,128)S(1)}, f32[129,8,128]{2,1,0:T(8,128)S(1)}, u32[]{:S(2)}, u32[]{:S(2)}) collective-permute-start(f32[129,8,128]{2,1,0:T(8,128)S(1)} %second01.1.after_ref.sent_ref), channel_id=1, source_target_pairs={{0,4},{1,3},{2,6},{3,5},{4,8},{5,7},{6,10},{7,9},{8,12},{9,11},{10... | collective-permute-start | bytes 1585160 | tf_op jit(solution)/shard_map/ppermute | solution.py:426
  23.3 16.4 %collective-permute-start.3 = (f32[129,8,128]{2,1,0:T(8,128)S(1)}, f32[129,8,128]{2,1,0:T(8,128)S(1)}, u32[]{:S(2)}, u32[]{:S(2)}) collective-permute-start(f32[129,8,128]{2,1,0:T(8,128)S(1)} %get-tuple-element.49), channel_id=1, source_target_pairs={{0,4},{3,5},{4,8},{7,9},{8,12},{11,13},{16,20},{19,21},{20,24},{23... | collective-permute-start | bytes 1585160 | tf_op jit(solution)/shard_map/ppermute | solution.py:426
  25.2 14.4 %copy-start.1 = (bf16[256,2048]{1,0:T(8,128)(2,1)S(1)}, bf16[256,2048]{1,0:T(8,128)(2,1)}, u32[]{:S(2)}) copy-start(bf16[256,2048]{1,0:T(8,128)(2,1)} %do_ref.7) | copy-start | bytes 3145732
  25.2 14.4 %copy-start.2 = (f32[2048]{0:T(1024)S(1)}, f32[2048]{0:T(1024)}, u32[]{:S(2)}) copy-start(f32[2048]{0:T(1024)} %param.10) | copy-start | bytes 24580
  25.2 14.4 %collective-permute-start.4 = (f32[129,8,128]{2,1,0:T(8,128)S(1)}, f32[129,8,128]{2,1,0:T(8,128)S(1)}, u32[]{:S(2)}, u32[]{:S(2)}) collective-permute-start(f32[129,8,128]{2,1,0:T(8,128)S(1)} %get-tuple-element.50), channel_id=1, source_target_pairs={{0,2},{4,6},{8,10},{12,14},{16,18},{20,22},{24,26},{28,30}} | collective-permute-start | bytes 1585160 | tf_op jit(solution)/shard_map/ppermute | solution.py:426
  32.7 7.5 %collective-permute-start.6 = (f32[129,8,128]{2,1,0:T(8,128)S(1)}, f32[129,8,128]{2,1,0:T(8,128)S(1)}, u32[]{:S(2)}, u32[]{:S(2)}) collective-permute-start(f32[129,8,128]{2,1,0:T(8,128)S(1)} %third01.1), channel_id=1, source_target_pairs={{0,4},{4,8},{8,12},{16,20},{20,24},{24,28}} | collective-permute-start | bytes 1585160 | tf_op jit(solution)/shard_map/ppermute | solution.py:426
  40.7 1.4 %collective-permute-start.7 = (f32[256,128]{1,0:T(8,128)S(1)}, f32[256,128]{1,0:T(8,128)S(1)}, u32[]{:S(2)}, u32[]{:S(2)}) collective-permute-start(f32[256,128]{1,0:T(8,128)S(1)} %get-tuple-element.53.mine_ref), channel_id=1, source_target_pairs={{0,1},{1,0},{2,3},{3,2},{4,5},{5,4},{6,7},{7,6},{8,9},{9,8},{10,11... | collective-permute-start | bytes 393224 | tf_op jit(solution)/shard_map/ppermute | solution.py:507
  42.9 11.5 %collective-permute-start.8 = (f32[129,8,128]{2,1,0:T(8,128)S(1)}, f32[129,8,128]{2,1,0:T(8,128)S(1)}, u32[]{:S(2)}, u32[]{:S(2)}) collective-permute-start(f32[129,8,128]{2,1,0:T(8,128)S(1)} %get-tuple-element.56.rest_0_.own_ref), channel_id=1, source_target_pairs={{15,13},{12,14},{11,9},{8,10},{7,5},{4,6},{3,1},{0,2},{31,29},{28,... | collective-permute-start | bytes 1585160 | tf_op jit(solution)/shard_map/ppermute | solution.py:426
  50.2 10.8 %collective-permute-start.9 = (f32[129,8,128]{2,1,0:T(8,128)S(1)}, f32[129,8,128]{2,1,0:T(8,128)S(1)}, u32[]{:S(2)}, u32[]{:S(2)}) collective-permute-start(f32[129,8,128]{2,1,0:T(8,128)S(1)} %get-tuple-element.60.after_ref.own_ref), channel_id=1, source_target_pairs={{14,12},{15,11},{12,14},{13,9},{10,8},{11,7},{8,10},{9,5},{6,4},{7... | collective-permute-start | bytes 1585160 | tf_op jit(solution)/shard_map/ppermute | solution.py:426
  54.5 10.4 %collective-permute-start.12 = (f32[129,8,128]{2,1,0:T(8,128)S(1)}, f32[129,8,128]{2,1,0:T(8,128)S(1)}, u32[]{:S(2)}, u32[]{:S(2)}) collective-permute-start(f32[129,8,128]{2,1,0:T(8,128)S(1)} %second10.1.rest_0_.sent_ref), channel_id=1, source_target_pairs={{14,10},{13,9},{10,6},{9,5},{6,2},{5,1},{30,26},{29,25},{26,22},{2... | collective-permute-start | bytes 1585160 | tf_op jit(solution)/shard_map/ppermute | solution.py:426
  61.0 16.5 %collective-permute-start.10 = (f32[129,8,128]{2,1,0:T(8,128)S(1)}, f32[129,8,128]{2,1,0:T(8,128)S(1)}, u32[]{:S(2)}, u32[]{:S(2)}) collective-permute-start(f32[129,8,128]{2,1,0:T(8,128)S(1)} %second11.1.rest_0_.sent_ref.after_ref), channel_id=1, source_target_pairs={{14,10},{15,13},{12,8},{13,11},{10,6},{11,9},{8,4},{9,7},{6,2},{7,... | collective-permute-start | bytes 1585160 | tf_op jit(solution)/shard_map/ppermute | solution.py:426
  65.0 18.4 %collective-permute-start.13 = (f32[129,8,128]{2,1,0:T(8,128)S(1)}, f32[129,8,128]{2,1,0:T(8,128)S(1)}, u32[]{:S(2)}, u32[]{:S(2)}) collective-permute-start(f32[129,8,128]{2,1,0:T(8,128)S(1)} %get-tuple-element.76), channel_id=1, source_target_pairs={{14,10},{13,11},{10,6},{9,7},{6,2},{5,3},{30,26},{29,27},{26,22},{... | collective-permute-start | bytes 1585160 | tf_op jit(solution)/shard_map/ppermute | solution.py:426
  66.3 17.1 %collective-permute-start.14 = (f32[129,8,128]{2,1,0:T(8,128)S(1)}, f32[129,8,128]{2,1,0:T(8,128)S(1)}, u32[]{:S(2)}, u32[]{:S(2)}) collective-permute-start(f32[129,8,128]{2,1,0:T(8,128)S(1)} %get-tuple-element.77), channel_id=1, source_target_pairs={{14,12},{10,8},{6,4},{2,0},{30,28},{26,24},{22,20},{18,16}} | collective-permute-start | bytes 1585160 | tf_op jit(solution)/shard_map/ppermute | solution.py:426
  77.6 6.4 %collective-permute-start.11 = (f32[129,8,128]{2,1,0:T(8,128)S(1)}, f32[129,8,128]{2,1,0:T(8,128)S(1)}, u32[]{:S(2)}, u32[]{:S(2)}) collective-permute-start(f32[129,8,128]{2,1,0:T(8,128)S(1)} %third11.1), channel_id=1, source_target_pairs={{14,10},{10,6},{6,2},{30,26},{26,22},{22,18}} | collective-permute-start | bytes 1585160 | tf_op jit(solution)/shard_map/ppermute | solution.py:426

commit v6 on v5

--- a/solution.py
+++ b/solution.py
@@ -238,7 +238,7 @@
 
 
 def grad_kernel(n, hh, width, doc_ref, q_ref, att_ref, do_ref, gain_ref, mine_ref, other_ref, *rest):
-    normed_ref, ag_ref, out_ref = rest[-3:]
+    ag_ref, out_ref = rest[-2:]
     total = mine_ref[...] + other_ref[...]
     inverse = lax.rsqrt(total[:, 0:1] / width + norm_eps)
     coef = inverse * inverse * inverse * total[:, 1:2] / width
@@ -246,22 +246,26 @@
         at = cols(n * hh + j)
         att = att_ref[:, cols(j)]
         scaled = gain_ref[:, at] * do_ref[:, at].astype(F32)
-        normed_ref[:, at] = (att * inverse * gain_ref[:, at]).astype(BF)
         ag = (inverse * scaled - att * coef).astype(BF)
         ag_ref[:, cols(j)] = ag
         put_head(out_ref, j, tn(q_ref[:, at], ag))
     put_tag(out_ref, doc_ref)
 
 
-def back_kernel(c, hh, q_ref, k_ref, v_ref, ag_ref, state_ref, *rest):
-    qg_ref, qg_sems, normed_sem = rest[-3:]
+def back_kernel(c, hh, width, q_ref, k_ref, v_ref, ag_ref, state_ref, *rest):
+    qg_ref, qg_sems, normed_ref, normed_sem = rest[-4:]
     if c == 1:
-        normed_ref = rest[2]
-        normed_hbm, qg_hbm, kin_ref, vin_ref = rest[-7:-3]
+        first_ref, second_ref, gain_ref, mine_ref, other_ref = rest[2:7]
+        normed_hbm, qg_hbm, kin_ref, vin_ref = rest[-8:-4]
+        total = mine_ref[...] + other_ref[...]
+        inverse = lax.rsqrt(total[:, 0:1] / width + norm_eps)
+        half = first_ref.shape[1]
+        normed_ref[:, :half] = (first_ref[...] * inverse * gain_ref[:, :half]).astype(BF)
+        normed_ref[:, half:] = (second_ref[...] * inverse * gain_ref[:, half:]).astype(BF)
         normed_copy = pltpu.make_async_copy(normed_ref, normed_hbm, normed_sem)
         normed_copy.start()
     else:
-        qg_hbm, kin_ref, vin_ref = rest[-6:-3]
+        qg_hbm, kin_ref, vin_ref = rest[-7:-4]
     mask = lower(q_ref.shape[0])
     mask_t = upper(q_ref.shape[0])
     count = hh // 2
@@ -505,33 +509,34 @@
         attended.append(att)
         state.append(st)
     other = lax.ppermute(sums, "head", [(c, c ^ 1) for c in range(head)])
-    def grad(n, normed, *after):
+    def grad(n, *after):
         return call(
             functools.partial(grad_kernel, n, hh, full), f"grad{n}",
-            [docs] + near(queries, attended[n], output_grad, gain, sums, other, *([normed] if n else []), *after),
-            [wide, half16, message], aliases={7: 0} if n else None, flops=mm,
+            [docs] + near(queries, attended[n], output_grad, gain, sums, other, *after),
+            [half16, message], flops=mm,
         )
 
     def back(c, query_grad, after):
         n = c // 2
         ins = near(queries, keys[n], values[n], ag[n], state[n], after)
         ins += [(HBM, query_grad)] if c else []
-        ins += near(normed) if c == 1 else []
+        ins += near(*attended, gain, sums, other) if c == 1 else []
         outs = [(HBM, (tokens, width), BF), quarter32, quarter32]
         return call(
-            functools.partial(back_kernel, c, hh), f"back{c}", ins, [outs[0]] + outs if c == 1 else outs,
+            functools.partial(back_kernel, c, hh, full), f"back{c}", ins, [outs[0]] + outs if c == 1 else outs,
             scratch=[
-                pltpu.VMEM((tokens, hw // 2), BF), pltpu.SemaphoreType.DMA((hh // 2,)), pltpu.SemaphoreType.DMA(())
+                pltpu.VMEM((tokens, hw // 2), BF), pltpu.SemaphoreType.DMA((hh // 2,)),
+                pltpu.VMEM((tokens, width), BF), pltpu.SemaphoreType.DMA(()),
             ],
             aliases={6: int(c == 1)} if c else None, flops=7 * mm // 2,
         )
 
     way0, way1 = routes(seq, head, -1)
-    normed, ag0, bg0 = grad(0, None)
+    ag0, bg0 = grad(0)
     ag = [ag0]
     got1 = [send(bg0, way0[0])]
     query_grad, kin0, vin0 = back(0, None, bg0)
-    normed, ag1, bg1 = grad(1, normed, kin0)
+    ag1, bg1 = grad(1, kin0)
     ag.append(ag1)
     bg = [bg0, bg1]
     got1.append(send(bg1, way1[0]))

time: 85.9 us -> 85.9 us (level)
  waiting for transfers between devices: 37.5 us -> 36.6 us
where the time goes in v6:
time: 85.9 us; the launch traced here: 85.4 us
  waiting for transfers between devices  36.6 us (43%)
  starting transfers between devices  28.8 us (34%)
  Pallas kernels  18.4 us (21%)
  between operations  1.58 us (2%)
    ppermute x14, waiting for transfers between devices, send(): return lax.ppermute(x, ('seq', 'head'), pairs)  35.3 us
    ppermute x14, starting transfers between devices, send(): return lax.ppermute(x, ('seq', 'head'), pairs)  28.8 us
    pallas_call x22, Pallas kernels, call(): pl.pallas_call(kernel, in_specs=[spec(m) for m, _ in ins], out_specs=out_...  18.4 us
  transfers between devices with their start and end apart: 15, of which 9 were waited for; matrix products, arithmetic and copies ran while one was open for 0% of the time, Pallas kernels for 16%

profile of v6, /device:TPU:19, one launch (start us, length us, event | category | flops | bytes accessed | tf_op | source)
XLA Modules:
  0.0 85.4 jit_solution(16496507828045986284)
XLA Ops:
  1.3 1.7 %kv0.1 = (bf16[256,1024]{1,0:T(8,128)(2,1)S(1)}, bf16[256,1024]{1,0:T(8,128)(2,1)S(1)}, f32[129,8,128]{2,1,0:T(8,128)S(1)}) custom-call(s32[1]{0:T(128)S(6)} %copy.16.doc_ref, bf16[256,2048]{1,0:T(8,128)(2,1)} %k_hbm.3, bf16[256,2048]{1,0:T(8,128)(2,1)} %v_hbm.3), custom_call_target="tpu_custom_call" | custom-call | flops 67108864 | bytes 4194304 | tf_op jit(solution)/shard_map/kv0/pallas_call | solution.py:377
  3.0 1.3 %collective-permute-start = (f32[129,8,128]{2,1,0:T(8,128)S(1)}, f32[129,8,128]{2,1,0:T(8,128)S(1)}, u32[]{:S(2)}, u32[]{:S(2)}) collective-permute-start(f32[129,8,128]{2,1,0:T(8,128)S(1)} %get-tuple-element.43.after_ref.own_ref), channel_id=1, source_target_pairs={{1,3},{2,0},{5,7},{6,4},{9,11},{10,8},{13,15},{14,12},{17,19},{18,... | collective-permute-start | bytes 1585160 | tf_op jit(solution)/shard_map/ppermute | solution.py:430
  4.3 0.9 %intra0.1.rest_0_.intra_ref = f32[256,1024]{1,0:T(8,128)S(1)} custom-call(bf16[256,2048]{1,0:T(8,128)(2,1)S(1)} %copy-done, bf16[256,1024]{1,0:T(8,128)(2,1)S(1)} %get-tuple-element.41.k_ref, bf16[256,1024]{1,0:T(8,128)(2,1)S(1)} %get-tuple-element.42.v_ref, f32[129,8,128]{2,1,0:T(8,128)S(1)} %get-tuple-element.43.after_ref.own_ref), custom_call_target="tpu_custom_call" | custom-call | flops 268435456 | bytes 4194304 | tf_op jit(solution)/shard_map/intra0/pallas_call | solution.py:377
  5.2 1.6 %kv1.1 = (bf16[256,1024]{1,0:T(8,128)(2,1)S(1)}, bf16[256,1024]{1,0:T(8,128)(2,1)S(1)}, f32[129,8,128]{2,1,0:T(8,128)S(1)}) custom-call(s32[1]{0:T(128)S(6)} %copy.16.doc_ref, bf16[256,2048]{1,0:T(8,128)(2,1)} %k_hbm.3, bf16[256,2048]{1,0:T(8,128)(2,1)} %v_hbm.3, f32[256,1024]{1,0:T(8,128)S(1)} %intra0.1.rest_0_.intra_ref), custom_call_target="tpu_custom_call" | custom-call | flops 67108864 | bytes 4194304 | tf_op jit(solution)/shard_map/kv1/pallas_call | solution.py:377
  6.8 3.2 %collective-permute-start.2 = (f32[129,8,128]{2,1,0:T(8,128)S(1)}, f32[129,8,128]{2,1,0:T(8,128)S(1)}, u32[]{:S(2)}, u32[]{:S(2)}) collective-permute-start(f32[129,8,128]{2,1,0:T(8,128)S(1)} %get-tuple-element.44.after_ref.own_ref), channel_id=1, source_target_pairs={{0,2},{1,5},{2,0},{3,7},{4,6},{5,9},{6,4},{7,11},{8,10},{9,13},{10... | collective-permute-start | bytes 1585160 | tf_op jit(solution)/shard_map/ppermute | solution.py:430
  10.0 2.9 %collective-permute-done.got_ref.rest_0_ = f32[129,8,128]{2,1,0:T(8,128)S(1)} collective-permute-done((f32[129,8,128]{2,1,0:T(8,128)S(1)}, f32[129,8,128]{2,1,0:T(8,128)S(1)}, u32[]{:S(2)}, u32[]{:S(2)}) %collective-permute-start) | collective-permute-done | bytes 528416 | tf_op jit(solution)/shard_map/ppermute | solution.py:430
  12.9 0.1 second00.1.after_ref.sent_ref
  13.0 3.2 %collective-permute-start.1 = (f32[129,8,128]{2,1,0:T(8,128)S(1)}, f32[129,8,128]{2,1,0:T(8,128)S(1)}, u32[]{:S(2)}, u32[]{:S(2)}) collective-permute-start(f32[129,8,128]{2,1,0:T(8,128)S(1)} %second00.1.after_ref.sent_ref), channel_id=1, source_target_pairs={{0,4},{3,7},{4,8},{7,11},{8,12},{11,15},{16,20},{19,23},{20,24},{2... | collective-permute-start | bytes 1585160 | tf_op jit(solution)/shard_map/ppermute | solution.py:430
  16.2 0.8 collective-permute-done.2.got_ref.rest_0_
  17.1 0.1 second01.1.after_ref.sent_ref
  17.1 5.0 %collective-permute-start.5 = (f32[129,8,128]{2,1,0:T(8,128)S(1)}, f32[129,8,128]{2,1,0:T(8,128)S(1)}, u32[]{:S(2)}, u32[]{:S(2)}) collective-permute-start(f32[129,8,128]{2,1,0:T(8,128)S(1)} %second01.1.after_ref.sent_ref), channel_id=1, source_target_pairs={{0,4},{1,3},{2,6},{3,5},{4,8},{5,7},{6,10},{7,9},{8,12},{9,11},{10... | collective-permute-start | bytes 1585160 | tf_op jit(solution)/shard_map/ppermute | solution.py:430
  22.2 0.9 %intra1.1.after_ref.intra_ref = f32[256,1024]{1,0:T(8,128)S(1)} custom-call(bf16[256,2048]{1,0:T(8,128)(2,1)S(1)} %copy-done, bf16[256,1024]{1,0:T(8,128)(2,1)S(1)} %get-tuple-element.45.k_ref, bf16[256,1024]{1,0:T(8,128)(2,1)S(1)} %get-tuple-element.46.v_ref, f32[129,8,128]{2,1,0:T(8,128)S(1)} %second01.1.after_ref.sent_ref), custom_call_target="tpu_custom_call" | custom-call | flops 268435456 | bytes 4194304 | tf_op jit(solution)/shard_map/intra1/pallas_call | solution.py:377
  23.1 0.1 third00.1
  23.3 1.9 %collective-permute-start.3 = (f32[129,8,128]{2,1,0:T(8,128)S(1)}, f32[129,8,128]{2,1,0:T(8,128)S(1)}, u32[]{:S(2)}, u32[]{:S(2)}) collective-permute-start(f32[129,8,128]{2,1,0:T(8,128)S(1)} %get-tuple-element.47), channel_id=1, source_target_pairs={{0,4},{3,5},{4,8},{7,9},{8,12},{11,13},{16,20},{19,21},{20,24},{23... | collective-permute-start | bytes 1585160 | tf_op jit(solution)/shard_map/ppermute | solution.py:430
  25.2 0.0 copy-start.1
  25.2 0.0 copy-start.2
  25.2 0.8 collective-permute-start.4
  26.1 6.5 %collective-permute-done.5.got_ref.rest_1_ = f32[129,8,128]{2,1,0:T(8,128)S(1)} collective-permute-done((f32[129,8,128]{2,1,0:T(8,128)S(1)}, f32[129,8,128]{2,1,0:T(8,128)S(1)}, u32[]{:S(2)}, u32[]{:S(2)}) %collective-permute-start.5) | collective-permute-done | bytes 528416 | tf_op jit(solution)/shard_map/ppermute | solution.py:430
  32.6 0.1 third01.1
  32.7 0.7 collective-permute-start.6
  33.4 6.3 %collective-permute-done.3.rest_2_ = f32[129,8,128]{2,1,0:T(8,128)S(1)} collective-permute-done((f32[129,8,128]{2,1,0:T(8,128)S(1)}, f32[129,8,128]{2,1,0:T(8,128)S(1)}, u32[]{:S(2)}, u32[]{:S(2)}) %collective-permute-start.3) | collective-permute-done | bytes 528416 | tf_op jit(solution)/shard_map/ppermute | solution.py:430
  39.7 0.5 attend0.1
  40.1 0.6 attend1.1
  40.7 0.1 collective-permute-start.7
  40.8 1.3 %collective-permute-done.7.other_ref.rest_6_ = f32[256,128]{1,0:T(8,128)S(1)} collective-permute-done((f32[256,128]{1,0:T(8,128)S(1)}, f32[256,128]{1,0:T(8,128)S(1)}, u32[]{:S(2)}, u32[]{:S(2)}) %collective-permute-start.7) | collective-permute-done | bytes 131104 | tf_op jit(solution)/shard_map/ppermute | solution.py:511
  42.2 0.6 grad0.1
  42.8 4.6 %collective-permute-start.8 = (f32[129,8,128]{2,1,0:T(8,128)S(1)}, f32[129,8,128]{2,1,0:T(8,128)S(1)}, u32[]{:S(2)}, u32[]{:S(2)}) collective-permute-start(f32[129,8,128]{2,1,0:T(8,128)S(1)} %get-tuple-element.54.rest_0_.own_ref), channel_id=1, source_target_pairs={{15,13},{12,14},{11,9},{8,10},{7,5},{4,6},{3,1},{0,2},{31,29},{28,... | collective-permute-start | bytes 1585160 | tf_op jit(solution)/shard_map/ppermute | solution.py:430
  47.4 1.9 %back0.1 = (bf16[256,2048]{1,0:T(8,128)(2,1)}, f32[256,512]{1,0:T(8,128)S(1)}, f32[256,512]{1,0:T(8,128)S(1)}) custom-call(bf16[256,2048]{1,0:T(8,128)(2,1)S(1)} %copy-done, bf16[256,1024]{1,0:T(8,128)(2,1)S(1)} %get-tuple-element.41.k_ref, bf16[256,1024]{1,0:T(8,128)(2,1)S(1)} %get-tuple-element.42.v_ref, bf16[256,1024]{1,0:T(8,128)(2,1)S(1)} %get-tuple-element.52.ag_ref, ...), custom_call_target="tpu_custom_call" | custom-call | flops 234881024 | bytes 4194304 | tf_op jit(solution)/shard_map/back0/pallas_call | solution.py:377
  49.3 0.6 grad1.1
  50.0 2.1 %collective-permute-start.9 = (f32[129,8,128]{2,1,0:T(8,128)S(1)}, f32[129,8,128]{2,1,0:T(8,128)S(1)}, u32[]{:S(2)}, u32[]{:S(2)}) collective-permute-start(f32[129,8,128]{2,1,0:T(8,128)S(1)} %get-tuple-element.57.after_ref.own_ref), channel_id=1, source_target_pairs={{14,12},{15,11},{12,14},{13,9},{10,8},{11,7},{8,10},{9,5},{6,4},{7... | collective-permute-start | bytes 1585160 | tf_op jit(solution)/shard_map/ppermute | solution.py:430
  52.1 2.3 %collective-permute-done.8.got_ref.rest_0_ = f32[129,8,128]{2,1,0:T(8,128)S(1)} collective-permute-done((f32[129,8,128]{2,1,0:T(8,128)S(1)}, f32[129,8,128]{2,1,0:T(8,128)S(1)}, u32[]{:S(2)}, u32[]{:S(2)}) %collective-permute-start.8) | collective-permute-done | bytes 528416 | tf_op jit(solution)/shard_map/ppermute | solution.py:430
  54.4 0.1 second10.1.rest_0_.sent_ref
  54.5 0.7 collective-permute-start.12
  55.2 2.5 %back1.1 = (bf16[256,2048]{1,0:T(8,128)(2,1)}, bf16[256,2048]{1,0:T(8,128)(2,1)}, f32[256,512]{1,0:T(8,128)S(1)}, f32[256,512]{1,0:T(8,128)S(1)}) custom-call(bf16[256,2048]{1,0:T(8,128)(2,1)S(1)} %copy-done, bf16[256,1024]{1,0:T(8,128)(2,1)S(1)} %get-tuple-element.41.k_ref, ...), custom_call_target="tpu_custom_call", output_to_operand_aliasing={{1}: (6, {})} | custom-call | flops 234881024 | bytes 4194304 | tf_op jit(solution)/shard_map/back1/pallas_call | solution.py:377
  57.7 3.0 %collective-permute-done.9.got_ref.rest_0_ = f32[129,8,128]{2,1,0:T(8,128)S(1)} collective-permute-done((f32[129,8,128]{2,1,0:T(8,128)S(1)}, f32[129,8,128]{2,1,0:T(8,128)S(1)}, u32[]{:S(2)}, u32[]{:S(2)}) %collective-permute-start.9) | collective-permute-done | bytes 528416 | tf_op jit(solution)/shard_map/ppermute | solution.py:430
  60.7 0.1 second11.1.rest_0_.sent_ref.after_ref
  60.8 2.5 %collective-permute-start.10 = (f32[129,8,128]{2,1,0:T(8,128)S(1)}, f32[129,8,128]{2,1,0:T(8,128)S(1)}, u32[]{:S(2)}, u32[]{:S(2)}) collective-permute-start(f32[129,8,128]{2,1,0:T(8,128)S(1)} %second11.1.rest_0_.sent_ref.after_ref), channel_id=1, source_target_pairs={{14,10},{15,13},{12,8},{13,11},{10,6},{11,9},{8,4},{9,7},{6,2},{7,... | collective-permute-start | bytes 1585160 | tf_op jit(solution)/shard_map/ppermute | solution.py:430
  63.2 1.9 %back2.1 = (bf16[256,2048]{1,0:T(8,128)(2,1)}, f32[256,512]{1,0:T(8,128)S(1)}, f32[256,512]{1,0:T(8,128)S(1)}) custom-call(bf16[256,2048]{1,0:T(8,128)(2,1)S(1)} %copy-done, bf16[256,1024]{1,0:T(8,128)(2,1)S(1)} %get-tuple-element.45.k_ref, bf16[256,1024]{1,0:T(8,128)(2,1)S(1)} %get-tuple-element.46.v_ref, ...), custom_call_target="tpu_custom_call", output_to_operand_aliasing={{0}: (6, {})} | custom-call | flops 234881024 | bytes 4194304 | tf_op jit(solution)/shard_map/back2/pallas_call | solution.py:377
  65.2 0.1 third10.1
  65.3 1.3 %collective-permute-start.13 = (f32[129,8,128]{2,1,0:T(8,128)S(1)}, f32[129,8,128]{2,1,0:T(8,128)S(1)}, u32[]{:S(2)}, u32[]{:S(2)}) collective-permute-start(f32[129,8,128]{2,1,0:T(8,128)S(1)} %get-tuple-element.72), channel_id=1, source_target_pairs={{14,10},{13,11},{10,6},{9,7},{6,2},{5,3},{30,26},{29,27},{26,22},{... | collective-permute-start | bytes 1585160 | tf_op jit(solution)/shard_map/ppermute | solution.py:430
  66.6 0.7 collective-permute-start.14
  67.3 10.3 %collective-permute-done.10.rest_0_.got_ref.rest_1_ = f32[129,8,128]{2,1,0:T(8,128)S(1)} collective-permute-done((f32[129,8,128]{2,1,0:T(8,128)S(1)}, f32[129,8,128]{2,1,0:T(8,128)S(1)}, u32[]{:S(2)}, u32[]{:S(2)}) %collective-permute-start.10) | collective-permute-done | bytes 528416 | tf_op jit(solution)/shard_map/ppermute | solution.py:430
  77.7 0.1 third11.1
  77.7 0.7 collective-permute-start.11
  78.4 1.9 %back3.1 = (bf16[256,2048]{1,0:T(8,128)(2,1)}, f32[256,512]{1,0:T(8,128)S(1)}, f32[256,512]{1,0:T(8,128)S(1)}) custom-call(bf16[256,2048]{1,0:T(8,128)(2,1)S(1)} %copy-done, bf16[256,1024]{1,0:T(8,128)(2,1)S(1)} %get-tuple-element.45.k_ref, bf16[256,1024]{1,0:T(8,128)(2,1)S(1)} %get-tuple-element.46.v_ref, ...), custom_call_target="tpu_custom_call", output_to_operand_aliasing={{0}: (6, {})} | custom-call | flops 234881024 | bytes 4194304 | tf_op jit(solution)/shard_map/back3/pallas_call | solution.py:377
  80.4 3.0 %collective-permute-done.13.rest_2_ = f32[129,8,128]{2,1,0:T(8,128)S(1)} collective-permute-done((f32[129,8,128]{2,1,0:T(8,128)S(1)}, f32[129,8,128]{2,1,0:T(8,128)S(1)}, u32[]{:S(2)}, u32[]{:S(2)}) %collective-permute-start.13) | collective-permute-done | bytes 528416 | tf_op jit(solution)/shard_map/ppermute | solution.py:430
  83.4 0.6 final0.1
  84.0 1.5 %final1.1 = (bf16[256,2048]{1,0:T(8,128)(2,1)}, bf16[256,2048]{1,0:T(8,128)(2,1)}) custom-call(s32[1]{0:T(128)S(6)} %copy.16.doc_ref, bf16[256,1024]{1,0:T(8,128)(2,1)S(1)} %get-tuple-element.45.k_ref, bf16[256,1024]{1,0:T(8,128)(2,1)S(1)} %get-tuple-element.46.v_ref, f32[256,512]{1,0:T(8,128)S(1)} %get-tuple-element.66.after_ref.kin0, ...), custom_call_target="tpu_custom_call" | custom-call | flops 134217728 | bytes 4194304 | tf_op jit(solution)/shard_map/final1/pallas_call | solution.py:377
  (10 shorter events, 0.0 us)
Async XLA Ops:
  1.3 3.0 %copy-start = (bf16[256,2048]{1,0:T(8,128)(2,1)S(1)}, bf16[256,2048]{1,0:T(8,128)(2,1)}, u32[]{:S(2)}) copy-start(bf16[256,2048]{1,0:T(8,128)(2,1)} %q_ref.19) | copy-start | bytes 3145732
  3.0 10.0 %collective-permute-start = (f32[129,8,128]{2,1,0:T(8,128)S(1)}, f32[129,8,128]{2,1,0:T(8,128)S(1)}, u32[]{:S(2)}, u32[]{:S(2)}) collective-permute-start(f32[129,8,128]{2,1,0:T(8,128)S(1)} %get-tuple-element.43.after_ref.own_ref), channel_id=1, source_target_pairs={{1,3},{2,0},{5,7},{6,4},{9,11},{10,8},{13,15},{14,12},{17,19},{18,... | collective-permute-start | bytes 1585160 | tf_op jit(solution)/shard_map/ppermute | solution.py:430
  6.8 10.3 %collective-permute-start.2 = (f32[129,8,128]{2,1,0:T(8,128)S(1)}, f32[129,8,128]{2,1,0:T(8,128)S(1)}, u32[]{:S(2)}, u32[]{:S(2)}) collective-permute-start(f32[129,8,128]{2,1,0:T(8,128)S(1)} %get-tuple-element.44.after_ref.own_ref), channel_id=1, source_target_pairs={{0,2},{1,5},{2,0},{3,7},{4,6},{5,9},{6,4},{7,11},{8,10},{9,13},{10... | collective-permute-start | bytes 1585160 | tf_op jit(solution)/shard_map/ppermute | solution.py:430
  13.0 10.1 %collective-permute-start.1 = (f32[129,8,128]{2,1,0:T(8,128)S(1)}, f32[129,8,128]{2,1,0:T(8,128)S(1)}, u32[]{:S(2)}, u32[]{:S(2)}) collective-permute-start(f32[129,8,128]{2,1,0:T(8,128)S(1)} %second00.1.after_ref.sent_ref), channel_id=1, source_target_pairs={{0,4},{3,7},{4,8},{7,11},{8,12},{11,15},{16,20},{19,23},{20,24},{2... | collective-permute-start | bytes 1585160 | tf_op jit(solution)/shard_map/ppermute | solution.py:430
  17.1 15.5 %collective-permute-start.5 = (f32[129,8,128]{2,1,0:T(8,128)S(1)}, f32[129,8,128]{2,1,0:T(8,128)S(1)}, u32[]{:S(2)}, u32[]{:S(2)}) collective-permute-start(f32[129,8,128]{2,1,0:T(8,128)S(1)} %second01.1.after_ref.sent_ref), channel_id=1, source_target_pairs={{0,4},{1,3},{2,6},{3,5},{4,8},{5,7},{6,10},{7,9},{8,12},{9,11},{10... | collective-permute-start | bytes 1585160 | tf_op jit(solution)/shard_map/ppermute | solution.py:430
  23.3 16.4 %collective-permute-start.3 = (f32[129,8,128]{2,1,0:T(8,128)S(1)}, f32[129,8,128]{2,1,0:T(8,128)S(1)}, u32[]{:S(2)}, u32[]{:S(2)}) collective-permute-start(f32[129,8,128]{2,1,0:T(8,128)S(1)} %get-tuple-element.47), channel_id=1, source_target_pairs={{0,4},{3,5},{4,8},{7,9},{8,12},{11,13},{16,20},{19,21},{20,24},{23... | collective-permute-start | bytes 1585160 | tf_op jit(solution)/shard_map/ppermute | solution.py:430
  25.2 14.4 %copy-start.1 = (bf16[256,2048]{1,0:T(8,128)(2,1)S(1)}, bf16[256,2048]{1,0:T(8,128)(2,1)}, u32[]{:S(2)}) copy-start(bf16[256,2048]{1,0:T(8,128)(2,1)} %do_ref.7) | copy-start | bytes 3145732
  25.2 14.4 %copy-start.2 = (f32[2048]{0:T(1024)S(1)}, f32[2048]{0:T(1024)}, u32[]{:S(2)}) copy-start(f32[2048]{0:T(1024)} %param.10) | copy-start | bytes 24580
  25.2 14.4 %collective-permute-start.4 = (f32[129,8,128]{2,1,0:T(8,128)S(1)}, f32[129,8,128]{2,1,0:T(8,128)S(1)}, u32[]{:S(2)}, u32[]{:S(2)}) collective-permute-start(f32[129,8,128]{2,1,0:T(8,128)S(1)} %get-tuple-element.48), channel_id=1, source_target_pairs={{0,2},{4,6},{8,10},{12,14},{16,18},{20,22},{24,26},{28,30}} | collective-permute-start | bytes 1585160 | tf_op jit(solution)/shard_map/ppermute | solution.py:430
  32.7 7.5 %collective-permute-start.6 = (f32[129,8,128]{2,1,0:T(8,128)S(1)}, f32[129,8,128]{2,1,0:T(8,128)S(1)}, u32[]{:S(2)}, u32[]{:S(2)}) collective-permute-start(f32[129,8,128]{2,1,0:T(8,128)S(1)} %third01.1), channel_id=1, source_target_pairs={{0,4},{4,8},{8,12},{16,20},{20,24},{24,28}} | collective-permute-start | bytes 1585160 | tf_op jit(solution)/shard_map/ppermute | solution.py:430
  40.7 1.4 %collective-permute-start.7 = (f32[256,128]{1,0:T(8,128)S(1)}, f32[256,128]{1,0:T(8,128)S(1)}, u32[]{:S(2)}, u32[]{:S(2)}) collective-permute-start(f32[256,128]{1,0:T(8,128)S(1)} %get-tuple-element.51.mine_ref.rest_5_), channel_id=1, source_target_pairs={{0,1},{1,0},{2,3},{3,2},{4,5},{5,4},{6,7},{7,6},{8,9},{9,8},{10,11... | collective-permute-start | bytes 393224 | tf_op jit(solution)/shard_map/ppermute | solution.py:511
  42.8 11.6 %collective-permute-start.8 = (f32[129,8,128]{2,1,0:T(8,128)S(1)}, f32[129,8,128]{2,1,0:T(8,128)S(1)}, u32[]{:S(2)}, u32[]{:S(2)}) collective-permute-start(f32[129,8,128]{2,1,0:T(8,128)S(1)} %get-tuple-element.54.rest_0_.own_ref), channel_id=1, source_target_pairs={{15,13},{12,14},{11,9},{8,10},{7,5},{4,6},{3,1},{0,2},{31,29},{28,... | collective-permute-start | bytes 1585160 | tf_op jit(solution)/shard_map/ppermute | solution.py:430
  50.0 10.7 %collective-permute-start.9 = (f32[129,8,128]{2,1,0:T(8,128)S(1)}, f32[129,8,128]{2,1,0:T(8,128)S(1)}, u32[]{:S(2)}, u32[]{:S(2)}) collective-permute-start(f32[129,8,128]{2,1,0:T(8,128)S(1)} %get-tuple-element.57.after_ref.own_ref), channel_id=1, source_target_pairs={{14,12},{15,11},{12,14},{13,9},{10,8},{11,7},{8,10},{9,5},{6,4},{7... | collective-permute-start | bytes 1585160 | tf_op jit(solution)/shard_map/ppermute | solution.py:430
  54.5 10.7 %collective-permute-start.12 = (f32[129,8,128]{2,1,0:T(8,128)S(1)}, f32[129,8,128]{2,1,0:T(8,128)S(1)}, u32[]{:S(2)}, u32[]{:S(2)}) collective-permute-start(f32[129,8,128]{2,1,0:T(8,128)S(1)} %second10.1.rest_0_.sent_ref), channel_id=1, source_target_pairs={{14,10},{13,9},{10,6},{9,5},{6,2},{5,1},{30,26},{29,25},{26,22},{2... | collective-permute-start | bytes 1585160 | tf_op jit(solution)/shard_map/ppermute | solution.py:430
  60.8 16.9 %collective-permute-start.10 = (f32[129,8,128]{2,1,0:T(8,128)S(1)}, f32[129,8,128]{2,1,0:T(8,128)S(1)}, u32[]{:S(2)}, u32[]{:S(2)}) collective-permute-start(f32[129,8,128]{2,1,0:T(8,128)S(1)} %second11.1.rest_0_.sent_ref.after_ref), channel_id=1, source_target_pairs={{14,10},{15,13},{12,8},{13,11},{10,6},{11,9},{8,4},{9,7},{6,2},{7,... | collective-permute-start | bytes 1585160 | tf_op jit(solution)/shard_map/ppermute | solution.py:430
  65.3 18.0 %collective-permute-start.13 = (f32[129,8,128]{2,1,0:T(8,128)S(1)}, f32[129,8,128]{2,1,0:T(8,128)S(1)}, u32[]{:S(2)}, u32[]{:S(2)}) collective-permute-start(f32[129,8,128]{2,1,0:T(8,128)S(1)} %get-tuple-element.72), channel_id=1, source_target_pairs={{14,10},{13,11},{10,6},{9,7},{6,2},{5,3},{30,26},{29,27},{26,22},{... | collective-permute-start | bytes 1585160 | tf_op jit(solution)/shard_map/ppermute | solution.py:430
  66.6 16.7 %collective-permute-start.14 = (f32[129,8,128]{2,1,0:T(8,128)S(1)}, f32[129,8,128]{2,1,0:T(8,128)S(1)}, u32[]{:S(2)}, u32[]{:S(2)}) collective-permute-start(f32[129,8,128]{2,1,0:T(8,128)S(1)} %get-tuple-element.73), channel_id=1, source_target_pairs={{14,12},{10,8},{6,4},{2,0},{30,28},{26,24},{22,20},{18,16}} | collective-permute-start | bytes 1585160 | tf_op jit(solution)/shard_map/ppermute | solution.py:430
  77.7 6.2 %collective-permute-start.11 = (f32[129,8,128]{2,1,0:T(8,128)S(1)}, f32[129,8,128]{2,1,0:T(8,128)S(1)}, u32[]{:S(2)}, u32[]{:S(2)}) collective-permute-start(f32[129,8,128]{2,1,0:T(8,128)S(1)} %third11.1), channel_id=1, source_target_pairs={{14,10},{10,6},{6,2},{30,26},{26,22},{22,18}} | collective-permute-start | bytes 1585160 | tf_op jit(solution)/shard_map/ppermute | solution.py:430
